TPU v7x, 256 devices: a whole 4x4x8 slice. The times are simulated.
256 devices in a mesh: samp: 4 (over y), var: 64 (over x, z, core).
Axes of the slice: x: 4, y: 4, z: 8, core: 2. Of those that a mesh axis runs over, the one named last changes fastest.
Arguments:
- observed: bfloat16 [1024, 262144], P('samp', 'var'), may hold values from -6 to 6
- blocks: float32 [2048, 2, 128, 128], P('var'), may hold values from -6 to 6
- diagonal: float32 [262144], P('var'), may hold values from 1 to 4
- pattern: int32 [2048, 2], P('var'), may hold values from 0 to 2047, as said below
Outputs:
- new_blocks: float32 [2048, 2, 128, 128], P('var')
- new_diagonal: float32 [262144], P('var')
- objective: float32 [2], replicated
Inputs may be any that keep to these rules, and one draw needn't show every extreme that they name: pattern[c, 0] and pattern[c, 1] are two different row-block indices, one of them equal to c. For each index v of var, among its block columns c = v * 32 to v * 32 + 31, for every u, at most 2 of the entries that differ from c name row blocks in the range u * 32 to u * 32 + 31, and for some u exactly 2 do.
All inputs are finite; a program needn't handle non-finite values.
Results may differ from a plain program's by a relative error of at most 0.0049.
Values may be sent and summed in bfloat16 or wider, within the bound.
No kernel may reach another device: no remote copies, remote signals or barrier semaphores. Data moves between devices by JAX's collectives and lax.ppermute only.
A program may use at most 128 MiB of HBM per device.

v0:
```python
import functools

import jax
import jax.numpy as jnp
from jax import lax
from jax.sharding import Mesh
from jax.sharding import PartitionSpec as P

STEPS = 2
VAR = ("var_0", "var_1", "var_2")
SAMP_VAR = ("samp", "var_0", "var_1", "var_2")


step_length = 0.5
penalty = 0.5


def in_one_piece(arrays, axis, dim, along):
    ends, at = ([], 0)
    for a in arrays[:-1]:
        at += a.shape[along]
        ends.append(at)
    both = jnp.concatenate(arrays, axis=along)
    return tuple(
        jnp.split(lax.psum_scatter(both, axis, scatter_dimension=dim, tiled=True), ends, axis=along)
    )


def one_axis_at_a_time(x, axes):
    return functools.reduce(lax.psum, axes, x)


def shrink(moved, level):
    return jnp.sign(moved) * jnp.maximum(jnp.abs(moved) - level, 0.0)


def advance(diag_block, off_block, diag_values, grad_diag, grad_off, diag_mask, total_rows):
    grad_diag = grad_diag / total_rows
    grad_off = grad_off / total_rows
    new_off = shrink(off_block - step_length * grad_off, step_length * penalty)
    new_diag_block = jnp.where(
        diag_mask, 0.0, shrink(diag_block - step_length * grad_diag, step_length * penalty)
    )
    along = jnp.sum(jnp.where(diag_mask, grad_diag, 0.0), axis=1)
    moved = diag_values - step_length * along
    new_values = 0.5 * (moved + jnp.sqrt(moved * moved + 4.0 * step_length))
    return (new_diag_block, new_off, new_values)


def body(observed, blocks, diagonal, pattern):
    col_count = blocks.shape[0]
    block_width = blocks.shape[2]
    sample_rows = observed.shape[0]
    var_count = lax.axis_size(VAR)
    samp_count = lax.axis_size("samp")
    capacity = max(2, -(-col_count // var_count))
    total_rows = sample_rows * samp_count
    matrix_order = col_count * block_width * var_count
    var_index = lax.axis_index(VAR)
    column_ids = jnp.arange(col_count, dtype=jnp.int32)
    columns = var_index * col_count + column_ids
    on_diag = pattern == columns[:, None]
    off_row = jnp.sum(jnp.where(on_diag, 0, pattern), axis=1)
    owner_index = off_row // col_count
    resident_block = off_row % col_count
    earlier = (owner_index[None, :] == owner_index[:, None]) & (
        column_ids[None, :] < column_ids[:, None]
    )
    position_rank = jnp.sum(earlier, axis=1)
    slot_index = owner_index * capacity + position_rank
    all_slots = jnp.arange(var_count * capacity, dtype=jnp.int32)
    slot_match = slot_index[:, None] == all_slots[None, :]
    wanted = jnp.sum(jnp.where(slot_match, resident_block[:, None], 0), axis=0)
    asked_blocks = lax.all_to_all(wanted, VAR, split_axis=0, concat_axis=0, tiled=True)
    nearby_panels = observed.reshape(sample_rows, col_count, block_width)
    outgoing = jnp.take(nearby_panels, asked_blocks, axis=1)
    arrived = lax.all_to_all(outgoing, VAR, split_axis=1, concat_axis=1, tiled=True)
    distant_panels = jnp.take(arrived, slot_index, axis=1)
    diag_mask = jnp.eye(block_width, dtype=bool)
    flags = on_diag[:, :, None, None]
    diag_block = jnp.sum(jnp.where(flags, blocks, 0.0), axis=1)
    diag_block = jnp.where(diag_mask, 0.0, diag_block)
    off_block = jnp.sum(jnp.where(flags, 0.0, blocks), axis=1)
    diag_values = diagonal.reshape(col_count, block_width)
    samp_first = (lax.axis_index("samp") == 0).astype(jnp.float32)
    objective_parts = []
    for iteration in range(STEPS):
        full_diag = jnp.where(diag_mask, diag_values[:, None, :], diag_block)
        product = jnp.einsum(
            "qlh,lhy->qly",
            nearby_panels,
            full_diag.astype(jnp.bfloat16),
            preferred_element_type=jnp.float32,
        )
        product = product + jnp.einsum(
            "qlh,lhy->qly",
            distant_panels,
            off_block.astype(jnp.bfloat16),
            preferred_element_type=jnp.float32,
        )
        squares = jnp.sum(product * product)
        local_terms = -jnp.sum(jnp.log(diag_values)) + penalty * (
            jnp.sum(jnp.abs(diag_block)) + jnp.sum(jnp.abs(off_block))
        )
        part_value = (squares / (2.0 * total_rows) + samp_first * local_terms) / matrix_order
        objective_parts.append(part_value)
        lower_precision_product = product.astype(jnp.bfloat16)
        grad_diag = jnp.einsum(
            "rei,reo->eio",
            nearby_panels,
            lower_precision_product,
            preferred_element_type=jnp.float32,
        )
        grad_off = jnp.einsum(
            "rei,reo->eio",
            distant_panels,
            lower_precision_product,
            preferred_element_type=jnp.float32,
        )
        grad_diag, grad_off = in_one_piece((grad_diag, grad_off), "samp", 0, 1)
        share_size = col_count // samp_count
        share_start = lax.axis_index("samp") * share_size
        part_diag = lax.dynamic_slice_in_dim(diag_block, share_start, share_size, 0)
        part_off = lax.dynamic_slice_in_dim(off_block, share_start, share_size, 0)
        part_values = lax.dynamic_slice_in_dim(diag_values, share_start, share_size, 0)
        updated = advance(
            part_diag, part_off, part_values, grad_diag, grad_off, diag_mask, total_rows
        )
        diag_block, off_block, diag_values = (
            lax.all_gather(updated[0], "samp", axis=0, tiled=True),
            lax.all_gather(updated[1], "samp", axis=0, tiled=True),
            lax.all_gather(updated[2], "samp", axis=0, tiled=True),
        )
    objective = one_axis_at_a_time(jnp.stack(objective_parts), SAMP_VAR)
    new_blocks = jnp.where(flags, diag_block[:, None], off_block[:, None])
    return (new_blocks, diag_values.reshape(-1), objective)


def solution(mesh):
    torus = Mesh(
        mesh.devices.reshape(mesh.shape["samp"], 4, 8, 2), ("samp", "var_0", "var_1", "var_2")
    )
    placed = (P("samp", VAR), P(VAR, None, None, None), P(VAR), P(VAR, None))
    return jax.shard_map(
        body,
        mesh=torus,
        in_specs=placed,
        out_specs=(P(VAR, None, None, None), P(VAR), P()),
        check_vma=False,
    )
```

profile of v0, /device:TPU:1, one launch (start us, length us, event | category | flops | bytes accessed | tf_op | source)
XLA Modules:
  0.0 518.3 jit_solution(557768312172980150)
XLA Ops:
  8.9 13.0 %all-to-all-start = ((s32[64,2,1]{1,2,0:T(1,128)}), s32[64,2,1]{1,2,0:T(1,128)S(1)}, u32[]{:S(2)}, u32[]{:S(2)}) async-start(s32[64,2,1]{1,2,0:T(1,128)} %bitcast.2), calls=%async_computation | async-start | bytes 65536 | tf_op jit(solution)/shard_map/all_to_all | solution.py:74
  21.9 3.3 copy.67
  28.1 3.1 all-to-all-done
  32.8 7.9 %gather_fusion = bf16[128,256,128]{2,1,0:T(8,128)(2,1)} fusion(bf16[256,32,128]{2,0,1:T(8,128)(2,1)} %copy.71, s32[1024]{0:T(1024)S(1)} %pad_clamp_fusion.1), kind=kCustom, calls=%fused_computation | custom fusion | bytes 16777728 | tf_op jit(solution)/shard_map/jit(_take)/gather | solution.py:76
  40.7 7.4 %select_bitcast_fusion = bf16[256,128,128]{2,0,1:T(8,128)(2,1)} fusion(bf16[128,256,128]{2,1,0:T(8,128)(2,1)} %gather_fusion, pred[128]{0:T(512)(128)(4,1)S(1)} %compare_and_fusion), kind=kLoop, calls=%fused_computation.2 | loop fusion | flops 4194304 | bytes 16777344 | tf_op jit(solution)/shard_map/jit(_take)/select_n | solution.py:76
  48.1 7.5 %all-to-all-start.1 = ((bf16[256,128,128]{2,0,1:T(8,128)(2,1)}), bf16[256,128,128]{2,0,1:T(8,128)(2,1)}, u32[]{:S(2)}, u32[]{:S(2)}) async-start(bf16[256,128,128]{2,0,1:T(8,128)(2,1)} %select_bitcast_fusion), calls=%async_computation.1 | async-start | bytes 16777216 | tf_op jit(solution)/shard_map/all_to_all | solution.py:77
  56.0 5.4 %select_reduce_fusion = (f32[32,128,128]{2,1,0:T(8,128)}, f32[32,128,128]{2,1,0:T(8,128)S(1)}) fusion(f32[32,2,128,128]{3,2,1,0:T(8,128)} %param.5, pred[32,2]{1,0:T(8,128)(4,1)S(1)} %copy.66), kind=kLoop, calls=%fused_computation.7 | loop fusion | flops 3145728 | bytes 8388672 | tf_op jit(solution)/shard_map/reduce_sum | solution.py:83
  66.6 174.8 %all-to-all-done.1 = bf16[256,128,128]{2,0,1:T(8,128)(2,1)} async-done(((bf16[256,128,128]{2,0,1:T(8,128)(2,1)}), bf16[256,128,128]{2,0,1:T(8,128)(2,1)}, u32[]{:S(2)}, u32[]{:S(2)}) %all-to-all-start.1) | async-done | bytes 8388640 | tf_op jit(solution)/shard_map/all_to_all | solution.py:77
  241.4 5.6 %gather_fusion.1 = bf16[32,256,128]{2,1,0:T(8,128)(2,1)} fusion(bf16[256,128,128]{2,0,1:T(8,128)(2,1)} %all-to-all-done.1, s32[1024]{0:T(1024)S(1)} %pad_clamp_fusion), kind=kCustom, calls=%fused_computation.1 | custom fusion | bytes 4194432 | tf_op jit(solution)/shard_map/jit(_take)/gather | solution.py:78
  247.0 5.5 %multiply_reduce_fusion.1 = (f32[]{:T(128)}, bf16[32,128,256]{2,1,0:T(8,128)(2,1)S(1)}) fusion(f32[32,128,256]{2,1,0:T(8,128)} %fusion.18, bf16[32,256,128]{2,1,0:T(8,128)(2,1)} %gather_fusion.1, pred[32]{0:T(512)(128)(4,1)S(1)} %get-tuple-element.7, f32[32,128,128]{2,1,0:T(8,128)} %get-tuple-element.3), kind=kOutput, calls=%fused_computation.6 | convolution fusion | flops 274202624 | bytes 10485796 | tf_op jit(solution)/shard_map/qlh,lhy->qly/dot_general | solution.py:95
  257.3 46.3 %reduce-scatter.3.cloned.1.call-done = f32[8,256,128]{2,1,0:T(8,128)} async-done(((f32[32,256,128]{2,1,0:T(8,128)}), f32[8,256,128]{2,1,0:T(8,128)}) %reduce-scatter.3.cloned.1.call-update) | async-done | bytes 1048592 | tf_op jit(solution)/shard_map/reduce_scatter | solution.py:25
  303.6 3.0 select_reduce_fusion.3
  307.4 9.0 %all_gather.19 = f32[32,128]{1,0:T(8,128)S(1)} all-gather(f32[8,128]{1,0:T(8,128)S(1)} %add_multiply_fusion.1), channel_id=1, replica_groups=mesh['samp'=4,'var_0'=4,'var_1'=8,'var_2'=2] {'samp'}, dimensions={0}, use_global_device_ids=true | all-gather | bytes 20480 | tf_op jit(solution)/shard_map/all_gather | solution.py:132
  316.5 23.4 %all-gather.7.cloned.1.call-done = f32[32,128,128]{2,1,0:T(8,128)} async-done(((f32[8,128,128]{2,1,0:T(8,128)}), f32[32,128,128]{2,1,0:T(8,128)}) %all-gather.7.cloned.1.call-update) | async-done | bytes 2097168 | tf_op jit(solution)/shard_map/all_gather | solution.py:131
  341.7 34.2 %all-gather.5.cloned.1.call-done = f32[32,128,128]{2,1,0:T(8,128)} async-done(((f32[8,128,128]{2,1,0:T(8,128)}), f32[32,128,128]{2,1,0:T(8,128)}) %all-gather.5.cloned.1.call-update) | async-done | bytes 2097168 | tf_op jit(solution)/shard_map/all_gather | solution.py:130
  384.3 49.6 %reduce-scatter.5.cloned.1.call-done = f32[8,256,128]{2,1,0:T(8,128)} async-done(((f32[32,256,128]{2,1,0:T(8,128)}), f32[8,256,128]{2,1,0:T(8,128)}) %reduce-scatter.5.cloned.1.call-update) | async-done | bytes 1048592 | tf_op jit(solution)/shard_map/reduce_scatter | solution.py:25
  433.8 3.0 select_reduce_fusion.2
  449.3 7.4 %psum.28 = f32[2]{0:T(128)S(1)} all-reduce(f32[2]{0:T(128)S(1)} %pad_maximum_fusion.2), channel_id=1, replica_groups=mesh['samp'=4,'var_0'=4,'var_1'=8,'var_2'=2] {'samp'}, use_global_device_ids=true, to_apply=%region_17.18 | all-reduce | flops 2 | bytes 16 | tf_op jit(solution)/shard_map/psum | solution.py:30
  456.6 9.2 %psum.29 = f32[2]{0:T(128)S(1)} all-reduce(f32[2]{0:T(128)S(1)} %psum.28), channel_id=1, replica_groups=mesh['samp'=4,'var_0'=4,'var_1'=8,'var_2'=2] {'var_0'}, use_global_device_ids=true, to_apply=%region_18.19 | all-reduce | flops 2 | bytes 16 | tf_op jit(solution)/shard_map/psum | solution.py:30
  465.8 13.8 %psum.30 = f32[2]{0:T(128)S(1)} all-reduce(f32[2]{0:T(128)S(1)} %psum.29), channel_id=1, replica_groups=mesh['samp'=4,'var_0'=4,'var_1'=8,'var_2'=2] {'var_1'}, use_global_device_ids=true, to_apply=%region_19.20 | all-reduce | flops 2 | bytes 16 | tf_op jit(solution)/shard_map/psum | solution.py:30
  479.6 9.4 %psum.31 = f32[2]{0:T(128)} all-reduce(f32[2]{0:T(128)S(1)} %psum.30), channel_id=1, replica_groups=mesh['samp'=4,'var_0'=4,'var_1'=8,'var_2'=2] {'var_2'}, use_global_device_ids=true, to_apply=%region_20.21 | all-reduce | flops 2 | bytes 16 | tf_op jit(solution)/shard_map/psum | solution.py:30
  489.0 10.0 %all_gather.23 = f32[32,128]{1,0:T(8,128)S(1)} all-gather(f32[8,128]{1,0:T(8,128)S(1)} %add_multiply_fusion), channel_id=1, replica_groups=mesh['samp'=4,'var_0'=4,'var_1'=8,'var_2'=2] {'samp'}, dimensions={0}, use_global_device_ids=true | all-gather | bytes 20480 | tf_op jit(solution)/shard_map/all_gather | solution.py:132
  499.0 7.1 %all-gather.9.cloned.1.call-done = f32[32,128,128]{2,1,0:T(8,128)} async-done(((f32[8,128,128]{2,1,0:T(8,128)}), f32[32,128,128]{2,1,0:T(8,128)}) %all-gather.9.cloned.1.call-update) | async-done | bytes 2097168 | tf_op jit(solution)/shard_map/all_gather | solution.py:130
  506.1 4.7 broadcast_select_fusion
  (67 shorter events, 35.1 us)
Async XLA Ops:
  8.9 22.3 %all-to-all-start = ((s32[64,2,1]{1,2,0:T(1,128)}), s32[64,2,1]{1,2,0:T(1,128)S(1)}, u32[]{:S(2)}, u32[]{:S(2)}) async-start(s32[64,2,1]{1,2,0:T(1,128)} %bitcast.2), calls=%async_computation | async-start | bytes 65536 | tf_op jit(solution)/shard_map/all_to_all | solution.py:74
  48.1 7.7 %copy-start.6 = (s32[32,2]{0,1:T(2,128)S(1)}, s32[32,2]{0,1:T(2,128)}, u32[]{:S(2)}) copy-start(s32[32,2]{0,1:T(2,128)} %param.7) | copy-start | bytes 772
  48.1 193.3 %all-to-all-start.1 = ((bf16[256,128,128]{2,0,1:T(8,128)(2,1)}), bf16[256,128,128]{2,0,1:T(8,128)(2,1)}, u32[]{:S(2)}, u32[]{:S(2)}) async-start(bf16[256,128,128]{2,0,1:T(8,128)(2,1)} %select_bitcast_fusion), calls=%async_computation.1 | async-start | bytes 16777216 | tf_op jit(solution)/shard_map/all_to_all | solution.py:77
  55.6 248.0 %reduce-scatter.3.cloned.1.call-start = ((), (), s32[]{:S(2)}) async-start(), calls=%async_computation.4 | async-start | bytes 5242880 | tf_op jit(solution)/shard_map/reduce_scatter | solution.py:25
  61.4 2.4 copy-start.5
  62.5 1.3 copy-start.4
  252.5 1.6 copy-start
  257.3 82.6 %all-gather.7.cloned.1.call-start = ((), (), s32[]{:S(2)}) async-start(), calls=%async_computation.6 | async-start | bytes 2621440 | tf_op jit(solution)/shard_map/all_gather | solution.py:131
  306.6 69.3 %all-gather.5.cloned.1.call-start = ((), (), s32[]{:S(2)}) async-start(), calls=%async_computation.5 | async-start | bytes 2621440 | tf_op jit(solution)/shard_map/all_gather | solution.py:130
  307.3 126.5 %reduce-scatter.5.cloned.1.call-start = ((), (), s32[]{:S(2)}) async-start(), calls=%async_computation.7 | async-start | bytes 5242880 | tf_op jit(solution)/shard_map/reduce_scatter | solution.py:25
  375.9 2.5 copy-start.1
  384.2 54.6 %copy-start.2 = (f32[32,128,128]{2,1,0:T(8,128)S(1)}, f32[32,128,128]{2,1,0:T(8,128)}, u32[]{:S(2)}) copy-start(f32[32,128,128]{2,1,0:T(8,128)} %get-tuple-element.3) | copy-start | bytes 6291460
  384.2 114.8 %all-gather.11.cloned.1.call-start = ((), (), s32[]{:S(2)}) async-start(), calls=%async_computation.9 | async-start | bytes 2621440 | tf_op jit(solution)/shard_map/all_gather | solution.py:131
  436.9 69.2 %all-gather.9.cloned.1.call-start = ((), (), s32[]{:S(2)}) async-start(), calls=%async_computation.8 | async-start | bytes 2621440 | tf_op jit(solution)/shard_map/all_gather | solution.py:130
  440.0 6.1 %copy-start.3 = (f32[32,128,128]{2,1,0:T(8,128)S(1)}, f32[32,128,128]{2,1,0:T(8,128)}, u32[]{:S(2)}) copy-start(f32[32,128,128]{2,1,0:T(8,128)} %all-gather.5.cloned.1.call-done) | copy-start | bytes 6291460
Sparse Core Ops, SparseCore 0:
  257.4 46.1 reduce-scatter.2
  306.7 33.0 all-gather.6
  342.4 33.4 all-gather.4
  384.3 49.4 reduce-scatter.4
  437.0 33.2 all-gather.10
  472.6 33.4 all-gather.8
where the time goes:
time: 519 us; the launch traced here: 518 us
  waiting for transfers between devices  340 us (66%)
  blocking collectives  58.8 us (11%)
  other arithmetic  37.5 us (7%)
  local copies, waits for them, and re-layouts  25.9 us (5%)
  starting transfers between devices  20.9 us (4%)
  between operations  19.6 us (4%)
  matrix products  15.8 us (3%)
    all_to_all x1, waiting for transfers between devices, body(): lax.all_to_all(outgoing, VAR, split_axis=1, concat_axis=1, tiled=True)  175 us
    reduce_scatter x2, waiting for transfers between devices, in_one_piece(): lax.psum_scatter(both, axis, scatter_dimension=dim, tiled=True)  95.8 us
    all_gather x2, waiting for transfers between devices, body(): lax.all_gather(updated[0], 'samp', axis=0, tiled=True)  41.3 us
    psum x4, blocking collectives, one_axis_at_a_time(): return functools.reduce(lax.psum, axes, x)  39.7 us
    all_gather x2, waiting for transfers between devices, body(): lax.all_gather(updated[1], 'samp', axis=0, tiled=True)  23.4 us
    all_gather x2, blocking collectives, body(): lax.all_gather(updated[2], 'samp', axis=0, tiled=True)  19 us
    all_to_all x1, starting transfers between devices, body(): lax.all_to_all(wanted, VAR, split_axis=0, concat_axis=0, tiled=True)  13 us
  transfers between devices with their start and end apart: 8, of which 7 were waited for; matrix products, arithmetic and copies ran while one was open for 5% of the time, Pallas kernels for 0%

commit v1 on v0

v1 whole, which is shorter than its diff:
```python
import functools

import jax
import jax.numpy as jnp
from jax import lax
from jax.experimental import pallas as pl
from jax.experimental.pallas import tpu as pltpu
from jax.sharding import Mesh
from jax.sharding import PartitionSpec as P

STEPS = 2
STEP_LENGTH = 0.5
PENALTY = 0.5
VAR = ("var_0", "var_1", "var_2")
ALL = ("samp", "var_0", "var_1", "var_2")
F32 = jnp.float32
BF16 = jnp.bfloat16


def shifts(x, axis, which):
    n = lax.axis_size(axis)
    return [lax.ppermute(x, axis, [(i, (i + k) % n) for i in range(n)]) for k in which]


def everyones(x, axes):
    for axis in axes:
        x = jnp.stack([x] + shifts(x, axis, range(1, lax.axis_size(axis))))
    return x


def pick_kernel(sizes, cols, at_ref, wanted_ref, table_ref, out_ref):
    n0, n1, n2 = sizes
    share = pl.program_id(0)

    @pl.loop(0, n0 * n1 * n2)
    def _(d):
        k0 = lax.rem(at_ref[0] - d // (n1 * n2) + n0, n0)
        k1 = lax.rem(at_ref[1] - lax.rem(d // n2, n1) + n1, n1)
        k2 = lax.rem(at_ref[2] - lax.rem(d, n2) + n2, n2)
        row = ((k0 * n2 + k2) * n1 + k1) * cols + share * out_ref.shape[1]
        for j in range(out_ref.shape[1]):
            out_ref[d, j] = table_ref[wanted_ref[row + j]]


def pick(wanted, table, sizes, cols, shares):
    devices = sizes[0] * sizes[1] * sizes[2]
    each = cols // shares
    at = jnp.stack([lax.axis_index(a) for a in VAR]).astype(jnp.int32)
    piece = table.shape[1:]
    return pl.pallas_call(
        functools.partial(pick_kernel, sizes, cols),
        grid_spec=pltpu.PrefetchScalarGridSpec(
            num_scalar_prefetch=2,
            grid=(shares,),
            in_specs=[pl.BlockSpec(table.shape, lambda i, a, w: (0, 0, 0))],
            out_specs=pl.BlockSpec((devices, each) + piece, lambda i, a, w: (i, 0, 0, 0)),
        ),
        out_shape=jax.ShapeDtypeStruct((shares * devices, each) + piece, table.dtype),
        compiler_params=pltpu.CompilerParams(vmem_limit_bytes=32 << 20),
    )(at, wanted, table)


def shrink(v, level):
    return jnp.where(v > level, v - level, jnp.where(v < -level, v + level, 0.0))


def split3(g):
    hi = g.astype(BF16)
    rest = g - hi.astype(F32)
    mid = rest.astype(BF16)
    return hi, mid, (rest - mid.astype(F32)).astype(BF16)


def steps_kernel(total_rows, info_ref, own_ref, p1_ref, p2_ref, p3_ref, far_ref, blocks_ref, diag_ref,
                 out_ref, new_diag_ref, obj_ref):
    j = pl.program_id(0)
    samp = info_ref[0]
    rows = own_ref.shape[0]
    gram = None
    for k, near_ref in enumerate((own_ref, p1_ref, p2_ref, p3_ref)):
        q = lax.rem(samp + 4 - k, 4)
        far = far_ref[0, pl.ds(pl.multiple_of(q * rows, rows), rows), :]
        x = jnp.concatenate([near_ref[...], far], axis=1)
        term = lax.dot_general(x, x, (((0,), (0,)), ((), ())), preferred_element_type=F32)
        gram = term if gram is None else gram + term
    parts = split3(gram)
    width = out_ref.shape[-1]
    eye = lax.broadcasted_iota(jnp.int32, (width, width), 0) == lax.broadcasted_iota(jnp.int32, (width, width), 1)
    where_diag = info_ref[2 + j]
    db = jnp.where(eye, 0.0, blocks_ref[0, where_diag])
    ob = blocks_ref[0, 1 - where_diag]
    dv = diag_ref[pl.ds(j, 1), :]
    objs = []
    for _ in range(STEPS):
        full = jnp.where(eye, jnp.broadcast_to(dv, (width, width)), db)
        w = jnp.concatenate([full, ob], axis=0).astype(BF16)
        g = sum(jnp.dot(p, w, preferred_element_type=F32) for p in reversed(parts))
        part = jnp.sum(w.astype(F32) * g, axis=0, keepdims=True) / (2.0 * total_rows)
        part = part - jnp.log(dv)
        part = part + PENALTY * (jnp.sum(jnp.abs(db), axis=0, keepdims=True) + jnp.sum(jnp.abs(ob), axis=0, keepdims=True))
        objs.append(part)
        g = g / total_rows
        gd, go = g[:width], g[width:]
        along = jnp.sum(jnp.where(eye, gd, 0.0), axis=0, keepdims=True)
        db = jnp.where(eye, 0.0, shrink(db - STEP_LENGTH * gd, STEP_LENGTH * PENALTY))
        ob = shrink(ob - STEP_LENGTH * go, STEP_LENGTH * PENALTY)
        m = dv - STEP_LENGTH * along
        dv = 0.5 * (m + jnp.sqrt(m * m + 4.0 * STEP_LENGTH))
    out_ref[0, where_diag] = db.astype(out_ref.dtype)
    out_ref[0, 1 - where_diag] = ob.astype(out_ref.dtype)
    new_diag_ref[pl.ds(j, 1), :] = dv

    @pl.when(j == 0)
    def _():
        obj_ref[...] = jnp.zeros_like(obj_ref)

    for i, part in enumerate(objs):
        obj_ref[i : i + 1, :] += part


def iterate(info, observed, received, far, blocks, diag_rows, total_rows):
    rows = observed.shape[0]
    each, width = diag_rows.shape
    near = pl.BlockSpec((rows, width), lambda j, f: (0, j))
    return pl.pallas_call(
        functools.partial(steps_kernel, total_rows),
        grid_spec=pltpu.PrefetchScalarGridSpec(
            num_scalar_prefetch=1,
            grid=(each,),
            in_specs=[
                pl.BlockSpec((rows, width), lambda j, f: (0, f[1] + j)),
                near,
                near,
                near,
                pl.BlockSpec((1, far.shape[1], width), lambda j, f: (j, 0, 0)),
                pl.BlockSpec((1, 2, width, width), lambda j, f: (f[1] + j, 0, 0, 0)),
                pl.BlockSpec((each, width), lambda j, f: (0, 0)),
            ],
            out_specs=[
                pl.BlockSpec((1, 2, width, width), lambda j, f: (j, 0, 0, 0)),
                pl.BlockSpec((each, width), lambda j, f: (0, 0)),
                pl.BlockSpec((8, width), lambda j, f: (0, 0)),
            ],
        ),
        out_shape=[
            jax.ShapeDtypeStruct((each, 2, width, width), BF16),
            jax.ShapeDtypeStruct((each, width), F32),
            jax.ShapeDtypeStruct((8, width), F32),
        ],
        compiler_params=pltpu.CompilerParams(vmem_limit_bytes=32 << 20),
    )(info, observed, *received, far, blocks, diag_rows)


def place_kernel(samp_ref, own_ref, p1_ref, p2a_ref, p2b_ref, p3_ref, out_ref):
    samp, half = samp_ref[0], pl.num_programs(0) // 2
    out_ref[samp, 0] = own_ref[0].astype(F32)
    out_ref[lax.rem(samp + 3, 4), 0] = p1_ref[0].astype(F32)
    out_ref[lax.rem(samp + 1, 4), 0] = p3_ref[0].astype(F32)

    @pl.when(pl.program_id(0) < half)
    def _():
        out_ref[lax.rem(samp + 2, 4), 0] = p2a_ref[0].astype(F32)

    @pl.when(pl.program_id(0) >= half)
    def _():
        out_ref[lax.rem(samp + 2, 4), 0] = p2b_ref[0].astype(F32)


def gather_blocks(new, samp):
    each, tail = new.shape[0], new.shape[1:]
    half = each // 2
    (p1,) = shifts(new, "samp", (1,))
    (p3,) = shifts(new, "samp", (3,))
    (p2a,) = shifts(p1[:half], "samp", (1,))
    (p2b,) = shifts(p3[half:], "samp", (3,))
    zeros = (0,) * len(tail)
    whole = pl.BlockSpec((1,) + tail, lambda j, f: (j,) + zeros)
    out = pl.pallas_call(
        place_kernel,
        grid_spec=pltpu.PrefetchScalarGridSpec(
            num_scalar_prefetch=1,
            grid=(each,),
            in_specs=[
                whole,
                whole,
                pl.BlockSpec((1,) + tail, lambda j, f: (jnp.minimum(j, half - 1),) + zeros),
                pl.BlockSpec((1,) + tail, lambda j, f: (jnp.maximum(j - half, 0),) + zeros),
                whole,
            ],
            out_specs=pl.BlockSpec((4, 1) + tail, lambda j, f: (0, j) + zeros),
        ),
        out_shape=jax.ShapeDtypeStruct((4, each) + tail, F32),
        compiler_params=pltpu.CompilerParams(vmem_limit_bytes=32 << 20),
    )(samp[None], new, p1, p2a, p2b, p3)
    return out.reshape((4 * each,) + tail)


def body(observed, blocks, diagonal, pattern):
    cols, _, width, _ = blocks.shape
    rows = observed.shape[0]
    sizes = tuple(lax.axis_size(a) for a in VAR)
    devices = sizes[0] * sizes[1] * sizes[2]
    shares = lax.axis_size("samp")
    each = cols // shares
    piece_rows = rows // devices
    total_rows = rows * shares
    samp = lax.axis_index("samp").astype(jnp.int32)
    columns = lax.axis_index(VAR) * cols + jnp.arange(cols, dtype=jnp.int32)
    on_diag = pattern == columns[:, None]
    off_row = jnp.where(on_diag[:, 0], pattern[:, 1], pattern[:, 0])

    received = [
        shifts(lax.dynamic_slice_in_dim(observed, lax.rem(samp + k, shares) * each * width, each * width, 1), "samp", (k,))[0]
        for k in (1, 2, 3)
    ]
    pieces = observed.reshape(devices, piece_rows, cols, width).transpose(0, 2, 1, 3)
    table = lax.all_to_all(pieces, VAR, split_axis=0, concat_axis=0, tiled=True)
    wanted = everyones(off_row, ("var_1", "var_2", "var_0"))
    outgoing = pick(wanted.reshape(-1), table.reshape(devices * cols, piece_rows, width), sizes, cols, shares)
    far = lax.all_to_all(outgoing, ALL, split_axis=0, concat_axis=0, tiled=True)
    far = far.transpose(1, 0, 2, 3).reshape(each, total_rows, width)

    start = samp * each
    which = jnp.where(on_diag[:, 0], 0, 1).astype(jnp.int32)
    info = jnp.concatenate([jnp.stack([samp, start]), lax.dynamic_slice_in_dim(which, start, each, 0)])
    diag_rows = lax.dynamic_slice_in_dim(diagonal.reshape(cols, width), start, each, 0)
    new, new_diag, obj = iterate(info, observed, received, far, blocks, diag_rows, total_rows)

    new_blocks = gather_blocks(new, samp)
    near_diags = [new_diag] + shifts(new_diag, "samp", (1, 2, 3))
    order = [jnp.where(samp == q, near_diags[0], jnp.where(lax.rem(samp + 3, 4) == q, near_diags[1], jnp.where(lax.rem(samp + 2, 4) == q, near_diags[2], near_diags[3]))) for q in range(4)]
    new_diagonal = jnp.stack(order).reshape(-1)
    objective = jnp.sum(obj[:STEPS], axis=1) / (cols * devices * width)
    objective = functools.reduce(lax.psum, ALL, objective)
    return (new_blocks, new_diagonal, objective)


def solution(mesh):
    torus = Mesh(mesh.devices.reshape(mesh.shape["samp"], 4, 8, 2), ALL)
    placed = (P("samp", VAR), P(VAR, None, None, None), P(VAR), P(VAR, None))
    return jax.shard_map(
        body,
        mesh=torus,
        in_specs=placed,
        out_specs=(P(VAR, None, None, None), P(VAR), P()),
        check_vma=False,
    )
```

time: 519 us -> 230 us (0.44)
  waiting for transfers between devices: 340 us -> 92.7 us
  starting transfers between devices: 20.9 us -> 60.4 us
  other arithmetic: 37.5 us -> 0.92 us
  Pallas kernels: 0 us -> 22.3 us
  between operations: 19.6 us -> 0.87 us
  blocking collectives: 58.8 us -> 40.8 us
  matrix products: 15.8 us -> 0 us
  local copies, waits for them, and re-layouts: 25.9 us -> 11.5 us
    all_to_all x2, waiting for transfers between devices: 178 us -> 47.6 us  [the longest x1 47.6 us: body(): far = lax.all_to_all(outgoing, ALL, split_axis=0, concat_axis=0, tiled=True)]
    reduce_scatter x2 -> x0, waiting for transfers between devices: 95.8 us -> none  [in_one_piece(): lax.psum_scatter(both, axis, scatter_dimension=dim, tiled=True)]
    all_gather x4 -> x0, waiting for transfers between devices: 64.7 us -> none  [the longest x2 41.3 us: body(): lax.all_gather(updated[0], 'samp', axis=0, tiled=True)]
    ppermute x0 -> x21, waiting for transfers between devices: none -> 45.1 us  [shifts(): lax.ppermute(x, axis, [(i, (i + k) % n) for i in range(n)])]
    ppermute x0 -> x21, starting transfers between devices: none -> 35.1 us  [shifts(): lax.ppermute(x, axis, [(i, (i + k) % n) for i in range(n)])]
    pallas_call x0 -> x3, Pallas kernels: none -> 22.3 us  [the longest x1 10.1 us: iterate(): pl.pallas_call(functools.partial(steps_kernel, total_rows), grid_spec=plt...]
    reduce_sum x12 -> x1, other arithmetic: 19.8 us -> 0.11 us  [body(): objective = jnp.sum(obj[:STEPS], axis=1) / (cols * devices * width)]
    all_gather x2 -> x0, blocking collectives: 19 us -> none  [body(): lax.all_gather(updated[2], 'samp', axis=0, tiled=True)]
  transfers between devices with their start and end apart: 8 -> 23, of which waited for: 7 -> 8; matrix products, arithmetic and copies ran while one was open for 5% -> 2% of each run, Pallas kernels for 0% -> 0%
where the time goes in v1:
time: 230 us; the launch traced here: 229 us
  waiting for transfers between devices  92.7 us (40%)
  starting transfers between devices  60.4 us (26%)
  blocking collectives  40.8 us (18%)
  Pallas kernels  22.3 us (10%)
  local copies, waits for them, and re-layouts  11.5 us (5%)
    all_to_all x1, waiting for transfers between devices, body(): far = lax.all_to_all(outgoing, ALL, split_axis=0, concat_axis=0, tiled=True)  47.6 us
    ppermute x21, waiting for transfers between devices, shifts(): lax.ppermute(x, axis, [(i, (i + k) % n) for i in range(n)])  45.1 us
    psum x4, blocking collectives, body(): objective = functools.reduce(lax.psum, ALL, objective)  40.8 us
    ppermute x21, starting transfers between devices, shifts(): lax.ppermute(x, axis, [(i, (i + k) % n) for i in range(n)])  35.1 us
    all_to_all x1, starting transfers between devices, body(): table = lax.all_to_all(pieces, VAR, split_axis=0, concat_axis=0, tiled=True)  13.1 us
    all_to_all x1, starting transfers between devices, body(): far = lax.all_to_all(outgoing, ALL, split_axis=0, concat_axis=0, tiled=True)  12.1 us
    pallas_call x1, Pallas kernels, iterate(): pl.pallas_call(functools.partial(steps_kernel, total_rows), grid_spec=plt...  10.1 us
    pallas_call x1, Pallas kernels, pick(): pl.pallas_call(functools.partial(pick_kernel, sizes, cols), grid_spec=plt...  8.69 us
  transfers between devices with their start and end apart: 23, of which 8 were waited for; matrix products, arithmetic and copies ran while one was open for 2% of the time, Pallas kernels for 0%

profile of v1, /device:TPU:1, one launch (start us, length us, event | category | flops | bytes accessed | tf_op | source)
XLA Modules:
  0.0 229.4 jit_solution(770290974962567207)
XLA Ops:
  2.7 2.4 %copy.11 = bf16[64,4,32,128]{3,1,2,0:T(4,128)(2,1)} copy(bf16[64,4,32,128]{3,2,1,0:T(8,128)(2,1)S(1)} %bitcast.51) | data formatting | bytes 4194304 | tf_op jit(solution)/shard_map/reshape | solution.py:216
  5.1 13.1 %all-to-all-start = ((bf16[64,32,4,128]{3,2,1,0:T(4,128)(2,1)}), bf16[64,32,4,128]{3,2,1,0:T(4,128)(2,1)S(1)}, u32[]{:S(2)}, u32[]{:S(2)}) async-start(bf16[64,32,4,128]{3,2,1,0:T(4,128)(2,1)} %bitcast.50), calls=%async_computation | async-start | bytes 4194304 | tf_op jit(solution)/shard_map/all_to_all | solution.py:217
  19.8 2.1 collective-permute-start.4
  21.9 2.4 %collective-permute-start.5 = (s32[32]{0:T(128)S(1)}, s32[32]{0:T(128)S(1)}, u32[]{:S(2)}, u32[]{:S(2)}) collective-permute-start(s32[32]{0:T(128)S(1)} %bitcast.60), channel_id=1, source_target_pairs={{0,6},{2,8},{4,10},{6,12},{8,14},{10,0},{12,2},{14,4},{1,7},{3,9},... | collective-permute-start | bytes 392 | tf_op jit(solution)/shard_map/ppermute | solution.py:22
  24.3 2.1 collective-permute-start.6
  26.3 2.4 %collective-permute-start.7 = (s32[32]{0:T(128)S(1)}, s32[32]{0:T(128)S(1)}, u32[]{:S(2)}, u32[]{:S(2)}) collective-permute-start(s32[32]{0:T(128)S(1)} %bitcast.62), channel_id=1, source_target_pairs={{0,10},{2,12},{4,14},{6,0},{8,2},{10,4},{12,6},{14,8},{1,11},{3,13... | collective-permute-start | bytes 392 | tf_op jit(solution)/shard_map/ppermute | solution.py:22
  28.7 35.0 %collective-permute-done.3 = s32[32]{0:T(128)S(1)} collective-permute-done((s32[32]{0:T(128)S(1)}, s32[32]{0:T(128)S(1)}, u32[]{:S(2)}, u32[]{:S(2)}) %collective-permute-start.3) | collective-permute-done | bytes 160 | tf_op jit(solution)/shard_map/ppermute | solution.py:22
  66.0 4.0 %collective-permute-start.9 = (s32[32]{0:T(128)S(1)}, s32[32]{0:T(128)S(1)}, u32[]{:S(2)}, u32[]{:S(2)}) collective-permute-start(s32[32]{0:T(128)S(1)} %bitcast.64), channel_id=1, source_target_pairs={{0,14},{2,0},{4,2},{6,4},{8,6},{10,8},{12,10},{14,12},{1,15},{3,1}... | collective-permute-start | bytes 392 | tf_op jit(solution)/shard_map/ppermute | solution.py:22
  73.4 2.7 %collective-permute-start.13 = (s32[2,8,32]{2,1,0:T(8,128)S(1)}, s32[2,8,32]{2,1,0:T(8,128)S(1)}, u32[]{:S(2)}, u32[]{:S(2)}) collective-permute-start(s32[2,8,32]{2,1,0:T(8,128)S(1)} %get-tuple-element.17), channel_id=1, source_target_pairs={{0,48},{16,0},{32,16},{48,32},{1,49},{17,1},{33,17},{49,33},{2,50}... | collective-permute-start | bytes 6152 | tf_op jit(solution)/shard_map/ppermute | solution.py:22
  77.2 2.9 %collective-permute-done.12 = s32[2,8,32]{2,1,0:T(8,128)S(1)} collective-permute-done((s32[2,8,32]{2,1,0:T(8,128)S(1)}, s32[2,8,32]{2,1,0:T(8,128)S(1)}, u32[]{:S(2)}, u32[]{:S(2)}) %collective-permute-start.12) | collective-permute-done | bytes 2080 | tf_op jit(solution)/shard_map/ppermute | solution.py:22
  80.2 8.7 %shard_map.67 = bf16[256,8,4,128]{3,2,1,0:T(4,128)(2,1)S(1)} custom-call(s32[3]{0:T(128)S(1)} %pad_add_fusion.3.at_ref, s32[2048]{0:T(1024)S(1)} %reshape.61.wanted_ref, bf16[2048,4,128]{2,1,0:T(4,128)(2,1)S(1)} %bitcast.48), custom_call_target="tpu_custom_call" | custom-call | tf_op jit(solution)/shard_map/pallas_call | solution.py:50
  90.2 12.1 %all-to-all-start.1 = ((bf16[256,8,4,128]{3,2,1,0:T(4,128)(2,1)}), bf16[256,8,4,128]{3,2,1,0:T(4,128)(2,1)}, u32[]{:S(2)}, u32[]{:S(2)}) async-start(bf16[256,8,4,128]{3,2,1,0:T(4,128)(2,1)} %copy-done.2), calls=%async_computation.1 | async-start | bytes 4194304 | tf_op jit(solution)/shard_map/all_to_all | solution.py:220
  105.0 2.4 %collective-permute-start.1 = (bf16[256,1024]{1,0:T(8,128)(2,1)}, bf16[256,1024]{1,0:T(8,128)(2,1)S(1)}, u32[]{:S(2)}, u32[]{:S(2)}) collective-permute-start(bf16[256,1024]{1,0:T(8,128)(2,1)} %get-tuple-element.10), channel_id=1, source_target_pairs={{0,128},{64,192},{128,0},{192,64},{1,129},{65,193},{129,1},{193,65... | collective-permute-start | bytes 1572872 | tf_op jit(solution)/shard_map/ppermute | solution.py:22
  108.7 47.6 %all-to-all-done.1 = bf16[256,8,4,128]{3,2,1,0:T(4,128)(2,1)} async-done(((bf16[256,8,4,128]{3,2,1,0:T(4,128)(2,1)}), bf16[256,8,4,128]{3,2,1,0:T(4,128)(2,1)}, u32[]{:S(2)}, u32[]{:S(2)}) %all-to-all-start.1) | async-done | bytes 2097184 | tf_op jit(solution)/shard_map/all_to_all | solution.py:220
  156.3 2.5 %copy.8 = bf16[8,256,4,128]{3,2,1,0:T(4,128)(2,1)S(1)} copy(bf16[8,256,4,128]{3,2,0,1:T(4,128)(2,1)} %bitcast.23) | data formatting | bytes 4194304 | tf_op jit(solution)/shard_map/transpose | solution.py:221
  160.6 10.1 %shard_map.68 = (bf16[8,2,128,128]{3,2,1,0:T(8,128)(2,1)S(1)}, f32[8,128]{1,0:T(8,128)S(1)}, f32[8,128]{1,0:T(8,128)S(1)}) custom-call(s32[10]{0:T(128)S(1)} %pad_add_fusion.2.info_ref, bf16[256,4096]{1,0:T(8,128)(2,1)S(1)} %copy-done.1, bf16[256,1024]{1,0:T(8,128)(2,1)S(1)} %collective-permute-done.p1_ref, bf16[256,1024]{1,0:T(8,128)(2,1)S(1)} %copy-done.5, ...), custom_call_target="tpu_custom_call" | custom-call | tf_op jit(solution)/shard_map/pallas_call | solution.py:125
  171.1 2.3 %collective-permute-start.16 = (bf16[8,2,128,128]{3,2,1,0:T(8,128)(2,1)S(1)}, bf16[8,2,128,128]{3,2,1,0:T(8,128)(2,1)S(1)}, u32[]{:S(2)}, u32[]{:S(2)}) collective-permute-start(bf16[8,2,128,128]{3,2,1,0:T(8,128)(2,1)S(1)} %get-tuple-element.6.own_ref), channel_id=1, source_target_pairs={{0,192},{64,0},{128,64},{192,128},{1,193},{65,1},{129,65},{193,129... | collective-permute-start | bytes 1572872 | tf_op jit(solution)/shard_map/ppermute | solution.py:22
  176.2 10.9 %psum.28 = f32[2]{0:T(128)S(1)} all-reduce(f32[2]{0:T(128)S(1)} %broadcast_multiply_fusion), channel_id=1, replica_groups=mesh['samp'=4,'var_0'=4,'var_1'=8,'var_2'=2] {'samp'}, use_global_device_ids=true, to_apply=%region_1.2 | all-reduce | flops 2 | bytes 16 | tf_op jit(solution)/shard_map/psum | solution.py:234
  187.1 8.5 %psum.29 = f32[2]{0:T(128)S(1)} all-reduce(f32[2]{0:T(128)S(1)} %psum.28), channel_id=1, replica_groups=mesh['samp'=4,'var_0'=4,'var_1'=8,'var_2'=2] {'var_0'}, use_global_device_ids=true, to_apply=%region_2.3 | all-reduce | flops 2 | bytes 16 | tf_op jit(solution)/shard_map/psum | solution.py:234
  195.6 12.0 %psum.30 = f32[2]{0:T(128)S(1)} all-reduce(f32[2]{0:T(128)S(1)} %psum.29), channel_id=1, replica_groups=mesh['samp'=4,'var_0'=4,'var_1'=8,'var_2'=2] {'var_1'}, use_global_device_ids=true, to_apply=%region_3.4 | all-reduce | flops 2 | bytes 16 | tf_op jit(solution)/shard_map/psum | solution.py:234
  207.6 9.4 %psum.31 = f32[2]{0:T(128)} all-reduce(f32[2]{0:T(128)S(1)} %psum.30), channel_id=1, replica_groups=mesh['samp'=4,'var_0'=4,'var_1'=8,'var_2'=2] {'var_2'}, use_global_device_ids=true, to_apply=%region_4.5 | all-reduce | flops 2 | bytes 16 | tf_op jit(solution)/shard_map/psum | solution.py:234
  217.2 2.7 %collective-permute-start.17 = (bf16[4,2,128,128]{3,2,1,0:T(8,128)(2,1)S(1)}, bf16[4,2,128,128]{3,2,1,0:T(8,128)(2,1)S(1)}, u32[]{:S(2)}, u32[]{:S(2)}) collective-permute-start(bf16[4,2,128,128]{3,2,1,0:T(8,128)(2,1)S(1)} %slice.26), channel_id=1, source_target_pairs={{0,192},{64,0},{128,64},{192,128},{1,193},{65,1},{129,65},{193,129... | collective-permute-start | bytes 786440 | tf_op jit(solution)/shard_map/ppermute | solution.py:22
  220.6 5.3 %collective-permute-done.15.p2a_ref = bf16[4,2,128,128]{3,2,1,0:T(8,128)(2,1)S(1)} collective-permute-done((bf16[4,2,128,128]{3,2,1,0:T(8,128)(2,1)S(1)}, bf16[4,2,128,128]{3,2,1,0:T(8,128)(2,1)S(1)}, u32[]{:S(2)}, u32[]{:S(2)}) %collective-permute-start.15) | collective-permute-done | bytes 262176 | tf_op jit(solution)/shard_map/ppermute | solution.py:22
  225.9 3.5 %shard_map.69 = f32[4,8,2,128,128]{4,3,2,1,0:T(8,128)} custom-call(s32[1]{0:T(128)} %bitcast.samp_ref, bf16[8,2,128,128]{3,2,1,0:T(8,128)(2,1)S(1)} %get-tuple-element.6.own_ref, bf16[8,2,128,128]{3,2,1,0:T(8,128)(2,1)S(1)} %collective-permute-done.14.p1_ref, bf16[4,2,128,128]{3,2,1,0:T(8,128)(2,1)S(1)} %collective-permute-done.15.p2a_ref, ...), custom_call_target="tpu_custom_call" | custom-call | tf_op jit(solution)/shard_map/pallas_call | solution.py:178
  (64 shorter events, 21.5 us)
Async XLA Ops:
  0.6 108.1 %copy-start = (f32[4096]{0:T(1024)S(1)}, f32[4096]{0:T(1024)}, u32[]{:S(2)}) copy-start(f32[4096]{0:T(1024)} %param.6) | copy-start | bytes 49156
  5.1 75.1 %all-to-all-start = ((bf16[64,32,4,128]{3,2,1,0:T(4,128)(2,1)}), bf16[64,32,4,128]{3,2,1,0:T(4,128)(2,1)S(1)}, u32[]{:S(2)}, u32[]{:S(2)}) async-start(bf16[64,32,4,128]{3,2,1,0:T(4,128)(2,1)} %bitcast.50), calls=%async_computation | async-start | bytes 4194304 | tf_op jit(solution)/shard_map/all_to_all | solution.py:217
  18.3 45.4 %collective-permute-start.3 = (s32[32]{0:T(128)S(1)}, s32[32]{0:T(128)S(1)}, u32[]{:S(2)}, u32[]{:S(2)}) collective-permute-start(s32[32]{0:T(128)S(1)} %bitcast.58), channel_id=1, source_target_pairs={{0,2},{2,4},{4,6},{6,8},{8,10},{10,12},{12,14},{14,0},{1,3},{3,5},... | collective-permute-start | bytes 392 | tf_op jit(solution)/shard_map/ppermute | solution.py:22
  19.8 46.2 %collective-permute-start.4 = (s32[32]{0:T(128)S(1)}, s32[32]{0:T(128)S(1)}, u32[]{:S(2)}, u32[]{:S(2)}) collective-permute-start(s32[32]{0:T(128)S(1)} %bitcast.59), channel_id=1, source_target_pairs={{0,4},{2,6},{4,8},{6,10},{8,12},{10,14},{12,0},{14,2},{1,5},{3,7},... | collective-permute-start | bytes 392 | tf_op jit(solution)/shard_map/ppermute | solution.py:22
  21.9 48.2 %collective-permute-start.5 = (s32[32]{0:T(128)S(1)}, s32[32]{0:T(128)S(1)}, u32[]{:S(2)}, u32[]{:S(2)}) collective-permute-start(s32[32]{0:T(128)S(1)} %bitcast.60), channel_id=1, source_target_pairs={{0,6},{2,8},{4,10},{6,12},{8,14},{10,0},{12,2},{14,4},{1,7},{3,9},... | collective-permute-start | bytes 392 | tf_op jit(solution)/shard_map/ppermute | solution.py:22
  24.3 45.8 %collective-permute-start.6 = (s32[32]{0:T(128)S(1)}, s32[32]{0:T(128)S(1)}, u32[]{:S(2)}, u32[]{:S(2)}) collective-permute-start(s32[32]{0:T(128)S(1)} %bitcast.61), channel_id=1, source_target_pairs={{0,8},{2,10},{4,12},{6,14},{8,0},{10,2},{12,4},{14,6},{1,9},{3,11}... | collective-permute-start | bytes 392 | tf_op jit(solution)/shard_map/ppermute | solution.py:22
  26.3 43.7 %collective-permute-start.7 = (s32[32]{0:T(128)S(1)}, s32[32]{0:T(128)S(1)}, u32[]{:S(2)}, u32[]{:S(2)}) collective-permute-start(s32[32]{0:T(128)S(1)} %bitcast.62), channel_id=1, source_target_pairs={{0,10},{2,12},{4,14},{6,0},{8,2},{10,4},{12,6},{14,8},{1,11},{3,13... | collective-permute-start | bytes 392 | tf_op jit(solution)/shard_map/ppermute | solution.py:22
  63.7 6.3 %collective-permute-start.8 = (s32[32]{0:T(128)S(1)}, s32[32]{0:T(128)S(1)}, u32[]{:S(2)}, u32[]{:S(2)}) collective-permute-start(s32[32]{0:T(128)S(1)} %bitcast.63), channel_id=1, source_target_pairs={{0,12},{2,14},{4,0},{6,2},{8,4},{10,6},{12,8},{14,10},{1,13},{3,15... | collective-permute-start | bytes 392 | tf_op jit(solution)/shard_map/ppermute | solution.py:22
  66.0 4.7 %collective-permute-start.9 = (s32[32]{0:T(128)S(1)}, s32[32]{0:T(128)S(1)}, u32[]{:S(2)}, u32[]{:S(2)}) collective-permute-start(s32[32]{0:T(128)S(1)} %bitcast.64), channel_id=1, source_target_pairs={{0,14},{2,0},{4,2},{6,4},{8,6},{10,8},{12,10},{14,12},{1,15},{3,1}... | collective-permute-start | bytes 392 | tf_op jit(solution)/shard_map/ppermute | solution.py:22
  70.8 2.6 %collective-permute-start.10 = (s32[8,32]{1,0:T(8,128)S(1)}, s32[8,32]{1,0:T(8,128)S(1)}, u32[]{:S(2)}, u32[]{:S(2)}) collective-permute-start(s32[8,32]{1,0:T(8,128)S(1)} %stack.92), channel_id=1, source_target_pairs={{0,1},{1,0},{2,3},{3,2},{4,5},{5,4},{6,7},{7,6},{8,9},{9,8},{10,11... | collective-permute-start | bytes 3080 | tf_op jit(solution)/shard_map/ppermute | solution.py:22
  73.4 3.8 %collective-permute-start.13 = (s32[2,8,32]{2,1,0:T(8,128)S(1)}, s32[2,8,32]{2,1,0:T(8,128)S(1)}, u32[]{:S(2)}, u32[]{:S(2)}) collective-permute-start(s32[2,8,32]{2,1,0:T(8,128)S(1)} %get-tuple-element.17), channel_id=1, source_target_pairs={{0,48},{16,0},{32,16},{48,32},{1,49},{17,1},{33,17},{49,33},{2,50}... | collective-permute-start | bytes 6152 | tf_op jit(solution)/shard_map/ppermute | solution.py:22
  76.0 4.0 %collective-permute-start.12 = (s32[2,8,32]{2,1,0:T(8,128)S(1)}, s32[2,8,32]{2,1,0:T(8,128)S(1)}, u32[]{:S(2)}, u32[]{:S(2)}) collective-permute-start(s32[2,8,32]{2,1,0:T(8,128)S(1)} %get-tuple-element.17), channel_id=1, source_target_pairs={{0,32},{16,48},{32,0},{48,16},{1,33},{17,49},{33,1},{49,17},{2,34}... | collective-permute-start | bytes 6152 | tf_op jit(solution)/shard_map/ppermute | solution.py:22
  76.4 3.7 %collective-permute-start.11 = (s32[2,8,32]{2,1,0:T(8,128)S(1)}, s32[2,8,32]{2,1,0:T(8,128)S(1)}, u32[]{:S(2)}, u32[]{:S(2)}) collective-permute-start(s32[2,8,32]{2,1,0:T(8,128)S(1)} %get-tuple-element.17), channel_id=1, source_target_pairs={{0,16},{16,32},{32,48},{48,0},{1,17},{17,33},{33,49},{49,1},{2,18}... | collective-permute-start | bytes 6152 | tf_op jit(solution)/shard_map/ppermute | solution.py:22
  90.2 66.0 %all-to-all-start.1 = ((bf16[256,8,4,128]{3,2,1,0:T(4,128)(2,1)}), bf16[256,8,4,128]{3,2,1,0:T(4,128)(2,1)}, u32[]{:S(2)}, u32[]{:S(2)}) async-start(bf16[256,8,4,128]{3,2,1,0:T(4,128)(2,1)} %copy-done.2), calls=%async_computation.1 | async-start | bytes 4194304 | tf_op jit(solution)/shard_map/all_to_all | solution.py:220
  103.6 55.2 %collective-permute-start = (bf16[256,1024]{1,0:T(8,128)(2,1)}, bf16[256,1024]{1,0:T(8,128)(2,1)S(1)}, u32[]{:S(2)}, u32[]{:S(2)}) collective-permute-start(bf16[256,1024]{1,0:T(8,128)(2,1)} %get-tuple-element.11), channel_id=1, source_target_pairs={{0,64},{64,128},{128,192},{192,0},{1,65},{65,129},{129,193},{193,1... | collective-permute-start | bytes 1572872 | tf_op jit(solution)/shard_map/ppermute | solution.py:22
  105.0 53.8 %collective-permute-start.1 = (bf16[256,1024]{1,0:T(8,128)(2,1)}, bf16[256,1024]{1,0:T(8,128)(2,1)S(1)}, u32[]{:S(2)}, u32[]{:S(2)}) collective-permute-start(bf16[256,1024]{1,0:T(8,128)(2,1)} %get-tuple-element.10), channel_id=1, source_target_pairs={{0,128},{64,192},{128,0},{192,64},{1,129},{65,193},{129,1},{193,65... | collective-permute-start | bytes 1572872 | tf_op jit(solution)/shard_map/ppermute | solution.py:22
  107.4 52.2 %collective-permute-start.2 = (bf16[256,1024]{1,0:T(8,128)(2,1)}, bf16[256,1024]{1,0:T(8,128)(2,1)}, u32[]{:S(2)}, u32[]{:S(2)}) collective-permute-start(bf16[256,1024]{1,0:T(8,128)(2,1)} %get-tuple-element.9), channel_id=1, source_target_pairs={{0,192},{64,0},{128,64},{192,128},{1,193},{65,1},{129,65},{193,129... | collective-permute-start | bytes 1572872 | tf_op jit(solution)/shard_map/ppermute | solution.py:22
  170.7 46.4 %collective-permute-start.14 = (bf16[8,2,128,128]{3,2,1,0:T(8,128)(2,1)S(1)}, bf16[8,2,128,128]{3,2,1,0:T(8,128)(2,1)S(1)}, u32[]{:S(2)}, u32[]{:S(2)}) collective-permute-start(bf16[8,2,128,128]{3,2,1,0:T(8,128)(2,1)S(1)} %get-tuple-element.6.own_ref), channel_id=1, source_target_pairs={{0,64},{64,128},{128,192},{192,0},{1,65},{65,129},{129,193},{193,1... | collective-permute-start | bytes 1572872 | tf_op jit(solution)/shard_map/ppermute | solution.py:22
  171.1 46.0 %collective-permute-start.16 = (bf16[8,2,128,128]{3,2,1,0:T(8,128)(2,1)S(1)}, bf16[8,2,128,128]{3,2,1,0:T(8,128)(2,1)S(1)}, u32[]{:S(2)}, u32[]{:S(2)}) collective-permute-start(bf16[8,2,128,128]{3,2,1,0:T(8,128)(2,1)S(1)} %get-tuple-element.6.own_ref), channel_id=1, source_target_pairs={{0,192},{64,0},{128,64},{192,128},{1,193},{65,1},{129,65},{193,129... | collective-permute-start | bytes 1572872 | tf_op jit(solution)/shard_map/ppermute | solution.py:22
  173.4 46.5 %collective-permute-start.18 = (f32[8,128]{1,0:T(8,128)S(1)}, f32[8,128]{1,0:T(8,128)S(1)}, u32[]{:S(2)}, u32[]{:S(2)}) collective-permute-start(f32[8,128]{1,0:T(8,128)S(1)} %get-tuple-element.7), channel_id=1, source_target_pairs={{0,64},{64,128},{128,192},{192,0},{1,65},{65,129},{129,193},{193,1... | collective-permute-start | bytes 12296 | tf_op jit(solution)/shard_map/ppermute | solution.py:22
  173.4 46.5 %collective-permute-start.19 = (f32[8,128]{1,0:T(8,128)S(1)}, f32[8,128]{1,0:T(8,128)S(1)}, u32[]{:S(2)}, u32[]{:S(2)}) collective-permute-start(f32[8,128]{1,0:T(8,128)S(1)} %get-tuple-element.7), channel_id=1, source_target_pairs={{0,128},{64,192},{128,0},{192,64},{1,129},{65,193},{129,1},{193,65... | collective-permute-start | bytes 12296 | tf_op jit(solution)/shard_map/ppermute | solution.py:22
  174.6 45.3 %collective-permute-start.20 = (f32[8,128]{1,0:T(8,128)S(1)}, f32[8,128]{1,0:T(8,128)S(1)}, u32[]{:S(2)}, u32[]{:S(2)}) collective-permute-start(f32[8,128]{1,0:T(8,128)S(1)} %get-tuple-element.7), channel_id=1, source_target_pairs={{0,192},{64,0},{128,64},{192,128},{1,193},{65,1},{129,65},{193,129... | collective-permute-start | bytes 12296 | tf_op jit(solution)/shard_map/ppermute | solution.py:22
  217.1 8.8 %collective-permute-start.15 = (bf16[4,2,128,128]{3,2,1,0:T(8,128)(2,1)S(1)}, bf16[4,2,128,128]{3,2,1,0:T(8,128)(2,1)S(1)}, u32[]{:S(2)}, u32[]{:S(2)}) collective-permute-start(bf16[4,2,128,128]{3,2,1,0:T(8,128)(2,1)S(1)} %slice.25), channel_id=1, source_target_pairs={{0,64},{64,128},{128,192},{192,0},{1,65},{65,129},{129,193},{193,1... | collective-permute-start | bytes 786440 | tf_op jit(solution)/shard_map/ppermute | solution.py:22
  217.2 8.7 %collective-permute-start.17 = (bf16[4,2,128,128]{3,2,1,0:T(8,128)(2,1)S(1)}, bf16[4,2,128,128]{3,2,1,0:T(8,128)(2,1)S(1)}, u32[]{:S(2)}, u32[]{:S(2)}) collective-permute-start(bf16[4,2,128,128]{3,2,1,0:T(8,128)(2,1)S(1)} %slice.26), channel_id=1, source_target_pairs={{0,192},{64,0},{128,64},{192,128},{1,193},{65,1},{129,65},{193,129... | collective-permute-start | bytes 786440 | tf_op jit(solution)/shard_map/ppermute | solution.py:22
  (6 other events, 31.7 us)

commit v2 on v1

v2 whole, which is shorter than its diff:
```python
import functools

import jax
import jax.numpy as jnp
from jax import lax
from jax.experimental import pallas as pl
from jax.experimental.pallas import tpu as pltpu
from jax.sharding import Mesh
from jax.sharding import PartitionSpec as P

STEPS = 2
STEP_LENGTH = 0.5
PENALTY = 0.5
DIGIT = 64
HALVES = 2
VAR = ("var_0", "var_1", "var_2")
ALL = ("samp", "var_0", "var_1", "var_2")
F32 = jnp.float32
BF16 = jnp.bfloat16
VMEM = pl.BlockSpec(memory_space=pltpu.VMEM)
ANY = pl.BlockSpec(memory_space=pl.ANY)
HBM = pl.BlockSpec(memory_space=pltpu.HBM)


def params(mib):
    return pltpu.CompilerParams(vmem_limit_bytes=mib << 20)


def cost(flops, bytes_accessed):
    return pl.CostEstimate(flops=flops, bytes_accessed=bytes_accessed, transcendentals=0)


def shift(x, axis, k):
    n = lax.axis_size(axis)
    return lax.ppermute(x, axis, [(i, (i + k) % n) for i in range(n)])


def cut_kernel(cols, at_ref, pattern_ref, data_ref, out_ref, note):
    width = note.shape[1]

    @pl.when(pl.program_id(0) == 0)
    def _():
        lane = lax.broadcasted_iota(jnp.int32, note.shape, 1)
        row = lax.broadcasted_iota(jnp.int32, note.shape, 0)
        digits = jnp.zeros(note.shape, jnp.int32)
        for k in range(cols):
            first, second = pattern_ref[2 * k], pattern_ref[2 * k + 1]
            block = jnp.where(first == at_ref[0] * cols + k, second, first)
            place = block + lax.div(block, cols)
            digit = jnp.where(row == 0, lax.div(place, DIGIT), lax.rem(place, DIGIT))
            digits = jnp.where(lane == k, digit, digits)
        note[...] = digits.astype(F32)

    wanted = note[...].astype(BF16)
    pieces, rows = out_ref.shape[0], out_ref.shape[2]
    for b in range(cols):
        tile = data_ref[:, b * width : (b + 1) * width]
        for i in range(pieces):
            out_ref[i, b] = tile[i * rows : (i + 1) * rows]
    for i in range(pieces):
        out_ref[i, cols] = wanted[:rows]


def cut(var_index, pattern, data, devices, cols, width):
    rows = data.shape[0] // devices
    pieces = 8
    return pl.pallas_call(
        functools.partial(cut_kernel, cols),
        grid_spec=pltpu.PrefetchScalarGridSpec(
            num_scalar_prefetch=2,
            grid=(devices // pieces,),
            in_specs=[pl.BlockSpec((pieces * rows, cols * width), lambda i, a, p: (i, 0))],
            out_specs=pl.BlockSpec((pieces, cols + 1, rows, width), lambda i, a, p: (i, 0, 0, 0)),
            scratch_shapes=[pltpu.VMEM((8, width), F32)],
        ),
        out_shape=jax.ShapeDtypeStruct((devices, cols + 1, rows, width), data.dtype),
        compiler_params=params(56),
    )(var_index[None], pattern.reshape(-1), data)


def pick_kernel(cols, shares, table_ref, *rest):
    out_ref, digits, wanted, held, sem, sems = rest[-6:]
    devices = digits.shape[0]
    each = cols // shares
    for u in range(devices):
        note = table_ref[u * (cols + 1) + cols].astype(F32)
        digits[u : u + 1, :] = (note[:1] * DIGIT + note[1:2]).astype(jnp.int32)
    move = pltpu.make_async_copy(digits, wanted, sem)
    move.start()
    move.wait()
    sent = []
    for s in range(shares):

        @pl.loop(0, devices, unroll=4)
        def _(d):
            for j in range(each):
                held[s, d, j] = table_ref[wanted[d, s * each + j]]

        copy = pltpu.make_async_copy(held.at[s], out_ref.at[pl.ds(s * devices, devices)], sems.at[s])
        copy.start()
        sent.append(copy)
    for copy in sent:
        copy.wait()


def pick(table, cols, shares, after):
    devices, _, rows, width = table.shape
    each = cols // shares
    return pl.pallas_call(
        functools.partial(pick_kernel, cols, shares),
        in_specs=[VMEM] + [HBM] * len(after),
        out_specs=HBM,
        out_shape=jax.ShapeDtypeStruct((shares * devices, each, rows, width), table.dtype),
        scratch_shapes=[
            pltpu.VMEM((devices, width), jnp.int32),
            pltpu.SMEM((devices, width), jnp.int32),
            pltpu.VMEM((shares, devices, each, rows, width), table.dtype),
            pltpu.SemaphoreType.DMA(()),
            pltpu.SemaphoreType.DMA((shares,)),
        ],
        compiler_params=params(56),
    )(table.reshape((devices * (cols + 1), rows, width)), *after)


def near_kernel(info_ref, own_ref, p1_ref, p2_ref, p3_ref, blocks_ref, near_ref, turned_ref, start_ref):
    samp, rows, width = info_ref[0], own_ref.shape[0], own_ref.shape[1]
    for k, ref in enumerate((own_ref, p1_ref, p2_ref, p3_ref)):
        q = lax.rem(samp + 4 - k, 4)
        at = pl.multiple_of(q * rows, rows)
        x = ref[...]
        near_ref[0, pl.ds(at, rows), :] = x
        turned_ref[0, :, pl.ds(at, rows)] = x.T
    where_diag = info_ref[2 + pl.program_id(0)]
    start_ref[0, :width] = blocks_ref[0, where_diag]
    start_ref[0, width:] = blocks_ref[0, 1 - where_diag]


def near_panels(info, observed, received, blocks, each):
    rows, width = observed.shape[0], blocks.shape[-1]
    part = pl.BlockSpec((rows, width), lambda j, f: (0, j))
    return pl.pallas_call(
        near_kernel,
        grid_spec=pltpu.PrefetchScalarGridSpec(
            num_scalar_prefetch=1,
            grid=(each,),
            in_specs=[
                pl.BlockSpec((rows, width), lambda j, f: (0, f[1] + j)),
                part,
                part,
                part,
                pl.BlockSpec((1, 2, width, width), lambda j, f: (f[1] + j, 0, 0, 0)),
            ],
            out_specs=[
                pl.BlockSpec((1, 4 * rows, width), lambda j, f: (j, 0, 0)),
                pl.BlockSpec((1, width, 4 * rows), lambda j, f: (j, 0, 0)),
                pl.BlockSpec((1, 2 * width, width), lambda j, f: (j, 0, 0)),
            ],
        ),
        out_shape=[
            jax.ShapeDtypeStruct((each, 4 * rows, width), BF16),
            jax.ShapeDtypeStruct((each, width, 4 * rows), BF16),
            jax.ShapeDtypeStruct((each, 2 * width, width), F32),
        ],
        compiler_params=params(56),
        cost_estimate=cost(1 << 20, 10 << 20),
    )(info, observed, *received, blocks)


def shrink(v, level):
    return jnp.where(v > level, v - level, jnp.where(v < -level, v + level, 0.0))


def split3(g):
    hi = g.astype(BF16)
    rest = g - hi.astype(F32)
    mid = rest.astype(BF16)
    return hi, mid, (rest - mid.astype(F32)).astype(BF16)


def steps_kernel(first, info_ref, far_ref, near_ref, turned_ref, start_ref, diag_ref, out_ref, new_diag_ref, obj_ref):
    count, total_rows, width = near_ref.shape
    step = pl.program_id(0)
    eye = lax.broadcasted_iota(jnp.int32, (width, width), 0) == lax.broadcasted_iota(jnp.int32, (width, width), 1)
    objs = [jnp.zeros((1, width), F32) for _ in range(STEPS)]
    for c in range(count):
        j = first + step * count + c
        far = far_ref[c]
        both = jnp.concatenate([near_ref[c], far], axis=1)
        top = jnp.dot(turned_ref[c], both, preferred_element_type=F32)
        low = lax.dot_general(far, both, (((0,), (0,)), ((), ())), preferred_element_type=F32)
        parts = split3(jnp.concatenate([top, low], axis=0))
        db = jnp.where(eye, 0.0, start_ref[c, :width])
        ob = start_ref[c, width:]
        dv = diag_ref[pl.ds(info_ref[1] + j, 1), :]
        for i in range(STEPS):
            full = jnp.where(eye, jnp.broadcast_to(dv, (width, width)), db)
            w = jnp.concatenate([full, ob], axis=0).astype(BF16)
            g = sum(jnp.dot(p, w, preferred_element_type=F32) for p in reversed(parts))
            fit = jnp.sum(w.astype(F32) * g, axis=0, keepdims=True) / (2.0 * total_rows)
            size = jnp.sum(jnp.abs(db) + jnp.abs(ob), axis=0, keepdims=True)
            objs[i] = objs[i] + (fit - jnp.log(dv) + PENALTY * size)
            g = g / total_rows
            gd, go = g[:width], g[width:]
            along = jnp.sum(jnp.where(eye, gd, 0.0), axis=0, keepdims=True)
            db = jnp.where(eye, 0.0, shrink(db - STEP_LENGTH * gd, STEP_LENGTH * PENALTY))
            ob = shrink(ob - STEP_LENGTH * go, STEP_LENGTH * PENALTY)
            m = dv - STEP_LENGTH * along
            dv = 0.5 * (m + jnp.sqrt(m * m + 4.0 * STEP_LENGTH))
        where_diag = info_ref[2 + j]
        out_ref[c, where_diag] = db.astype(out_ref.dtype)
        out_ref[c, 1 - where_diag] = ob.astype(out_ref.dtype)
        new_diag_ref[pl.ds(step * count + c, 1), :] = dv
    lane = lax.broadcasted_iota(jnp.int32, (1, width), 1)
    total = jnp.zeros((1, width), F32)
    for i in range(STEPS):
        total = jnp.where(lane == i, jnp.sum(objs[i], axis=1, keepdims=True), total)

    @pl.when(step == 0)
    def _():
        obj_ref[...] = total

    @pl.when(step > 0)
    def _():
        obj_ref[...] += total


def iterate(first, info, far, near, turned, start, diag_rows):
    count, total_rows, width = far.shape
    block = 2

    def columns(shape, offset):
        return pl.BlockSpec((block,) + shape, lambda i, f: (offset // block + i, 0, 0))

    return pl.pallas_call(
        functools.partial(steps_kernel, first),
        grid_spec=pltpu.PrefetchScalarGridSpec(
            num_scalar_prefetch=1,
            grid=(count // block,),
            in_specs=[
                columns((total_rows, width), 0),
                columns((total_rows, width), first),
                columns((width, total_rows), first),
                columns((2 * width, width), first),
                pl.BlockSpec(diag_rows.shape, lambda i, f: (0, 0)),
            ],
            out_specs=[
                pl.BlockSpec((block, 2, width, width), lambda i, f: (i, 0, 0, 0)),
                pl.BlockSpec((count, width), lambda i, f: (0, 0)),
                pl.BlockSpec((1, width), lambda i, f: (0, 0)),
            ],
        ),
        out_shape=[
            jax.ShapeDtypeStruct((count, 2, width, width), BF16),
            jax.ShapeDtypeStruct((count, width), F32),
            jax.ShapeDtypeStruct((1, width), F32),
        ],
        compiler_params=params(40),
        cost_estimate=cost(count << 29, 4 << 20),
    )(info, far, near, turned, start, diag_rows)


def first_places_kernel(samp_ref, h00, h01, h10, h11, h30, h31, out_ref):
    samp = samp_ref[0]
    for k, refs in ((0, (h00, h01)), (1, (h10, h11)), (3, (h30, h31))):
        q = lax.rem(samp + 4 - k, 4)
        for h, ref in enumerate(refs):
            out_ref[q, h, 0] = ref[0].astype(F32)


def last_places_kernel(samp_ref, h20, h21, _, out_ref):
    out_ref[0, 0, 0] = h20[0].astype(F32)
    out_ref[0, 1, 0] = h21[0].astype(F32)


def place_blocks(samp, own, one, three, two):
    count, tail = own[0].shape[0], own[0].shape[1:]
    zeros = (0,) * len(tail)
    part = pl.BlockSpec((1,) + tail, lambda j, f: (j,) + zeros)
    shape = jax.ShapeDtypeStruct((4, HALVES, count) + tail, F32)
    out = pl.pallas_call(
        first_places_kernel,
        grid_spec=pltpu.PrefetchScalarGridSpec(
            num_scalar_prefetch=1,
            grid=(count,),
            in_specs=[part] * 6,
            out_specs=pl.BlockSpec((4, HALVES, 1) + tail, lambda j, f: (0, 0, j) + zeros),
        ),
        out_shape=shape,
        compiler_params=params(24),
        cost_estimate=cost(1 << 20, 6 << 20),
    )(samp[None], *own, *one, *three)
    out = pl.pallas_call(
        last_places_kernel,
        grid_spec=pltpu.PrefetchScalarGridSpec(
            num_scalar_prefetch=1,
            grid=(count,),
            in_specs=[part, part, ANY],
            out_specs=pl.BlockSpec((1, HALVES, 1) + tail, lambda j, f: (lax.rem(f[0] + 2, 4), 0, j) + zeros),
        ),
        out_shape=shape,
        input_output_aliases={3: 0},
        compiler_params=params(16),
        cost_estimate=cost(1 << 20, 2 << 20),
    )(samp[None], *two, out)
    return out.reshape((4 * HALVES * count,) + tail)


def body(observed, blocks, diagonal, pattern):
    cols, _, width, _ = blocks.shape
    rows = observed.shape[0]
    devices = lax.axis_size(VAR)
    shares = lax.axis_size("samp")
    each = cols // shares
    half = each // HALVES
    total_rows = rows * shares
    samp = lax.axis_index("samp").astype(jnp.int32)
    var_index = lax.axis_index(VAR).astype(jnp.int32)

    pieces = cut(var_index, pattern, observed, devices, cols, width)
    panel = each * width
    received = [shift(lax.dynamic_slice_in_dim(observed, lax.rem(samp + k, shares) * panel, panel, 1), "samp", k) for k in (1, 2, 3)]
    table = lax.all_to_all(pieces, VAR, split_axis=0, concat_axis=0, tiled=True)
    start = samp * each
    columns = var_index * cols + jnp.arange(cols, dtype=jnp.int32)
    which = jnp.where(pattern[:, 0] == columns, 0, 1).astype(jnp.int32)
    info = jnp.concatenate([jnp.stack([samp, start]), lax.dynamic_slice_in_dim(which, start, each, 0)])
    near, turned, begin = near_panels(info, observed, received, blocks, each)
    outgoing = pick(table, cols, shares, (near, turned, begin))
    far = lax.all_to_all(outgoing, ALL, split_axis=0, concat_axis=0, tiled=True)

    diag_rows = diagonal.reshape(cols, width)
    new, diags, objs = [], [], []
    for h in range(HALVES):
        far_h = far[:, h * half : (h + 1) * half].transpose(1, 0, 2, 3).reshape(half, total_rows, width)
        done = iterate(h * half, info, far_h, near, turned, begin, diag_rows)
        new.append(done[0])
        diags.append(done[1])
        objs.append(done[2])

    one = [shift(x, "samp", 1) for x in new]
    three = [shift(x, "samp", 3) for x in new]
    two = [shift(one[0], "samp", 1), shift(three[1], "samp", 3)]
    new_blocks = place_blocks(samp, new, one, three, two)

    new_diag = jnp.concatenate(diags, axis=0)
    before = [new_diag] + [shift(new_diag, "samp", k) for k in (1, 2, 3)]
    order = []
    for q in range(4):
        k = lax.rem(samp + 4 - q, 4)
        order.append(jnp.where(k == 0, before[0], jnp.where(k == 1, before[1], jnp.where(k == 2, before[2], before[3]))))
    new_diagonal = jnp.stack(order).reshape(-1)

    mine = jnp.broadcast_to(objs[0] + objs[1], (shares * devices, width))
    objective = jnp.sum(lax.all_to_all(mine, ALL, split_axis=0, concat_axis=0, tiled=True), axis=0)
    return (new_blocks, new_diagonal, objective[:STEPS] / (cols * devices * width))


def solution(mesh):
    torus = Mesh(mesh.devices.reshape(mesh.shape["samp"], 4, 8, 2), ALL)
    placed = (P("samp", VAR), P(VAR, None, None, None), P(VAR), P(VAR, None))
    return jax.shard_map(
        body,
        mesh=torus,
        in_specs=placed,
        out_specs=(P(VAR, None, None, None), P(VAR), P()),
        check_vma=False,
    )
```

time: 230 us -> 188 us (0.82); the launches traced: 229 us -> 185 us
  blocking collectives: 40.8 us -> 0 us
  starting transfers between devices: 60.4 us -> 45.1 us
  Pallas kernels: 22.3 us -> 31.7 us
  waiting for transfers between devices: 92.7 us -> 97.5 us
  local copies, waits for them, and re-layouts: 11.5 us -> 7.92 us
    psum x4 -> x0, blocking collectives: 40.8 us -> none  [body(): objective = functools.reduce(lax.psum, ALL, objective)]
    ppermute x21 -> x12, starting transfers between devices: 35.1 us -> 16.3 us  [shift(): return lax.ppermute(x, axis, [(i, (i + k) % n) for i in range(n)])]
    ppermute x21 -> x12, waiting for transfers between devices: 45.1 us -> 26.7 us  [shift(): return lax.ppermute(x, axis, [(i, (i + k) % n) for i in range(n)])]
    all_to_all x1, waiting for transfers between devices: 0.01 us -> 15.2 us  [body(): table = lax.all_to_all(pieces, VAR, split_axis=0, concat_axis=0, tiled=True)]
    pallas_call x3 -> x7, Pallas kernels: 22.3 us -> 31.7 us  [the longest x1 7.57 us: near_panels(): pl.pallas_call(near_kernel, grid_spec=pltpu.PrefetchScalarGridSpec(num_sc...]
    all_to_all x1, waiting for transfers between devices: 47.6 us -> 54.8 us  [body(): far = lax.all_to_all(outgoing, ALL, split_axis=0, concat_axis=0, tiled=True)]
    all_to_all x0 -> x1, starting transfers between devices: none -> 6.91 us  [body(): lax.all_to_all(mine, ALL, split_axis=0, concat_axis=0, tiled=True)]
    all_to_all x1, starting transfers between devices: 12.1 us -> 8.59 us  [body(): far = lax.all_to_all(outgoing, ALL, split_axis=0, concat_axis=0, tiled=True)]
  transfers between devices with their start and end apart: 23 -> 15, of which waited for: 8 -> 7; matrix products, arithmetic and copies ran while one was open for 2% -> 2% of each run, Pallas kernels for 0% -> 7%
where the time goes in v2:
time: 188 us; the launch traced here: 185 us
  waiting for transfers between devices  97.5 us (52%)
  starting transfers between devices  45.1 us (24%)
  Pallas kernels  31.7 us (17%)
  local copies, waits for them, and re-layouts  7.92 us (4%)
    all_to_all x1, waiting for transfers between devices, body(): far = lax.all_to_all(outgoing, ALL, split_axis=0, concat_axis=0, tiled=True)  54.8 us
    ppermute x12, waiting for transfers between devices, shift(): return lax.ppermute(x, axis, [(i, (i + k) % n) for i in range(n)])  26.7 us
    ppermute x12, starting transfers between devices, shift(): return lax.ppermute(x, axis, [(i, (i + k) % n) for i in range(n)])  16.3 us
    all_to_all x1, waiting for transfers between devices, body(): table = lax.all_to_all(pieces, VAR, split_axis=0, concat_axis=0, tiled=True)  15.2 us
    all_to_all x1, starting transfers between devices, body(): table = lax.all_to_all(pieces, VAR, split_axis=0, concat_axis=0, tiled=True)  13.3 us
    all_to_all x1, starting transfers between devices, body(): far = lax.all_to_all(outgoing, ALL, split_axis=0, concat_axis=0, tiled=True)  8.59 us
    pallas_call x1, Pallas kernels, near_panels(): pl.pallas_call(near_kernel, grid_spec=pltpu.PrefetchScalarGridSpec(num_sc...  7.57 us
    pallas_call x2, Pallas kernels, iterate(): pl.pallas_call(functools.partial(steps_kernel, first), grid_spec=pltpu.Pr...  7.35 us
  transfers between devices with their start and end apart: 15, of which 7 were waited for; matrix products, arithmetic and copies ran while one was open for 2% of the time, Pallas kernels for 7%

profile of v2, /device:TPU:1, one launch (start us, length us, event | category | flops | bytes accessed | tf_op | source)
XLA Modules:
  0.0 184.8 jit_solution(1449772671157227423)
XLA Ops:
  2.0 6.7 %shard_map.67 = bf16[64,33,4,128]{3,2,1,0:T(4,128)(2,1)} custom-call(s32[1]{0:T(128)} %bitcast.3.at_ref, s32[64]{0:T(128)} %reshape.33.pattern_ref, bf16[256,4096]{1,0:T(8,128)(2,1)} %own_ref.1), custom_call_target="tpu_custom_call" | custom-call | tf_op jit(solution)/shard_map/pallas_call | solution.py:67
  8.8 13.3 %all-to-all-start = ((bf16[64,33,4,128]{3,2,1,0:T(4,128)(2,1)}), bf16[64,33,4,128]{3,2,1,0:T(4,128)(2,1)}, u32[]{:S(2)}, u32[]{:S(2)}) async-start(bf16[64,33,4,128]{3,2,1,0:T(4,128)(2,1)} %shard_map.67), calls=%async_computation | async-start | bytes 4325376 | tf_op jit(solution)/shard_map/all_to_all | solution.py:322
  22.1 1.0 constant_dynamic-slice_fusion
  23.1 1.3 collective-permute-start
  24.4 2.6 %collective-permute-start.1 = (bf16[256,1024]{1,0:T(8,128)(2,1)S(1)}, bf16[256,1024]{1,0:T(8,128)(2,1)S(1)}, u32[]{:S(2)}, u32[]{:S(2)}) collective-permute-start(bf16[256,1024]{1,0:T(8,128)(2,1)S(1)} %get-tuple-element.24), channel_id=1, source_target_pairs={{0,128},{64,192},{128,0},{192,64},{1,129},{65,193},{129,1},{193,65... | collective-permute-start | bytes 1572872 | tf_op jit(solution)/shard_map/ppermute | solution.py:35
  27.0 1.1 collective-permute-start.2
  28.7 9.0 %collective-permute-done.p1_ref = bf16[256,1024]{1,0:T(8,128)(2,1)S(1)} collective-permute-done((bf16[256,1024]{1,0:T(8,128)(2,1)}, bf16[256,1024]{1,0:T(8,128)(2,1)S(1)}, u32[]{:S(2)}, u32[]{:S(2)}) %collective-permute-start) | collective-permute-done | bytes 524320 | tf_op jit(solution)/shard_map/ppermute | solution.py:35
  37.7 12.3 %collective-permute-done.1.p2_ref = bf16[256,1024]{1,0:T(8,128)(2,1)S(1)} collective-permute-done((bf16[256,1024]{1,0:T(8,128)(2,1)S(1)}, bf16[256,1024]{1,0:T(8,128)(2,1)S(1)}, u32[]{:S(2)}, u32[]{:S(2)}) %collective-permute-start.1) | collective-permute-done | bytes 524320 | tf_op jit(solution)/shard_map/ppermute | solution.py:35
  51.7 7.6 %shard_map.68 = (bf16[8,1024,128]{2,1,0:T(8,128)(2,1)}, bf16[8,128,1024]{2,1,0:T(8,128)(2,1)}, f32[8,256,128]{2,1,0:T(8,128)}) custom-call(s32[10]{0:T(128)} %pad_add_fusion.info_ref, bf16[256,4096]{1,0:T(8,128)(2,1)} %own_ref.1, bf16[256,1024]{1,0:T(8,128)(2,1)} %copy-done.6, bf16[256,1024]{1,0:T(8,128)(2,1)} %copy-done.7, bf16[256,1024]{1,0:T(8,128)(2,1)} %copy-done.8, ...), custom_call_target="tpu_custom_call" | custom-call | flops 1048576 | bytes 10485760 | tf_op jit(solution)/shard_map/pallas_call | solution.py:141
  59.3 15.2 %all-to-all-done = bf16[64,33,4,128]{3,2,1,0:T(4,128)(2,1)} async-done(((bf16[64,33,4,128]{3,2,1,0:T(4,128)(2,1)}), bf16[64,33,4,128]{3,2,1,0:T(4,128)(2,1)}, u32[]{:S(2)}, u32[]{:S(2)}) %all-to-all-start) | async-done | bytes 2162720 | tf_op jit(solution)/shard_map/all_to_all | solution.py:322
  74.5 6.0 %shard_map.69 = bf16[256,8,4,128]{3,2,1,0:T(4,128)(2,1)} custom-call(bf16[2112,4,128]{2,1,0:T(4,128)(2,1)} %bitcast.4.table_ref, bf16[8,1024,128]{2,1,0:T(8,128)(2,1)} %get-tuple-element.12.rest_0_.near_ref, bf16[8,128,1024]{2,1,0:T(8,128)(2,1)} %get-tuple-element.13.rest_1_.turned_ref, f32[8,256,128]{2,1,0:T(8,128)} %get-tuple-element.14.rest_2_.start_ref), custom_call_target="tpu_custom_call" | custom-call | tf_op jit(solution)/shard_map/pallas_call | solution.py:109
  80.6 8.6 %all-to-all-start.1 = ((bf16[256,8,4,128]{3,2,1,0:T(4,128)(2,1)}), bf16[256,8,4,128]{3,2,1,0:T(4,128)(2,1)S(1)}, u32[]{:S(2)}, u32[]{:S(2)}) async-start(bf16[256,8,4,128]{3,2,1,0:T(4,128)(2,1)} %shard_map.69), calls=%async_computation.1 | async-start | bytes 4194304 | tf_op jit(solution)/shard_map/all_to_all | solution.py:329
  89.2 54.8 %all-to-all-done.1 = bf16[256,8,4,128]{3,2,1,0:T(4,128)(2,1)S(1)} async-done(((bf16[256,8,4,128]{3,2,1,0:T(4,128)(2,1)}), bf16[256,8,4,128]{3,2,1,0:T(4,128)(2,1)S(1)}, u32[]{:S(2)}, u32[]{:S(2)}) %all-to-all-start.1) | async-done | bytes 2097184 | tf_op jit(solution)/shard_map/all_to_all | solution.py:329
  146.8 3.7 %shard_map.71 = (bf16[4,2,128,128]{3,2,1,0:T(8,128)(2,1)S(1)}, f32[4,128]{1,0:T(4,128)S(1)}, f32[1,128]{1,0:T(1,128)S(1)}) custom-call(s32[10]{0:T(128)S(1)} %copy-done.3, bf16[4,1024,128]{2,1,0:T(8,128)(2,1)S(1)} %bitcast.28, bf16[8,1024,128]{2,1,0:T(8,128)(2,1)S(1)} %copy-done, bf16[8,128,1024]{2,1,0:T(8,128)(2,1)S(1)} %copy-done.1, ...), custom_call_target="tpu_custom_call" | custom-call | flops 2147483648 | bytes 4194304 | tf_op jit(solution)/shard_map/pallas_call | solution.py:234
  152.3 3.7 %shard_map.70 = (bf16[4,2,128,128]{3,2,1,0:T(8,128)(2,1)S(1)}, f32[4,128]{1,0:T(4,128)S(1)}, f32[1,128]{1,0:T(1,128)S(1)}) custom-call(s32[10]{0:T(128)S(1)} %copy-done.3, bf16[4,1024,128]{2,1,0:T(8,128)(2,1)S(1)} %bitcast.27, bf16[8,1024,128]{2,1,0:T(8,128)(2,1)S(1)} %copy-done, bf16[8,128,1024]{2,1,0:T(8,128)(2,1)S(1)} %copy-done.1, ...), custom_call_target="tpu_custom_call" | custom-call | flops 2147483648 | bytes 4194304 | tf_op jit(solution)/shard_map/pallas_call | solution.py:234
  156.4 2.8 %collective-permute-start.10 = (f32[8,128]{1,0:T(8,128)S(1)}, f32[8,128]{1,0:T(8,128)S(1)}, u32[]{:S(2)}, u32[]{:S(2)}) collective-permute-start(f32[8,128]{1,0:T(8,128)S(1)} %pad_maximum_fusion), channel_id=1, source_target_pairs={{0,128},{64,192},{128,0},{192,64},{1,129},{65,193},{129,1},{193,65... | collective-permute-start | bytes 12296 | tf_op jit(solution)/shard_map/ppermute | solution.py:35
  160.0 6.9 %all-to-all-start.2 = ((f32[256,1,128]{2,1,0:T(1,128)}), f32[256,1,128]{2,1,0:T(1,128)S(1)}, u32[]{:S(2)}, u32[]{:S(2)}) async-start(f32[256,1,128]{2,1,0:T(1,128)} %broadcast_in_dim.24), calls=%async_computation.2 | async-start | bytes 262144 | tf_op jit(solution)/shard_map/all_to_all | solution.py:354
  166.9 1.5 collective-permute-start.3
  168.4 1.4 collective-permute-start.8
  169.8 4.8 %collective-permute-done.3.h10 = bf16[4,2,128,128]{3,2,1,0:T(8,128)(2,1)S(1)} collective-permute-done((bf16[4,2,128,128]{3,2,1,0:T(8,128)(2,1)S(1)}, bf16[4,2,128,128]{3,2,1,0:T(8,128)(2,1)S(1)}, u32[]{:S(2)}, u32[]{:S(2)}) %collective-permute-start.3) | collective-permute-done | bytes 262176 | tf_op jit(solution)/shard_map/ppermute | solution.py:35
  174.6 2.4 %collective-permute-start.4 = (bf16[4,2,128,128]{3,2,1,0:T(8,128)(2,1)S(1)}, bf16[4,2,128,128]{3,2,1,0:T(8,128)(2,1)S(1)}, u32[]{:S(2)}, u32[]{:S(2)}) collective-permute-start(bf16[4,2,128,128]{3,2,1,0:T(8,128)(2,1)S(1)} %collective-permute-done.3.h10), channel_id=1, source_target_pairs={{0,64},{64,128},{128,192},{192,0},{1,65},{65,129},{129,193},{193,1... | collective-permute-start | bytes 786440 | tf_op jit(solution)/shard_map/ppermute | solution.py:35
  177.0 1.4 collective-permute-start.6
  180.3 2.4 %shard_map.72._ = f32[4,2,4,2,128,128]{5,4,3,2,1,0:T(8,128)} custom-call(s32[1]{0:T(128)} %bitcast.samp_ref, bf16[4,2,128,128]{3,2,1,0:T(8,128)(2,1)S(1)} %get-tuple-element.15.h00, bf16[4,2,128,128]{3,2,1,0:T(8,128)(2,1)S(1)} %get-tuple-element.16.h01, bf16[4,2,128,128]{3,2,1,0:T(8,128)(2,1)S(1)} %collective-permute-done.3.h10, ...), custom_call_target="tpu_custom_call" | custom-call | flops 1048576 | bytes 6291456 | tf_op jit(solution)/shard_map/pallas_call | solution.py:280
  183.3 1.5 shard_map.73
  (50 shorter events, 12.0 us)
Async XLA Ops:
  8.8 13.3 %copy-start.5 = (bf16[256,4096]{1,0:T(8,128)(2,1)S(1)}, bf16[256,4096]{1,0:T(8,128)(2,1)}, u32[]{:S(2)}) copy-start(bf16[256,4096]{1,0:T(8,128)(2,1)} %own_ref.1) | copy-start | bytes 6291460
  8.8 65.8 %all-to-all-start = ((bf16[64,33,4,128]{3,2,1,0:T(4,128)(2,1)}), bf16[64,33,4,128]{3,2,1,0:T(4,128)(2,1)}, u32[]{:S(2)}, u32[]{:S(2)}) async-start(bf16[64,33,4,128]{3,2,1,0:T(4,128)(2,1)} %shard_map.67), calls=%async_computation | async-start | bytes 4325376 | tf_op jit(solution)/shard_map/all_to_all | solution.py:322
  22.1 6.0 %copy-start.9 = (s32[32,2]{0,1:T(2,128)S(1)}, s32[32,2]{0,1:T(2,128)}, u32[]{:S(2)}) copy-start(s32[32,2]{0,1:T(2,128)} %param.7) | copy-start | bytes 772
  23.1 14.6 %collective-permute-start = (bf16[256,1024]{1,0:T(8,128)(2,1)}, bf16[256,1024]{1,0:T(8,128)(2,1)S(1)}, u32[]{:S(2)}, u32[]{:S(2)}) collective-permute-start(bf16[256,1024]{1,0:T(8,128)(2,1)} %get-tuple-element.25), channel_id=1, source_target_pairs={{0,64},{64,128},{128,192},{192,0},{1,65},{65,129},{129,193},{193,1... | collective-permute-start | bytes 1572872 | tf_op jit(solution)/shard_map/ppermute | solution.py:35
  24.4 25.7 %collective-permute-start.1 = (bf16[256,1024]{1,0:T(8,128)(2,1)S(1)}, bf16[256,1024]{1,0:T(8,128)(2,1)S(1)}, u32[]{:S(2)}, u32[]{:S(2)}) collective-permute-start(bf16[256,1024]{1,0:T(8,128)(2,1)S(1)} %get-tuple-element.24), channel_id=1, source_target_pairs={{0,128},{64,192},{128,0},{192,64},{1,129},{65,193},{129,1},{193,65... | collective-permute-start | bytes 1572872 | tf_op jit(solution)/shard_map/ppermute | solution.py:35
  27.0 23.1 %collective-permute-start.2 = (bf16[256,1024]{1,0:T(8,128)(2,1)S(1)}, bf16[256,1024]{1,0:T(8,128)(2,1)S(1)}, u32[]{:S(2)}, u32[]{:S(2)}) collective-permute-start(bf16[256,1024]{1,0:T(8,128)(2,1)S(1)} %get-tuple-element.23), channel_id=1, source_target_pairs={{0,192},{64,0},{128,64},{192,128},{1,193},{65,1},{129,65},{193,129... | collective-permute-start | bytes 1572872 | tf_op jit(solution)/shard_map/ppermute | solution.py:35
  37.7 12.4 %copy-start.6 = (bf16[256,1024]{1,0:T(8,128)(2,1)}, bf16[256,1024]{1,0:T(8,128)(2,1)S(1)}, u32[]{:S(2)}) copy-start(bf16[256,1024]{1,0:T(8,128)(2,1)S(1)} %collective-permute-done.p1_ref) | copy-start | bytes 1572868
  50.9 0.8 copy-start.8
  80.6 63.4 %all-to-all-start.1 = ((bf16[256,8,4,128]{3,2,1,0:T(4,128)(2,1)}), bf16[256,8,4,128]{3,2,1,0:T(4,128)(2,1)S(1)}, u32[]{:S(2)}, u32[]{:S(2)}) async-start(bf16[256,8,4,128]{3,2,1,0:T(4,128)(2,1)} %shard_map.69), calls=%async_computation.1 | async-start | bytes 4194304 | tf_op jit(solution)/shard_map/all_to_all | solution.py:329
  144.0 1.6 copy-start.1
  144.0 1.9 %copy-start.2 = (f32[8,256,128]{2,1,0:T(8,128)S(1)}, f32[8,256,128]{2,1,0:T(8,128)}, u32[]{:S(2)}) copy-start(f32[8,256,128]{2,1,0:T(8,128)} %get-tuple-element.14.rest_2_.start_ref) | copy-start | bytes 3145732
  144.0 1.9 %copy-start.4 = (f32[4096]{0:T(1024)S(1)}, f32[4096]{0:T(1024)}, u32[]{:S(2)}) copy-start(f32[4096]{0:T(1024)} %param.6) | copy-start | bytes 49156
  144.8 2.0 %copy-start = (bf16[8,1024,128]{2,1,0:T(8,128)(2,1)S(1)}, bf16[8,1024,128]{2,1,0:T(8,128)(2,1)}, u32[]{:S(2)}) copy-start(bf16[8,1024,128]{2,1,0:T(8,128)(2,1)} %get-tuple-element.12.rest_0_.near_ref) | copy-start | bytes 6291460
  144.8 2.0 %copy-start.3 = (s32[10]{0:T(128)S(1)}, s32[10]{0:T(128)}, u32[]{:S(2)}) copy-start(s32[10]{0:T(128)} %pad_add_fusion.info_ref) | copy-start | bytes 124
  150.5 26.6 %collective-permute-start.5 = (bf16[4,2,128,128]{3,2,1,0:T(8,128)(2,1)S(1)}, bf16[4,2,128,128]{3,2,1,0:T(8,128)(2,1)S(1)}, u32[]{:S(2)}, u32[]{:S(2)}) collective-permute-start(bf16[4,2,128,128]{3,2,1,0:T(8,128)(2,1)S(1)} %get-tuple-element.16.h01), channel_id=1, source_target_pairs={{0,192},{64,0},{128,64},{192,128},{1,193},{65,1},{129,65},{193,129... | collective-permute-start | bytes 786440 | tf_op jit(solution)/shard_map/ppermute | solution.py:35
  151.3 29.0 %collective-permute-start.7 = (bf16[4,2,128,128]{3,2,1,0:T(8,128)(2,1)S(1)}, bf16[4,2,128,128]{3,2,1,0:T(8,128)(2,1)S(1)}, u32[]{:S(2)}, u32[]{:S(2)}) collective-permute-start(bf16[4,2,128,128]{3,2,1,0:T(8,128)(2,1)S(1)} %get-tuple-element.16.h01), channel_id=1, source_target_pairs={{0,64},{64,128},{128,192},{192,0},{1,65},{65,129},{129,193},{193,1... | collective-permute-start | bytes 786440 | tf_op jit(solution)/shard_map/ppermute | solution.py:35
  156.0 10.9 %collective-permute-start.9 = (f32[8,128]{1,0:T(8,128)S(1)}, f32[8,128]{1,0:T(8,128)S(1)}, u32[]{:S(2)}, u32[]{:S(2)}) collective-permute-start(f32[8,128]{1,0:T(8,128)S(1)} %pad_maximum_fusion), channel_id=1, source_target_pairs={{0,64},{64,128},{128,192},{192,0},{1,65},{65,129},{129,193},{193,1... | collective-permute-start | bytes 12296 | tf_op jit(solution)/shard_map/ppermute | solution.py:35
  156.4 12.0 %collective-permute-start.10 = (f32[8,128]{1,0:T(8,128)S(1)}, f32[8,128]{1,0:T(8,128)S(1)}, u32[]{:S(2)}, u32[]{:S(2)}) collective-permute-start(f32[8,128]{1,0:T(8,128)S(1)} %pad_maximum_fusion), channel_id=1, source_target_pairs={{0,128},{64,192},{128,0},{192,64},{1,129},{65,193},{129,1},{193,65... | collective-permute-start | bytes 12296 | tf_op jit(solution)/shard_map/ppermute | solution.py:35
  159.3 10.5 %collective-permute-start.11 = (f32[8,128]{1,0:T(8,128)S(1)}, f32[8,128]{1,0:T(8,128)S(1)}, u32[]{:S(2)}, u32[]{:S(2)}) collective-permute-start(f32[8,128]{1,0:T(8,128)S(1)} %pad_maximum_fusion), channel_id=1, source_target_pairs={{0,192},{64,0},{128,64},{192,128},{1,193},{65,1},{129,65},{193,129... | collective-permute-start | bytes 12296 | tf_op jit(solution)/shard_map/ppermute | solution.py:35
  160.0 19.7 %all-to-all-start.2 = ((f32[256,1,128]{2,1,0:T(1,128)}), f32[256,1,128]{2,1,0:T(1,128)S(1)}, u32[]{:S(2)}, u32[]{:S(2)}) async-start(f32[256,1,128]{2,1,0:T(1,128)} %broadcast_in_dim.24), calls=%async_computation.2 | async-start | bytes 262144 | tf_op jit(solution)/shard_map/all_to_all | solution.py:354
  166.9 7.7 %collective-permute-start.3 = (bf16[4,2,128,128]{3,2,1,0:T(8,128)(2,1)S(1)}, bf16[4,2,128,128]{3,2,1,0:T(8,128)(2,1)S(1)}, u32[]{:S(2)}, u32[]{:S(2)}) collective-permute-start(bf16[4,2,128,128]{3,2,1,0:T(8,128)(2,1)S(1)} %get-tuple-element.15.h00), channel_id=1, source_target_pairs={{0,64},{64,128},{128,192},{192,0},{1,65},{65,129},{129,193},{193,1... | collective-permute-start | bytes 786440 | tf_op jit(solution)/shard_map/ppermute | solution.py:35
  168.4 11.9 %collective-permute-start.8 = (bf16[4,2,128,128]{3,2,1,0:T(8,128)(2,1)S(1)}, bf16[4,2,128,128]{3,2,1,0:T(8,128)(2,1)S(1)}, u32[]{:S(2)}, u32[]{:S(2)}) collective-permute-start(bf16[4,2,128,128]{3,2,1,0:T(8,128)(2,1)S(1)} %get-tuple-element.15.h00), channel_id=1, source_target_pairs={{0,192},{64,0},{128,64},{192,128},{1,193},{65,1},{129,65},{193,129... | collective-permute-start | bytes 786440 | tf_op jit(solution)/shard_map/ppermute | solution.py:35
  174.6 8.1 %collective-permute-start.4 = (bf16[4,2,128,128]{3,2,1,0:T(8,128)(2,1)S(1)}, bf16[4,2,128,128]{3,2,1,0:T(8,128)(2,1)S(1)}, u32[]{:S(2)}, u32[]{:S(2)}) collective-permute-start(bf16[4,2,128,128]{3,2,1,0:T(8,128)(2,1)S(1)} %collective-permute-done.3.h10), channel_id=1, source_target_pairs={{0,64},{64,128},{128,192},{192,0},{1,65},{65,129},{129,193},{193,1... | collective-permute-start | bytes 786440 | tf_op jit(solution)/shard_map/ppermute | solution.py:35
  177.0 6.2 %collective-permute-start.6 = (bf16[4,2,128,128]{3,2,1,0:T(8,128)(2,1)S(1)}, bf16[4,2,128,128]{3,2,1,0:T(8,128)(2,1)S(1)}, u32[]{:S(2)}, u32[]{:S(2)}) collective-permute-start(bf16[4,2,128,128]{3,2,1,0:T(8,128)(2,1)S(1)} %collective-permute-done.5.h31), channel_id=1, source_target_pairs={{0,192},{64,0},{128,64},{192,128},{1,193},{65,1},{129,65},{193,129... | collective-permute-start | bytes 786440 | tf_op jit(solution)/shard_map/ppermute | solution.py:35
  (1 other events, 0.8 us)

commit v3 on v2

v3 whole, which is shorter than its diff:
```python
import functools

import jax
import jax.numpy as jnp
from jax import lax
from jax.experimental import pallas as pl
from jax.experimental.pallas import tpu as pltpu
from jax.sharding import Mesh
from jax.sharding import PartitionSpec as P

STEPS = 2
STEP_LENGTH = 0.5
PENALTY = 0.5
DIGIT = 64
HALVES = 2
VAR = ("var_0", "var_1", "var_2")
ALL = ("samp", "var_0", "var_1", "var_2")
F32 = jnp.float32
BF16 = jnp.bfloat16
VMEM = pl.BlockSpec(memory_space=pltpu.VMEM)
ANY = pl.BlockSpec(memory_space=pl.ANY)
HBM = pl.BlockSpec(memory_space=pltpu.HBM)


def params(mib):
    return pltpu.CompilerParams(vmem_limit_bytes=mib << 20)


def cost(flops, bytes_accessed):
    return pl.CostEstimate(flops=flops, bytes_accessed=bytes_accessed, transcendentals=0)


def shift(x, axis, k):
    n = lax.axis_size(axis)
    return lax.ppermute(x, axis, [(i, (i + k) % n) for i in range(n)])


def cut_kernel(cols, at_ref, pattern_ref, data_ref, out_ref, note, sems):
    copies = [
        pltpu.make_async_copy(data_ref.at[:, :, h], out_ref.at[:, h, pl.ds(0, cols)], sems.at[h])
        for h in range(data_ref.shape[2])
    ]
    for copy in copies:
        copy.start()
    first, second = pattern_ref[0:1, :], pattern_ref[1:2, :]
    lane = lax.broadcasted_iota(jnp.int32, first.shape, 1)
    block = jnp.where(first == at_ref[0] * cols + lane, second, first)
    place = block + lax.div(block, cols)
    digits = jnp.concatenate([lax.div(place, DIGIT), lax.rem(place, DIGIT)], axis=0).astype(F32)
    rows, width = note.shape[-2:]
    wide = jnp.concatenate([digits, jnp.zeros((rows - 2, cols), F32)], axis=0)
    wide = jnp.concatenate([wide, jnp.zeros((rows, width - cols), F32)], axis=1).astype(note.dtype)
    note[...] = jnp.broadcast_to(wide, note.shape)
    tell = pltpu.make_async_copy(note, out_ref.at[:, :, pl.ds(cols, 1)], sems.at[len(copies)])
    tell.start()
    for copy in copies + [tell]:
        copy.wait()


def cut(var_index, pattern, data, devices, cols, width):
    rows = data.shape[0] // devices
    tile = 2 * rows
    view = data.reshape(devices // 2, tile, cols, width).transpose(0, 2, 1, 3).reshape(devices // 2, cols, 2, rows, width)
    out = pl.pallas_call(
        functools.partial(cut_kernel, cols),
        in_specs=[pl.BlockSpec(memory_space=pltpu.SMEM), VMEM, HBM],
        out_specs=HBM,
        out_shape=jax.ShapeDtypeStruct((devices // 2, 2, cols + 1, rows, width), data.dtype),
        scratch_shapes=[pltpu.VMEM((devices // 2, 2, 1, rows, width), data.dtype), pltpu.SemaphoreType.DMA((3,))],
        compiler_params=params(56),
    )(var_index[None], pattern.T, view)
    return out.reshape(devices, cols + 1, rows, width)


def pick_kernel(cols, shares, table_ref, out_ref, table, notes, digits, wanted, held, sem, sems):
    devices = digits.shape[0]
    each = cols // shares
    tell = pltpu.make_async_copy(table_ref.at[:, pl.ds(cols, 1)], notes, sem.at[0])
    load = pltpu.make_async_copy(table_ref.at[:, pl.ds(0, cols + 1)], table, sem.at[1])
    tell.start()
    load.start()
    tell.wait()
    for u in range(devices):
        note = notes[u, 0].astype(F32)
        digits[u : u + 1, :] = (note[:1] * DIGIT + note[1:2]).astype(jnp.int32)
    move = pltpu.make_async_copy(digits, wanted, sem.at[2])
    move.start()
    move.wait()
    load.wait()
    flat = table.reshape((devices * (cols + 1),) + table.shape[2:])
    sent = []
    for s in range(shares):

        @pl.loop(0, devices, unroll=8)
        def _(d):
            for j in range(each):
                held[s, d, j] = flat[wanted[d, s * each + j]]

        copy = pltpu.make_async_copy(held.at[s], out_ref.at[pl.ds(s * devices, devices)], sems.at[s])
        copy.start()
        sent.append(copy)
    for copy in sent:
        copy.wait()


def pick(table, cols, shares):
    devices, _, rows, width = table.shape
    each = cols // shares
    return pl.pallas_call(
        functools.partial(pick_kernel, cols, shares),
        in_specs=[HBM],
        out_specs=HBM,
        out_shape=jax.ShapeDtypeStruct((shares * devices, each, rows, width), table.dtype),
        scratch_shapes=[
            pltpu.VMEM((devices, cols + 1, rows, width), table.dtype),
            pltpu.VMEM((devices, 1, rows, width), table.dtype),
            pltpu.VMEM((devices, width), jnp.int32),
            pltpu.SMEM((devices, width), jnp.int32),
            pltpu.VMEM((shares, devices, each, rows, width), table.dtype),
            pltpu.SemaphoreType.DMA((3,)),
            pltpu.SemaphoreType.DMA((shares,)),
        ],
        compiler_params=params(56),
    )(table)


def near_kernel(info_ref, own_ref, p1_ref, p2_ref, p3_ref, blocks_ref, near_ref, turned_ref, start_ref):
    samp, rows, width = info_ref[0], own_ref.shape[0], own_ref.shape[1]
    for k, ref in enumerate((own_ref, p1_ref, p2_ref, p3_ref)):
        q = lax.rem(samp + 4 - k, 4)
        at = pl.multiple_of(q * rows, rows)
        x = ref[...]
        near_ref[0, pl.ds(at, rows), :] = x
        turned_ref[0, :, pl.ds(at, rows)] = x.T
    where_diag = info_ref[2 + pl.program_id(0)]
    start_ref[0, :width] = blocks_ref[0, where_diag]
    start_ref[0, width:] = blocks_ref[0, 1 - where_diag]


def near_panels(info, observed, received, blocks, each):
    rows, width = observed.shape[0], blocks.shape[-1]
    part = pl.BlockSpec((rows, width), lambda j, f: (0, j))
    return pl.pallas_call(
        near_kernel,
        grid_spec=pltpu.PrefetchScalarGridSpec(
            num_scalar_prefetch=1,
            grid=(each,),
            in_specs=[
                pl.BlockSpec((rows, width), lambda j, f: (0, f[1] + j)),
                part,
                part,
                part,
                pl.BlockSpec((1, 2, width, width), lambda j, f: (f[1] + j, 0, 0, 0)),
            ],
            out_specs=[
                pl.BlockSpec((1, 4 * rows, width), lambda j, f: (j, 0, 0)),
                pl.BlockSpec((1, width, 4 * rows), lambda j, f: (j, 0, 0)),
                pl.BlockSpec((1, 2 * width, width), lambda j, f: (j, 0, 0)),
            ],
        ),
        out_shape=[
            jax.ShapeDtypeStruct((each, 4 * rows, width), BF16),
            jax.ShapeDtypeStruct((each, width, 4 * rows), BF16),
            jax.ShapeDtypeStruct((each, 2 * width, width), F32),
        ],
        compiler_params=params(56),
        cost_estimate=cost(1 << 20, 10 << 20),
    )(info, observed, *received, blocks)


def shrink(v, level):
    return jnp.where(v > level, v - level, jnp.where(v < -level, v + level, 0.0))


def split3(g):
    hi = g.astype(BF16)
    rest = g - hi.astype(F32)
    mid = rest.astype(BF16)
    return hi, mid, (rest - mid.astype(F32)).astype(BF16)


def steps_kernel(first, info_ref, far_ref, near_ref, turned_ref, start_ref, diag_ref, out_ref, obj_ref):
    count, total_rows, width = far_ref.shape
    eye = lax.broadcasted_iota(jnp.int32, (width, width), 0) == lax.broadcasted_iota(jnp.int32, (width, width), 1)
    each = range(count)
    grams = []
    for c in each:
        far = far_ref[c]
        both = jnp.concatenate([near_ref[first + c], far], axis=1)
        top = jnp.dot(turned_ref[first + c], both, preferred_element_type=F32)
        low = lax.dot_general(far, both, (((0,), (0,)), ((), ())), preferred_element_type=F32)
        grams.append(split3(jnp.concatenate([top, low], axis=0)))
    db = [jnp.where(eye, 0.0, start_ref[first + c, :width]) for c in each]
    ob = [start_ref[first + c, width:] for c in each]
    dv = [diag_ref[pl.ds(info_ref[1] + first + c, 1), :] for c in each]
    lane = lax.broadcasted_iota(jnp.int32, (1, width), 1)
    total = jnp.zeros((1, width), F32)
    for i in range(STEPS):
        w = [
            jnp.concatenate([jnp.where(eye, jnp.broadcast_to(dv[c], (width, width)), db[c]), ob[c]], axis=0).astype(BF16)
            for c in each
        ]
        g = [sum(jnp.dot(p, w[c], preferred_element_type=F32) for p in reversed(grams[c])) for c in each]
        part = jnp.zeros((1, width), F32)
        for c in each:
            fit = jnp.sum(w[c].astype(F32) * g[c], axis=0, keepdims=True) / (2.0 * total_rows)
            size = jnp.sum(jnp.abs(db[c]) + jnp.abs(ob[c]), axis=0, keepdims=True)
            part = part + (fit - jnp.log(dv[c]) + PENALTY * size)
        total = jnp.where(lane == i, jnp.sum(part, axis=1, keepdims=True), total)
        for c in each:
            gd, go = g[c][:width] / total_rows, g[c][width:] / total_rows
            along = jnp.sum(jnp.where(eye, gd, 0.0), axis=0, keepdims=True)
            db[c] = jnp.where(eye, 0.0, shrink(db[c] - STEP_LENGTH * gd, STEP_LENGTH * PENALTY))
            ob[c] = shrink(ob[c] - STEP_LENGTH * go, STEP_LENGTH * PENALTY)
            m = dv[c] - STEP_LENGTH * along
            dv[c] = 0.5 * (m + jnp.sqrt(m * m + 4.0 * STEP_LENGTH))
    obj_ref[...] = total
    for c in each:
        where_diag = info_ref[2 + first + c]
        full = jnp.where(eye, jnp.broadcast_to(dv[c], (width, width)), db[c])
        out_ref[c, where_diag] = full.astype(out_ref.dtype)
        out_ref[c, 1 - where_diag] = ob[c].astype(out_ref.dtype)


def iterate(first, info, far, near, turned, start, diag_rows):
    count, width = far.shape[0], far.shape[2]
    return pl.pallas_call(
        functools.partial(steps_kernel, first),
        in_specs=[pl.BlockSpec(memory_space=pltpu.SMEM)] + [VMEM] * 5,
        out_specs=[VMEM] * 2,
        out_shape=[
            jax.ShapeDtypeStruct((count, 2, width, width), BF16),
            jax.ShapeDtypeStruct((1, width), F32),
        ],
        compiler_params=params(16),
        cost_estimate=cost(count << 29, 4 << 20),
    )(info, far, near, turned, start, diag_rows)


def put(which_ref, out_ref, diag_ref, share, half, count, at, ref):
    j = pl.program_id(0)
    column = (share * HALVES + half) * count + j
    width = ref.shape[-1]
    eye = lax.broadcasted_iota(jnp.int32, (width, width), 0) == lax.broadcasted_iota(jnp.int32, (width, width), 1)
    where_diag = which_ref[column]
    full = ref[0, where_diag].astype(F32)
    diag_ref[pl.ds(column, 1), :] = jnp.sum(jnp.where(eye, full, 0.0), axis=0, keepdims=True)
    out_ref[at, half, 0, where_diag] = jnp.where(eye, 0.0, full)
    out_ref[at, half, 0, 1 - where_diag] = ref[0, 1 - where_diag].astype(F32)


def first_places_kernel(count, samp_ref, which_ref, h00, h01, h10, h11, h30, h31, out_ref, diag_ref):
    for k, refs in ((0, (h00, h01)), (1, (h10, h11)), (3, (h30, h31))):
        q = lax.rem(samp_ref[0] + 4 - k, 4)
        for h, ref in enumerate(refs):
            put(which_ref, out_ref, diag_ref, q, h, count, q, ref)


def last_places_kernel(count, samp_ref, which_ref, h20, h21, _, old_diag_ref, out_ref, diag_ref):
    q = lax.rem(samp_ref[0] + 2, 4)

    @pl.when(pl.program_id(0) == 0)
    def _():
        diag_ref[...] = old_diag_ref[...]

    for h, ref in enumerate((h20, h21)):
        put(which_ref, out_ref, diag_ref, q, h, count, 0, ref)


def place_blocks(samp, which, own, one, three, two):
    count, tail = own[0].shape[0], own[0].shape[1:]
    zeros = (0,) * len(tail)
    part = pl.BlockSpec((1,) + tail, lambda j, f, w: (j,) + zeros)
    diag = pl.BlockSpec((4 * HALVES * count, tail[-1]), lambda j, f, w: (0, 0))
    shapes = [
        jax.ShapeDtypeStruct((4, HALVES, count) + tail, F32),
        jax.ShapeDtypeStruct((4 * HALVES * count, tail[-1]), F32),
    ]
    out, diagonal = pl.pallas_call(
        functools.partial(first_places_kernel, count),
        grid_spec=pltpu.PrefetchScalarGridSpec(
            num_scalar_prefetch=2,
            grid=(count,),
            in_specs=[part] * 6,
            out_specs=[pl.BlockSpec((4, HALVES, 1) + tail, lambda j, f, w: (0, 0, j) + zeros), diag],
        ),
        out_shape=shapes,
        compiler_params=params(24),
        cost_estimate=cost(1 << 20, 6 << 20),
    )(samp[None], which, *own, *one, *three)
    out, diagonal = pl.pallas_call(
        functools.partial(last_places_kernel, count),
        grid_spec=pltpu.PrefetchScalarGridSpec(
            num_scalar_prefetch=2,
            grid=(count,),
            in_specs=[part, part, ANY, diag],
            out_specs=[
                pl.BlockSpec((1, HALVES, 1) + tail, lambda j, f, w: (lax.rem(f[0] + 2, 4), 0, j) + zeros),
                diag,
            ],
        ),
        out_shape=shapes,
        input_output_aliases={4: 0},
        compiler_params=params(16),
        cost_estimate=cost(1 << 20, 2 << 20),
    )(samp[None], which, *two, out, diagonal)
    return out.reshape((4 * HALVES * count,) + tail), diagonal.reshape(-1)


def body(observed, blocks, diagonal, pattern):
    cols, _, width, _ = blocks.shape
    rows = observed.shape[0]
    devices = lax.axis_size(VAR)
    shares = lax.axis_size("samp")
    each = cols // shares
    half = each // HALVES
    total_rows = rows * shares
    samp = lax.axis_index("samp").astype(jnp.int32)
    var_index = lax.axis_index(VAR).astype(jnp.int32)

    pieces = cut(var_index, pattern, observed, devices, cols, width)
    panel = each * width
    received = [shift(lax.dynamic_slice_in_dim(observed, lax.rem(samp + k, shares) * panel, panel, 1), "samp", k) for k in (1, 2, 3)]
    table = lax.all_to_all(pieces, VAR, split_axis=0, concat_axis=0, tiled=True)
    start = samp * each
    columns = var_index * cols + jnp.arange(cols, dtype=jnp.int32)
    which = jnp.where(pattern[:, 0] == columns, 0, 1).astype(jnp.int32)
    info = jnp.concatenate([jnp.stack([samp, start]), lax.dynamic_slice_in_dim(which, start, each, 0)])
    near, turned, begin = near_panels(info, observed, received, blocks, each)
    outgoing = pick(table, cols, shares)
    far = lax.all_to_all(outgoing, ALL, split_axis=0, concat_axis=0, tiled=True)

    diag_rows = diagonal.reshape(cols, width)
    new, objs = [], []
    for h in range(HALVES):
        far_h = far[:, h * half : (h + 1) * half].transpose(1, 0, 2, 3).reshape(half, total_rows, width)
        done = iterate(h * half, info, far_h, near, turned, begin, diag_rows)
        new.append(done[0])
        objs.append(done[1])

    one = [shift(x, "samp", 1) for x in new]
    three = [shift(x, "samp", 3) for x in new]
    two = [shift(one[0], "samp", 1), shift(three[1], "samp", 3)]
    new_blocks, new_diagonal = place_blocks(samp, which, new, one, three, two)

    mine = jnp.broadcast_to(objs[0] + objs[1], (shares * devices, width))
    objective = jnp.sum(lax.all_to_all(mine, ALL, split_axis=0, concat_axis=0, tiled=True), axis=0)
    return (new_blocks, new_diagonal, objective[:STEPS] / (cols * devices * width))


def solution(mesh):
    torus = Mesh(mesh.devices.reshape(mesh.shape["samp"], 4, 8, 2), ALL)
    placed = (P("samp", VAR), P(VAR, None, None, None), P(VAR), P(VAR, None))
    return jax.shard_map(
        body,
        mesh=torus,
        in_specs=placed,
        out_specs=(P(VAR, None, None, None), P(VAR), P()),
        check_vma=False,
    )
```

time: 188 us -> 246 us (1.31); the launches traced: 185 us -> 246 us
  blocking collectives: 0 us -> 67.8 us
  Pallas kernels: 31.7 us -> 87.9 us
  waiting for transfers between devices: 97.5 us -> 50.5 us
  starting transfers between devices: 45.1 us -> 30.5 us
    all_to_all x0 -> x1, blocking collectives: none -> 67.8 us  [body(): table = lax.all_to_all(pieces, VAR, split_axis=0, concat_axis=0, tiled=True)]
    pallas_call x6, Pallas kernels: 24.1 us -> 80.4 us  [the longest x1 65.3 us: cut(): pl.pallas_call(functools.partial(cut_kernel, cols), in_specs=[pl.BlockSpe...]
    all_to_all x1, waiting for transfers between devices: 54.8 us -> 0.01 us  [body(): far = lax.all_to_all(outgoing, ALL, split_axis=0, concat_axis=0, tiled=True)]
    ppermute x12 -> x9, waiting for transfers between devices: 26.7 us -> 42 us  [shift(): return lax.ppermute(x, axis, [(i, (i + k) % n) for i in range(n)])]
    all_to_all x1 -> x0, waiting for transfers between devices: 15.2 us -> none  [body(): table = lax.all_to_all(pieces, VAR, split_axis=0, concat_axis=0, tiled=True)]
    all_to_all x1 -> x0, starting transfers between devices: 13.3 us -> none  [body(): table = lax.all_to_all(pieces, VAR, split_axis=0, concat_axis=0, tiled=True)]
    all_to_all x1, waiting for transfers between devices: 0.72 us -> 8.52 us  [body(): lax.all_to_all(mine, ALL, split_axis=0, concat_axis=0, tiled=True)]
    ppermute x12 -> x9, starting transfers between devices: 16.3 us -> 9.51 us  [shift(): return lax.ppermute(x, axis, [(i, (i + k) % n) for i in range(n)])]
  transfers between devices with their start and end apart: 15 -> 11, of which waited for: 7 -> 4; matrix products, arithmetic and copies ran while one was open for 2% -> 1% of each run, Pallas kernels for 7% -> 4%
where the time goes in v3:
time: 246 us
  Pallas kernels  87.9 us (36%)
  blocking collectives  67.8 us (28%)
  waiting for transfers between devices  50.5 us (21%)
  starting transfers between devices  30.5 us (12%)
  local copies, waits for them, and re-layouts  7.12 us (3%)
    all_to_all x1, blocking collectives, body(): table = lax.all_to_all(pieces, VAR, split_axis=0, concat_axis=0, tiled=True)  67.8 us
    pallas_call x1, Pallas kernels, cut(): pl.pallas_call(functools.partial(cut_kernel, cols), in_specs=[pl.BlockSpe...  65.3 us
    ppermute x9, waiting for transfers between devices, shift(): return lax.ppermute(x, axis, [(i, (i + k) % n) for i in range(n)])  42 us
    all_to_all x1, starting transfers between devices, body(): lax.all_to_all(mine, ALL, split_axis=0, concat_axis=0, tiled=True)  13.2 us
    ppermute x9, starting transfers between devices, shift(): return lax.ppermute(x, axis, [(i, (i + k) % n) for i in range(n)])  9.51 us
    all_to_all x1, waiting for transfers between devices, body(): lax.all_to_all(mine, ALL, split_axis=0, concat_axis=0, tiled=True)  8.52 us
    all_to_all x1, starting transfers between devices, body(): far = lax.all_to_all(outgoing, ALL, split_axis=0, concat_axis=0, tiled=True)  7.76 us
    pallas_call x1, Pallas kernels, near_panels(): pl.pallas_call(near_kernel, grid_spec=pltpu.PrefetchScalarGridSpec(num_sc...  7.53 us
  transfers between devices with their start and end apart: 11, of which 4 were waited for; matrix products, arithmetic and copies ran while one was open for 1% of the time, Pallas kernels for 4%

profile of v3, /device:TPU:1, one launch (start us, length us, event | category | flops | bytes accessed | tf_op | source)
XLA Modules:
  0.0 245.8 jit_solution(3473070936134050072)
XLA Ops:
  0.6 65.3 %shard_map.67 = bf16[32,2,33,4,128]{4,3,2,1,0:T(4,128)(2,1)} custom-call(s32[1]{0:T(128)} %bitcast.3.at_ref, s32[2,32]{1,0:T(2,128)} %bitcast.32, bf16[32,32,2,4,128]{4,3,2,1,0:T(4,128)(2,1)} %bitcast.28), custom_call_target="tpu_custom_call" | custom-call | tf_op jit(solution)/shard_map/pallas_call | solution.py:64
  66.0 67.8 %all_to_all.16.table_ref = bf16[64,33,4,128]{3,2,1,0:T(4,128)(2,1)} all-to-all(bf16[64,33,4,128]{3,2,1,0:T(4,128)(2,1)} %bitcast.29), channel_id=1, replica_groups=mesh['samp'=4,'var_0'=4,'var_1'=8,'var_2'=2] {'var_0','var_1','var_2'}, dimensions={0} | all-to-all | bytes 4325376 | tf_op jit(solution)/shard_map/all_to_all | solution.py:324
  133.8 5.2 %shard_map.68 = bf16[256,8,4,128]{3,2,1,0:T(4,128)(2,1)} custom-call(bf16[64,33,4,128]{3,2,1,0:T(4,128)(2,1)} %all_to_all.16.table_ref), custom_call_target="tpu_custom_call" | custom-call | tf_op jit(solution)/shard_map/pallas_call | solution.py:109
  139.0 7.8 %all-to-all-start.1 = ((bf16[256,8,4,128]{3,2,1,0:T(4,128)(2,1)}), bf16[256,8,4,128]{3,2,1,0:T(4,128)(2,1)}, u32[]{:S(2)}, u32[]{:S(2)}) async-start(bf16[256,8,4,128]{3,2,1,0:T(4,128)(2,1)} %shard_map.68), calls=%async_computation.1 | async-start | bytes 4194304 | tf_op jit(solution)/shard_map/all_to_all | solution.py:331
  146.8 1.0 constant_dynamic-slice_fusion
  147.8 2.6 %collective-permute-start.2 = (bf16[256,1024]{1,0:T(8,128)(2,1)}, bf16[256,1024]{1,0:T(8,128)(2,1)S(1)}, u32[]{:S(2)}, u32[]{:S(2)}) collective-permute-start(bf16[256,1024]{1,0:T(8,128)(2,1)} %get-tuple-element.27), channel_id=1, source_target_pairs={{0,192},{64,0},{128,64},{192,128},{1,193},{65,1},{129,65},{193,129... | collective-permute-start | bytes 1572872 | tf_op jit(solution)/shard_map/ppermute | solution.py:35
  152.2 20.1 %collective-permute-done.2.p3_ref = bf16[256,1024]{1,0:T(8,128)(2,1)S(1)} collective-permute-done((bf16[256,1024]{1,0:T(8,128)(2,1)}, bf16[256,1024]{1,0:T(8,128)(2,1)S(1)}, u32[]{:S(2)}, u32[]{:S(2)}) %collective-permute-start.2) | collective-permute-done | bytes 524320 | tf_op jit(solution)/shard_map/ppermute | solution.py:35
  172.9 21.3 %collective-permute-done.p1_ref = bf16[256,1024]{1,0:T(8,128)(2,1)S(1)} collective-permute-done((bf16[256,1024]{1,0:T(8,128)(2,1)S(1)}, bf16[256,1024]{1,0:T(8,128)(2,1)S(1)}, u32[]{:S(2)}, u32[]{:S(2)}) %collective-permute-start) | collective-permute-done | bytes 524320 | tf_op jit(solution)/shard_map/ppermute | solution.py:35
  194.2 0.8 copy-done.8
  195.0 7.5 %shard_map.69 = (bf16[8,1024,128]{2,1,0:T(8,128)(2,1)}, bf16[8,128,1024]{2,1,0:T(8,128)(2,1)}, f32[8,256,128]{2,1,0:T(8,128)}) custom-call(s32[10]{0:T(128)} %pad_add_fusion.info_ref, bf16[256,4096]{1,0:T(8,128)(2,1)} %own_ref.1, bf16[256,1024]{1,0:T(8,128)(2,1)} %copy-done.8, bf16[256,1024]{1,0:T(8,128)(2,1)} %copy-done.7, bf16[256,1024]{1,0:T(8,128)(2,1)} %copy-done.6, ...), custom_call_target="tpu_custom_call" | custom-call | flops 1048576 | bytes 10485760 | tf_op jit(solution)/shard_map/pallas_call | solution.py:143
  202.5 2.4 slice_bitcast_fusion
  205.7 0.8 copy-done.1
  206.5 0.6 copy-done.2
  207.1 2.3 shard_map.71
  209.4 2.3 shard_map.70
  211.7 1.5 collective-permute-start.3
  213.2 0.7 broadcast_in_dim.24
  213.9 13.2 %all-to-all-start.2 = ((f32[256,1,128]{2,1,0:T(1,128)}), f32[256,1,128]{2,1,0:T(1,128)S(1)}, u32[]{:S(2)}, u32[]{:S(2)}) async-start(f32[256,1,128]{2,1,0:T(1,128)} %broadcast_in_dim.24), calls=%async_computation.2 | async-start | bytes 262144 | tf_op jit(solution)/shard_map/all_to_all | solution.py:347
  227.1 1.5 collective-permute-start.7
  228.6 1.4 collective-permute-start.8
  230.0 1.4 collective-permute-start.6
  231.4 8.5 %all-to-all-done.2 = f32[256,1,128]{2,1,0:T(1,128)S(1)} async-done(((f32[256,1,128]{2,1,0:T(1,128)}), f32[256,1,128]{2,1,0:T(1,128)S(1)}, u32[]{:S(2)}, u32[]{:S(2)}) %all-to-all-start.2) | async-done | bytes 131104 | tf_op jit(solution)/shard_map/all_to_all | solution.py:347
  240.5 3.2 %shard_map.72 = (f32[4,2,4,2,128,128]{5,4,3,2,1,0:T(8,128)}, f32[32,128]{1,0:T(8,128)S(1)}) custom-call(s32[1]{0:T(128)} %bitcast.samp_ref, s32[32]{0:T(128)S(1)} %compare_select_fusion.which_ref, bf16[4,2,128,128]{3,2,1,0:T(8,128)(2,1)S(1)} %get-tuple-element.17.h00, bf16[4,2,128,128]{3,2,1,0:T(8,128)(2,1)S(1)} %get-tuple-element.18.h01, ...), custom_call_target="tpu_custom_call" | custom-call | flops 1048576 | bytes 6291456 | tf_op jit(solution)/shard_map/pallas_call | solution.py:279
  243.7 2.1 shard_map.73
  (37 shorter events, 3.8 us)
Async XLA Ops:
  139.0 7.8 %copy-start.5 = (bf16[256,4096]{1,0:T(8,128)(2,1)S(1)}, bf16[256,4096]{1,0:T(8,128)(2,1)}, u32[]{:S(2)}) copy-start(bf16[256,4096]{1,0:T(8,128)(2,1)} %own_ref.1) | copy-start | bytes 6291460
  139.0 63.5 %all-to-all-start.1 = ((bf16[256,8,4,128]{3,2,1,0:T(4,128)(2,1)}), bf16[256,8,4,128]{3,2,1,0:T(4,128)(2,1)}, u32[]{:S(2)}, u32[]{:S(2)}) async-start(bf16[256,8,4,128]{3,2,1,0:T(4,128)(2,1)} %shard_map.68), calls=%async_computation.1 | async-start | bytes 4194304 | tf_op jit(solution)/shard_map/all_to_all | solution.py:331
  146.8 4.8 %copy-start.9 = (s32[32,2]{0,1:T(2,128)S(1)}, s32[32,2]{0,1:T(2,128)}, u32[]{:S(2)}) copy-start(s32[32,2]{0,1:T(2,128)} %param.7) | copy-start | bytes 772
  147.8 24.5 %collective-permute-start.2 = (bf16[256,1024]{1,0:T(8,128)(2,1)}, bf16[256,1024]{1,0:T(8,128)(2,1)S(1)}, u32[]{:S(2)}, u32[]{:S(2)}) collective-permute-start(bf16[256,1024]{1,0:T(8,128)(2,1)} %get-tuple-element.27), channel_id=1, source_target_pairs={{0,192},{64,0},{128,64},{192,128},{1,193},{65,1},{129,65},{193,129... | collective-permute-start | bytes 1572872 | tf_op jit(solution)/shard_map/ppermute | solution.py:35
  150.4 22.5 %collective-permute-start.1 = (bf16[256,1024]{1,0:T(8,128)(2,1)S(1)}, bf16[256,1024]{1,0:T(8,128)(2,1)S(1)}, u32[]{:S(2)}, u32[]{:S(2)}) collective-permute-start(bf16[256,1024]{1,0:T(8,128)(2,1)S(1)} %get-tuple-element.28), channel_id=1, source_target_pairs={{0,128},{64,192},{128,0},{192,64},{1,129},{65,193},{129,1},{193,65... | collective-permute-start | bytes 1572872 | tf_op jit(solution)/shard_map/ppermute | solution.py:35
  150.9 43.2 %collective-permute-start = (bf16[256,1024]{1,0:T(8,128)(2,1)S(1)}, bf16[256,1024]{1,0:T(8,128)(2,1)S(1)}, u32[]{:S(2)}, u32[]{:S(2)}) collective-permute-start(bf16[256,1024]{1,0:T(8,128)(2,1)S(1)} %get-tuple-element.29), channel_id=1, source_target_pairs={{0,64},{64,128},{128,192},{192,0},{1,65},{65,129},{129,193},{193,1... | collective-permute-start | bytes 1572872 | tf_op jit(solution)/shard_map/ppermute | solution.py:35
  172.3 21.9 %copy-start.6 = (bf16[256,1024]{1,0:T(8,128)(2,1)}, bf16[256,1024]{1,0:T(8,128)(2,1)S(1)}, u32[]{:S(2)}) copy-start(bf16[256,1024]{1,0:T(8,128)(2,1)S(1)} %collective-permute-done.2.p3_ref) | copy-start | bytes 1572868
  172.9 21.3 %copy-start.7 = (bf16[256,1024]{1,0:T(8,128)(2,1)}, bf16[256,1024]{1,0:T(8,128)(2,1)S(1)}, u32[]{:S(2)}) copy-start(bf16[256,1024]{1,0:T(8,128)(2,1)S(1)} %collective-permute-done.1.p2_ref) | copy-start | bytes 1572868
  194.2 0.8 copy-start.8
  202.5 3.1 %copy-start.3 = (f32[8,256,128]{2,1,0:T(8,128)S(1)}, f32[8,256,128]{2,1,0:T(8,128)}, u32[]{:S(2)}) copy-start(f32[8,256,128]{2,1,0:T(8,128)} %get-tuple-element.16.start_ref) | copy-start | bytes 3145732
  202.5 3.2 %copy-start.4 = (f32[4096]{0:T(1024)S(1)}, f32[4096]{0:T(1024)}, u32[]{:S(2)}) copy-start(f32[4096]{0:T(1024)} %param.6) | copy-start | bytes 49156
  204.9 0.8 copy-start
  204.9 1.6 copy-start.1
  204.9 2.2 copy-start.2
  211.7 18.2 %collective-permute-start.5 = (bf16[4,2,128,128]{3,2,1,0:T(8,128)(2,1)S(1)}, bf16[4,2,128,128]{3,2,1,0:T(8,128)(2,1)S(1)}, u32[]{:S(2)}, u32[]{:S(2)}) collective-permute-start(bf16[4,2,128,128]{3,2,1,0:T(8,128)(2,1)S(1)} %get-tuple-element.18.h01), channel_id=1, source_target_pairs={{0,192},{64,0},{128,64},{192,128},{1,193},{65,1},{129,65},{193,129... | collective-permute-start | bytes 786440 | tf_op jit(solution)/shard_map/ppermute | solution.py:35
  211.7 19.6 %collective-permute-start.3 = (bf16[4,2,128,128]{3,2,1,0:T(8,128)(2,1)S(1)}, bf16[4,2,128,128]{3,2,1,0:T(8,128)(2,1)S(1)}, u32[]{:S(2)}, u32[]{:S(2)}) collective-permute-start(bf16[4,2,128,128]{3,2,1,0:T(8,128)(2,1)S(1)} %get-tuple-element.17.h00), channel_id=1, source_target_pairs={{0,64},{64,128},{128,192},{192,0},{1,65},{65,129},{129,193},{193,1... | collective-permute-start | bytes 786440 | tf_op jit(solution)/shard_map/ppermute | solution.py:35
  213.9 26.0 %all-to-all-start.2 = ((f32[256,1,128]{2,1,0:T(1,128)}), f32[256,1,128]{2,1,0:T(1,128)S(1)}, u32[]{:S(2)}, u32[]{:S(2)}) async-start(f32[256,1,128]{2,1,0:T(1,128)} %broadcast_in_dim.24), calls=%async_computation.2 | async-start | bytes 262144 | tf_op jit(solution)/shard_map/all_to_all | solution.py:347
  227.1 13.4 %collective-permute-start.7 = (bf16[4,2,128,128]{3,2,1,0:T(8,128)(2,1)S(1)}, bf16[4,2,128,128]{3,2,1,0:T(8,128)(2,1)S(1)}, u32[]{:S(2)}, u32[]{:S(2)}) collective-permute-start(bf16[4,2,128,128]{3,2,1,0:T(8,128)(2,1)S(1)} %get-tuple-element.18.h01), channel_id=1, source_target_pairs={{0,64},{64,128},{128,192},{192,0},{1,65},{65,129},{129,193},{193,1... | collective-permute-start | bytes 786440 | tf_op jit(solution)/shard_map/ppermute | solution.py:35
  228.6 11.9 %collective-permute-start.8 = (bf16[4,2,128,128]{3,2,1,0:T(8,128)(2,1)S(1)}, bf16[4,2,128,128]{3,2,1,0:T(8,128)(2,1)S(1)}, u32[]{:S(2)}, u32[]{:S(2)}) collective-permute-start(bf16[4,2,128,128]{3,2,1,0:T(8,128)(2,1)S(1)} %get-tuple-element.17.h00), channel_id=1, source_target_pairs={{0,192},{64,0},{128,64},{192,128},{1,193},{65,1},{129,65},{193,129... | collective-permute-start | bytes 786440 | tf_op jit(solution)/shard_map/ppermute | solution.py:35
  230.0 13.7 %collective-permute-start.6 = (bf16[4,2,128,128]{3,2,1,0:T(8,128)(2,1)S(1)}, bf16[4,2,128,128]{3,2,1,0:T(8,128)(2,1)S(1)}, u32[]{:S(2)}, u32[]{:S(2)}) collective-permute-start(bf16[4,2,128,128]{3,2,1,0:T(8,128)(2,1)S(1)} %collective-permute-done.5.h31), channel_id=1, source_target_pairs={{0,192},{64,0},{128,64},{192,128},{1,193},{65,1},{129,65},{193,129... | collective-permute-start | bytes 786440 | tf_op jit(solution)/shard_map/ppermute | solution.py:35
  231.3 12.3 %collective-permute-start.4 = (bf16[4,2,128,128]{3,2,1,0:T(8,128)(2,1)S(1)}, bf16[4,2,128,128]{3,2,1,0:T(8,128)(2,1)S(1)}, u32[]{:S(2)}, u32[]{:S(2)}) collective-permute-start(bf16[4,2,128,128]{3,2,1,0:T(8,128)(2,1)S(1)} %collective-permute-done.3.h10), channel_id=1, source_target_pairs={{0,64},{64,128},{128,192},{192,0},{1,65},{65,129},{129,193},{193,1... | collective-permute-start | bytes 786440 | tf_op jit(solution)/shard_map/ppermute | solution.py:35

commit v4 on v3

--- a/solution.py
+++ b/solution.py
@@ -35,44 +35,46 @@
     return lax.ppermute(x, axis, [(i, (i + k) % n) for i in range(n)])
 
 
-def cut_kernel(cols, at_ref, pattern_ref, data_ref, out_ref, note, sems):
-    copies = [
-        pltpu.make_async_copy(data_ref.at[:, :, h], out_ref.at[:, h, pl.ds(0, cols)], sems.at[h])
-        for h in range(data_ref.shape[2])
-    ]
-    for copy in copies:
-        copy.start()
+def cut_kernel(cols, at_ref, pattern_ref, data_ref, out_ref):
+    tiles, _, halves, rows, width = data_ref.shape
+    for t in range(tiles):
+        for b in range(cols):
+            for h in range(halves):
+                out_ref[t, h, b] = data_ref[t, b, h]
     first, second = pattern_ref[0:1, :], pattern_ref[1:2, :]
     lane = lax.broadcasted_iota(jnp.int32, first.shape, 1)
     block = jnp.where(first == at_ref[0] * cols + lane, second, first)
     place = block + lax.div(block, cols)
     digits = jnp.concatenate([lax.div(place, DIGIT), lax.rem(place, DIGIT)], axis=0).astype(F32)
-    rows, width = note.shape[-2:]
     wide = jnp.concatenate([digits, jnp.zeros((rows - 2, cols), F32)], axis=0)
-    wide = jnp.concatenate([wide, jnp.zeros((rows, width - cols), F32)], axis=1).astype(note.dtype)
-    note[...] = jnp.broadcast_to(wide, note.shape)
-    tell = pltpu.make_async_copy(note, out_ref.at[:, :, pl.ds(cols, 1)], sems.at[len(copies)])
-    tell.start()
-    for copy in copies + [tell]:
-        copy.wait()
+    wide = jnp.concatenate([wide, jnp.zeros((rows, width - cols), F32)], axis=1).astype(out_ref.dtype)
+    for t in range(tiles):
+        for h in range(halves):
+            out_ref[t, h, cols] = wide
 
 
 def cut(var_index, pattern, data, devices, cols, width):
     rows = data.shape[0] // devices
-    tile = 2 * rows
-    view = data.reshape(devices // 2, tile, cols, width).transpose(0, 2, 1, 3).reshape(devices // 2, cols, 2, rows, width)
+    tiles = devices // 2
+    view = data.reshape(tiles, 2 * rows, cols, width).transpose(0, 2, 1, 3).reshape(tiles, cols, 2, rows, width)
+    block = 4
     out = pl.pallas_call(
         functools.partial(cut_kernel, cols),
-        in_specs=[pl.BlockSpec(memory_space=pltpu.SMEM), VMEM, HBM],
-        out_specs=HBM,
-        out_shape=jax.ShapeDtypeStruct((devices // 2, 2, cols + 1, rows, width), data.dtype),
-        scratch_shapes=[pltpu.VMEM((devices // 2, 2, 1, rows, width), data.dtype), pltpu.SemaphoreType.DMA((3,))],
+        grid=(tiles // block,),
+        in_specs=[
+            pl.BlockSpec(memory_space=pltpu.SMEM),
+            pl.BlockSpec((2, cols), lambda i: (0, 0)),
+            pl.BlockSpec((block, cols, 2, rows, width), lambda i: (i, 0, 0, 0, 0)),
+        ],
+        out_specs=pl.BlockSpec((block, 2, cols + 1, rows, width), lambda i: (i, 0, 0, 0, 0)),
+        out_shape=jax.ShapeDtypeStruct((tiles, 2, cols + 1, rows, width), data.dtype),
         compiler_params=params(56),
     )(var_index[None], pattern.T, view)
     return out.reshape(devices, cols + 1, rows, width)
 
 
-def pick_kernel(cols, shares, table_ref, out_ref, table, notes, digits, wanted, held, sem, sems):
+def pick_kernel(cols, shares, table_ref, *rest):
+    out_ref, table, notes, digits, wanted, held, sem, sems = rest[-8:]
     devices = digits.shape[0]
     each = cols // shares
     tell = pltpu.make_async_copy(table_ref.at[:, pl.ds(cols, 1)], notes, sem.at[0])
@@ -103,12 +105,12 @@
         copy.wait()
 
 
-def pick(table, cols, shares):
+def pick(table, cols, shares, after):
     devices, _, rows, width = table.shape
     each = cols // shares
     return pl.pallas_call(
         functools.partial(pick_kernel, cols, shares),
-        in_specs=[HBM],
+        in_specs=[HBM] + [HBM] * len(after),
         out_specs=HBM,
         out_shape=jax.ShapeDtypeStruct((shares * devices, each, rows, width), table.dtype),
         scratch_shapes=[
@@ -121,7 +123,7 @@
             pltpu.SemaphoreType.DMA((shares,)),
         ],
         compiler_params=params(56),
-    )(table)
+    )(table, *after)
 
 
 def near_kernel(info_ref, own_ref, p1_ref, p2_ref, p3_ref, blocks_ref, near_ref, turned_ref, start_ref):
@@ -327,7 +329,7 @@
     which = jnp.where(pattern[:, 0] == columns, 0, 1).astype(jnp.int32)
     info = jnp.concatenate([jnp.stack([samp, start]), lax.dynamic_slice_in_dim(which, start, each, 0)])
     near, turned, begin = near_panels(info, observed, received, blocks, each)
-    outgoing = pick(table, cols, shares)
+    outgoing = pick(table, cols, shares, (near, turned, begin))
     far = lax.all_to_all(outgoing, ALL, split_axis=0, concat_axis=0, tiled=True)
 
     diag_rows = diagonal.reshape(cols, width)
@@ -343,7 +345,8 @@
     two = [shift(one[0], "samp", 1), shift(three[1], "samp", 3)]
     new_blocks, new_diagonal = place_blocks(samp, which, new, one, three, two)
 
-    mine = jnp.broadcast_to(objs[0] + objs[1], (shares * devices, width))
+    later = jnp.minimum(jnp.abs(three[1][0, 0, 0].astype(F32)), 0.0)
+    mine = jnp.broadcast_to(objs[0] + objs[1] + later, (shares * devices, width))
     objective = jnp.sum(lax.all_to_all(mine, ALL, split_axis=0, concat_axis=0, tiled=True), axis=0)
     return (new_blocks, new_diagonal, objective[:STEPS] / (cols * devices * width))
 

time: 246 us -> 177 us (0.72)
  Pallas kernels: 87.9 us -> 28.6 us
  waiting for transfers between devices: 50.5 us -> 45.6 us
  blocking collectives: 67.8 us -> 63.4 us
    pallas_call x1, Pallas kernels: 65.3 us -> 5.99 us  [cut(): pl.pallas_call(functools.partial(cut_kernel, cols), grid=(tiles // block,...]
    ppermute x9, waiting for transfers between devices: 42 us -> 25 us  [shift(): return lax.ppermute(x, axis, [(i, (i + k) % n) for i in range(n)])]
    all_to_all x1, waiting for transfers between devices: 0.01 us -> 13.7 us  [body(): table = lax.all_to_all(pieces, VAR, split_axis=0, concat_axis=0, tiled=True)]
    all_to_all x1, starting transfers between devices: 7.76 us -> 13.3 us  [body(): table = lax.all_to_all(pieces, VAR, split_axis=0, concat_axis=0, tiled=True)]
    all_to_all x1, starting transfers between devices: 13.2 us -> 7.88 us  [body(): lax.all_to_all(mine, ALL, split_axis=0, concat_axis=0, tiled=True)]
    all_to_all x1, blocking collectives: 67.8 us -> 63.4 us  [body(): far = lax.all_to_all(outgoing, ALL, split_axis=0, concat_axis=0, tiled=True)]
  transfers between devices with their start and end apart: 11 -> 11, of which waited for: 4 -> 4; matrix products, arithmetic and copies ran while one was open for 1% -> 2% of each run, Pallas kernels for 4% -> 7%
where the time goes in v4:
time: 177 us
  blocking collectives  63.4 us (36%)
  waiting for transfers between devices  45.6 us (26%)
  starting transfers between devices  31.3 us (18%)
  Pallas kernels  28.6 us (16%)
  local copies, waits for them, and re-layouts  5.68 us (3%)
    all_to_all x1, blocking collectives, body(): far = lax.all_to_all(outgoing, ALL, split_axis=0, concat_axis=0, tiled=True)  63.4 us
    ppermute x9, waiting for transfers between devices, shift(): return lax.ppermute(x, axis, [(i, (i + k) % n) for i in range(n)])  25 us
    all_to_all x1, waiting for transfers between devices, body(): table = lax.all_to_all(pieces, VAR, split_axis=0, concat_axis=0, tiled=True)  13.7 us
    all_to_all x1, starting transfers between devices, body(): table = lax.all_to_all(pieces, VAR, split_axis=0, concat_axis=0, tiled=True)  13.3 us
    ppermute x9, starting transfers between devices, shift(): return lax.ppermute(x, axis, [(i, (i + k) % n) for i in range(n)])  10.2 us
    all_to_all x1, starting transfers between devices, body(): lax.all_to_all(mine, ALL, split_axis=0, concat_axis=0, tiled=True)  7.88 us
    pallas_call x1, Pallas kernels, near_panels(): pl.pallas_call(near_kernel, grid_spec=pltpu.PrefetchScalarGridSpec(num_sc...  7.56 us
    all_to_all x1, waiting for transfers between devices, body(): lax.all_to_all(mine, ALL, split_axis=0, concat_axis=0, tiled=True)  6.96 us
  transfers between devices with their start and end apart: 11, of which 4 were waited for; matrix products, arithmetic and copies ran while one was open for 2% of the time, Pallas kernels for 7%

profile of v4, /device:TPU:1, one launch (start us, length us, event | category | flops | bytes accessed | tf_op | source)
XLA Modules:
  0.0 176.6 jit_solution(14913648589670955805)
XLA Ops:
  0.6 6.0 %shard_map.67 = bf16[32,2,33,4,128]{4,3,2,1,0:T(4,128)(2,1)} custom-call(s32[1]{0:T(128)} %bitcast.3.at_ref, s32[2,32]{1,0:T(2,128)} %bitcast.38, bf16[32,32,2,4,128]{4,3,2,1,0:T(4,128)(2,1)} %bitcast.34), custom_call_target="tpu_custom_call" | custom-call | tf_op jit(solution)/shard_map/pallas_call | solution.py:61
  6.6 13.3 %all-to-all-start = ((bf16[64,33,4,128]{3,2,1,0:T(4,128)(2,1)}), bf16[64,33,4,128]{3,2,1,0:T(4,128)(2,1)}, u32[]{:S(2)}, u32[]{:S(2)}) async-start(bf16[64,33,4,128]{3,2,1,0:T(4,128)(2,1)} %bitcast.35), calls=%async_computation | async-start | bytes 4325376 | tf_op jit(solution)/shard_map/all_to_all | solution.py:326
  20.0 1.0 constant_dynamic-slice_fusion
  20.9 2.7 %collective-permute-start.2 = (bf16[256,1024]{1,0:T(8,128)(2,1)}, bf16[256,1024]{1,0:T(8,128)(2,1)S(1)}, u32[]{:S(2)}, u32[]{:S(2)}) collective-permute-start(bf16[256,1024]{1,0:T(8,128)(2,1)} %get-tuple-element.27), channel_id=1, source_target_pairs={{0,192},{64,0},{128,64},{192,128},{1,193},{65,1},{129,65},{193,129... | collective-permute-start | bytes 1572872 | tf_op jit(solution)/shard_map/ppermute | solution.py:35
  24.0 0.7 collective-permute-start
  25.4 20.5 %collective-permute-done.2.p3_ref = bf16[256,1024]{1,0:T(8,128)(2,1)S(1)} collective-permute-done((bf16[256,1024]{1,0:T(8,128)(2,1)}, bf16[256,1024]{1,0:T(8,128)(2,1)S(1)}, u32[]{:S(2)}, u32[]{:S(2)}) %collective-permute-start.2) | collective-permute-done | bytes 524320 | tf_op jit(solution)/shard_map/ppermute | solution.py:35
  45.9 4.5 %collective-permute-done.p1_ref = bf16[256,1024]{1,0:T(8,128)(2,1)S(1)} collective-permute-done((bf16[256,1024]{1,0:T(8,128)(2,1)S(1)}, bf16[256,1024]{1,0:T(8,128)(2,1)S(1)}, u32[]{:S(2)}, u32[]{:S(2)}) %collective-permute-start) | collective-permute-done | bytes 524320 | tf_op jit(solution)/shard_map/ppermute | solution.py:35
  50.4 0.8 copy-done.8
  51.2 7.6 %shard_map.68 = (bf16[8,1024,128]{2,1,0:T(8,128)(2,1)}, bf16[8,128,1024]{2,1,0:T(8,128)(2,1)}, f32[8,256,128]{2,1,0:T(8,128)}) custom-call(s32[10]{0:T(128)} %pad_add_fusion.info_ref, bf16[256,4096]{1,0:T(8,128)(2,1)} %own_ref.1, bf16[256,1024]{1,0:T(8,128)(2,1)} %copy-done.8, bf16[256,1024]{1,0:T(8,128)(2,1)} %copy-done.7, bf16[256,1024]{1,0:T(8,128)(2,1)} %copy-done.6, ...), custom_call_target="tpu_custom_call" | custom-call | flops 1048576 | bytes 10485760 | tf_op jit(solution)/shard_map/pallas_call | solution.py:145
  58.7 13.7 %all-to-all-done.table_ref = bf16[64,33,4,128]{3,2,1,0:T(4,128)(2,1)} async-done(((bf16[64,33,4,128]{3,2,1,0:T(4,128)(2,1)}), bf16[64,33,4,128]{3,2,1,0:T(4,128)(2,1)}, u32[]{:S(2)}, u32[]{:S(2)}) %all-to-all-start) | async-done | bytes 2162720 | tf_op jit(solution)/shard_map/all_to_all | solution.py:326
  72.4 5.2 %shard_map.69 = bf16[256,8,4,128]{3,2,1,0:T(4,128)(2,1)} custom-call(bf16[64,33,4,128]{3,2,1,0:T(4,128)(2,1)} %all-to-all-done.table_ref, bf16[8,1024,128]{2,1,0:T(8,128)(2,1)} %get-tuple-element.14.rest_0_.near_ref, bf16[8,128,1024]{2,1,0:T(8,128)(2,1)} %get-tuple-element.15.rest_1_.turned_ref, f32[8,256,128]{2,1,0:T(8,128)} %get-tuple-element.16.rest_2_.start_ref), custom_call_target="tpu_custom_call" | custom-call | tf_op jit(solution)/shard_map/pallas_call | solution.py:111
  77.6 63.4 %all_to_all.16 = bf16[256,8,4,128]{3,2,1,0:T(4,128)(2,1)S(1)} all-to-all(bf16[256,8,4,128]{3,2,1,0:T(4,128)(2,1)} %shard_map.69), channel_id=1, replica_groups=mesh['samp'=4,'var_0'=4,'var_1'=8,'var_2'=2] {'samp','var_0','var_1','va..., dimensions={0} | all-to-all | bytes 4194304 | tf_op jit(solution)/shard_map/all_to_all | solution.py:333
  141.0 0.7 slice_bitcast_fusion
  142.9 0.9 copy-done
  143.8 2.3 %shard_map.71 = (bf16[4,2,128,128]{3,2,1,0:T(8,128)(2,1)S(1)}, f32[1,128]{1,0:T(1,128)S(1)}) custom-call(s32[10]{0:T(128)S(1)} %copy-done.3, bf16[4,1024,128]{2,1,0:T(8,128)(2,1)S(1)} %bitcast.31, bf16[8,1024,128]{2,1,0:T(8,128)(2,1)S(1)} %copy-done, bf16[8,128,1024]{2,1,0:T(8,128)(2,1)S(1)} %copy-done.1, f32[8,256,128]{2,1,0:T(8,128)S(1)} %copy-done.2, ...), custom_call_target="tpu_custom_call" | custom-call | flops 2147483648 | bytes 4194304 | tf_op jit(solution)/shard_map/pallas_call | solution.py:229
  146.1 0.8 collective-permute-start.5
  147.9 2.3 %shard_map.70 = (bf16[4,2,128,128]{3,2,1,0:T(8,128)(2,1)S(1)}, f32[1,128]{1,0:T(1,128)S(1)}) custom-call(s32[10]{0:T(128)S(1)} %copy-done.3, bf16[4,1024,128]{2,1,0:T(8,128)(2,1)S(1)} %bitcast.30, bf16[8,1024,128]{2,1,0:T(8,128)(2,1)S(1)} %copy-done, bf16[8,128,1024]{2,1,0:T(8,128)(2,1)S(1)} %copy-done.1, f32[8,256,128]{2,1,0:T(8,128)S(1)} %copy-done.2, ...), custom_call_target="tpu_custom_call" | custom-call | flops 2147483648 | bytes 4194304 | tf_op jit(solution)/shard_map/pallas_call | solution.py:229
  150.2 2.2 %collective-permute-start.8 = (bf16[4,2,128,128]{3,2,1,0:T(8,128)(2,1)S(1)}, bf16[4,2,128,128]{3,2,1,0:T(8,128)(2,1)S(1)}, u32[]{:S(2)}, u32[]{:S(2)}) collective-permute-start(bf16[4,2,128,128]{3,2,1,0:T(8,128)(2,1)S(1)} %get-tuple-element.17.h00), channel_id=1, source_target_pairs={{0,192},{64,0},{128,64},{192,128},{1,193},{65,1},{129,65},{193,129... | collective-permute-start | bytes 786440 | tf_op jit(solution)/shard_map/ppermute | solution.py:35
  152.4 0.7 broadcast_in_dim.25
  153.1 7.9 %all-to-all-start.2 = ((f32[256,1,128]{2,1,0:T(1,128)}), f32[256,1,128]{2,1,0:T(1,128)S(1)}, u32[]{:S(2)}, u32[]{:S(2)}) async-start(f32[256,1,128]{2,1,0:T(1,128)} %broadcast_in_dim.25), calls=%async_computation.2 | async-start | bytes 262144 | tf_op jit(solution)/shard_map/all_to_all | solution.py:350
  161.0 2.7 %collective-permute-start.6 = (bf16[4,2,128,128]{3,2,1,0:T(8,128)(2,1)S(1)}, bf16[4,2,128,128]{3,2,1,0:T(8,128)(2,1)S(1)}, u32[]{:S(2)}, u32[]{:S(2)}) collective-permute-start(bf16[4,2,128,128]{3,2,1,0:T(8,128)(2,1)S(1)} %collective-permute-done.5.h31), channel_id=1, source_target_pairs={{0,192},{64,0},{128,64},{192,128},{1,193},{65,1},{129,65},{193,129... | collective-permute-start | bytes 786440 | tf_op jit(solution)/shard_map/ppermute | solution.py:35
  163.8 3.2 %shard_map.72 = (f32[4,2,4,2,128,128]{5,4,3,2,1,0:T(8,128)}, f32[32,128]{1,0:T(8,128)S(1)}) custom-call(s32[1]{0:T(128)} %bitcast.samp_ref, s32[32]{0:T(128)S(1)} %compare_select_fusion.which_ref, bf16[4,2,128,128]{3,2,1,0:T(8,128)(2,1)S(1)} %get-tuple-element.17.h00, bf16[4,2,128,128]{3,2,1,0:T(8,128)(2,1)S(1)} %get-tuple-element.18.h01, ...), custom_call_target="tpu_custom_call" | custom-call | flops 1048576 | bytes 6291456 | tf_op jit(solution)/shard_map/pallas_call | solution.py:281
  166.9 7.0 %all-to-all-done.2 = f32[256,1,128]{2,1,0:T(1,128)S(1)} async-done(((f32[256,1,128]{2,1,0:T(1,128)}), f32[256,1,128]{2,1,0:T(1,128)S(1)}, u32[]{:S(2)}, u32[]{:S(2)}) %all-to-all-start.2) | async-done | bytes 131104 | tf_op jit(solution)/shard_map/all_to_all | solution.py:350
  174.5 2.1 %shard_map.73 = (f32[4,2,4,2,128,128]{5,4,3,2,1,0:T(8,128)}, f32[32,128]{1,0:T(8,128)}) custom-call(s32[1]{0:T(128)} %bitcast.samp_ref, s32[32]{0:T(128)S(1)} %compare_select_fusion.which_ref, bf16[4,2,128,128]{3,2,1,0:T(8,128)(2,1)S(1)} %collective-permute-done.4.h20, ...), custom_call_target="tpu_custom_call", output_to_operand_aliasing={{0}: (4, {})} | custom-call | flops 1048576 | bytes 2097152 | tf_op jit(solution)/shard_map/pallas_call | solution.py:293
  (37 shorter events, 3.8 us)
Async XLA Ops:
  6.6 13.3 %copy-start.5 = (bf16[256,4096]{1,0:T(8,128)(2,1)S(1)}, bf16[256,4096]{1,0:T(8,128)(2,1)}, u32[]{:S(2)}) copy-start(bf16[256,4096]{1,0:T(8,128)(2,1)} %own_ref.1) | copy-start | bytes 6291460
  6.6 65.8 %all-to-all-start = ((bf16[64,33,4,128]{3,2,1,0:T(4,128)(2,1)}), bf16[64,33,4,128]{3,2,1,0:T(4,128)(2,1)}, u32[]{:S(2)}, u32[]{:S(2)}) async-start(bf16[64,33,4,128]{3,2,1,0:T(4,128)(2,1)} %bitcast.35), calls=%async_computation | async-start | bytes 4325376 | tf_op jit(solution)/shard_map/all_to_all | solution.py:326
  19.9 4.8 %copy-start.9 = (s32[32,2]{0,1:T(2,128)S(1)}, s32[32,2]{0,1:T(2,128)}, u32[]{:S(2)}) copy-start(s32[32,2]{0,1:T(2,128)} %param.7) | copy-start | bytes 772
  20.9 24.9 %collective-permute-start.2 = (bf16[256,1024]{1,0:T(8,128)(2,1)}, bf16[256,1024]{1,0:T(8,128)(2,1)S(1)}, u32[]{:S(2)}, u32[]{:S(2)}) collective-permute-start(bf16[256,1024]{1,0:T(8,128)(2,1)} %get-tuple-element.27), channel_id=1, source_target_pairs={{0,192},{64,0},{128,64},{192,128},{1,193},{65,1},{129,65},{193,129... | collective-permute-start | bytes 1572872 | tf_op jit(solution)/shard_map/ppermute | solution.py:35
  23.7 22.2 %collective-permute-start.1 = (bf16[256,1024]{1,0:T(8,128)(2,1)S(1)}, bf16[256,1024]{1,0:T(8,128)(2,1)S(1)}, u32[]{:S(2)}, u32[]{:S(2)}) collective-permute-start(bf16[256,1024]{1,0:T(8,128)(2,1)S(1)} %get-tuple-element.28), channel_id=1, source_target_pairs={{0,128},{64,192},{128,0},{192,64},{1,129},{65,193},{129,1},{193,65... | collective-permute-start | bytes 1572872 | tf_op jit(solution)/shard_map/ppermute | solution.py:35
  24.0 26.3 %collective-permute-start = (bf16[256,1024]{1,0:T(8,128)(2,1)S(1)}, bf16[256,1024]{1,0:T(8,128)(2,1)S(1)}, u32[]{:S(2)}, u32[]{:S(2)}) collective-permute-start(bf16[256,1024]{1,0:T(8,128)(2,1)S(1)} %get-tuple-element.29), channel_id=1, source_target_pairs={{0,64},{64,128},{128,192},{192,0},{1,65},{65,129},{129,193},{193,1... | collective-permute-start | bytes 1572872 | tf_op jit(solution)/shard_map/ppermute | solution.py:35
  45.8 4.5 %copy-start.6 = (bf16[256,1024]{1,0:T(8,128)(2,1)}, bf16[256,1024]{1,0:T(8,128)(2,1)S(1)}, u32[]{:S(2)}) copy-start(bf16[256,1024]{1,0:T(8,128)(2,1)S(1)} %collective-permute-done.2.p3_ref) | copy-start | bytes 1572868
  45.9 4.5 %copy-start.7 = (bf16[256,1024]{1,0:T(8,128)(2,1)}, bf16[256,1024]{1,0:T(8,128)(2,1)S(1)}, u32[]{:S(2)}) copy-start(bf16[256,1024]{1,0:T(8,128)(2,1)S(1)} %collective-permute-done.1.p2_ref) | copy-start | bytes 1572868
  50.4 0.8 copy-start.8
  141.0 1.6 copy-start.1
  141.0 1.9 %copy-start.2 = (f32[8,256,128]{2,1,0:T(8,128)S(1)}, f32[8,256,128]{2,1,0:T(8,128)}, u32[]{:S(2)}) copy-start(f32[8,256,128]{2,1,0:T(8,128)} %get-tuple-element.16.rest_2_.start_ref) | copy-start | bytes 3145732
  141.0 1.9 %copy-start.4 = (f32[4096]{0:T(1024)S(1)}, f32[4096]{0:T(1024)}, u32[]{:S(2)}) copy-start(f32[4096]{0:T(1024)} %param.6) | copy-start | bytes 49156
  141.7 2.0 %copy-start = (bf16[8,1024,128]{2,1,0:T(8,128)(2,1)S(1)}, bf16[8,1024,128]{2,1,0:T(8,128)(2,1)}, u32[]{:S(2)}) copy-start(bf16[8,1024,128]{2,1,0:T(8,128)(2,1)} %get-tuple-element.14.rest_0_.near_ref) | copy-start | bytes 6291460
  141.8 2.0 %copy-start.3 = (s32[10]{0:T(128)S(1)}, s32[10]{0:T(128)}, u32[]{:S(2)}) copy-start(s32[10]{0:T(128)} %pad_add_fusion.info_ref) | copy-start | bytes 124
  146.1 6.3 %collective-permute-start.5 = (bf16[4,2,128,128]{3,2,1,0:T(8,128)(2,1)S(1)}, bf16[4,2,128,128]{3,2,1,0:T(8,128)(2,1)S(1)}, u32[]{:S(2)}, u32[]{:S(2)}) collective-permute-start(bf16[4,2,128,128]{3,2,1,0:T(8,128)(2,1)S(1)} %get-tuple-element.18.h01), channel_id=1, source_target_pairs={{0,192},{64,0},{128,64},{192,128},{1,193},{65,1},{129,65},{193,129... | collective-permute-start | bytes 786440 | tf_op jit(solution)/shard_map/ppermute | solution.py:35
  146.9 16.9 %collective-permute-start.7 = (bf16[4,2,128,128]{3,2,1,0:T(8,128)(2,1)S(1)}, bf16[4,2,128,128]{3,2,1,0:T(8,128)(2,1)S(1)}, u32[]{:S(2)}, u32[]{:S(2)}) collective-permute-start(bf16[4,2,128,128]{3,2,1,0:T(8,128)(2,1)S(1)} %get-tuple-element.18.h01), channel_id=1, source_target_pairs={{0,64},{64,128},{128,192},{192,0},{1,65},{65,129},{129,193},{193,1... | collective-permute-start | bytes 786440 | tf_op jit(solution)/shard_map/ppermute | solution.py:35
  150.2 13.6 %collective-permute-start.8 = (bf16[4,2,128,128]{3,2,1,0:T(8,128)(2,1)S(1)}, bf16[4,2,128,128]{3,2,1,0:T(8,128)(2,1)S(1)}, u32[]{:S(2)}, u32[]{:S(2)}) collective-permute-start(bf16[4,2,128,128]{3,2,1,0:T(8,128)(2,1)S(1)} %get-tuple-element.17.h00), channel_id=1, source_target_pairs={{0,192},{64,0},{128,64},{192,128},{1,193},{65,1},{129,65},{193,129... | collective-permute-start | bytes 786440 | tf_op jit(solution)/shard_map/ppermute | solution.py:35
  152.4 11.4 %collective-permute-start.3 = (bf16[4,2,128,128]{3,2,1,0:T(8,128)(2,1)S(1)}, bf16[4,2,128,128]{3,2,1,0:T(8,128)(2,1)S(1)}, u32[]{:S(2)}, u32[]{:S(2)}) collective-permute-start(bf16[4,2,128,128]{3,2,1,0:T(8,128)(2,1)S(1)} %get-tuple-element.17.h00), channel_id=1, source_target_pairs={{0,64},{64,128},{128,192},{192,0},{1,65},{65,129},{129,193},{193,1... | collective-permute-start | bytes 786440 | tf_op jit(solution)/shard_map/ppermute | solution.py:35
  153.1 20.8 %all-to-all-start.2 = ((f32[256,1,128]{2,1,0:T(1,128)}), f32[256,1,128]{2,1,0:T(1,128)S(1)}, u32[]{:S(2)}, u32[]{:S(2)}) async-start(f32[256,1,128]{2,1,0:T(1,128)} %broadcast_in_dim.25), calls=%async_computation.2 | async-start | bytes 262144 | tf_op jit(solution)/shard_map/all_to_all | solution.py:350
  161.0 13.4 %collective-permute-start.6 = (bf16[4,2,128,128]{3,2,1,0:T(8,128)(2,1)S(1)}, bf16[4,2,128,128]{3,2,1,0:T(8,128)(2,1)S(1)}, u32[]{:S(2)}, u32[]{:S(2)}) collective-permute-start(bf16[4,2,128,128]{3,2,1,0:T(8,128)(2,1)S(1)} %collective-permute-done.5.h31), channel_id=1, source_target_pairs={{0,192},{64,0},{128,64},{192,128},{1,193},{65,1},{129,65},{193,129... | collective-permute-start | bytes 786440 | tf_op jit(solution)/shard_map/ppermute | solution.py:35
  163.8 10.7 %collective-permute-start.4 = (bf16[4,2,128,128]{3,2,1,0:T(8,128)(2,1)S(1)}, bf16[4,2,128,128]{3,2,1,0:T(8,128)(2,1)S(1)}, u32[]{:S(2)}, u32[]{:S(2)}) collective-permute-start(bf16[4,2,128,128]{3,2,1,0:T(8,128)(2,1)S(1)} %collective-permute-done.3.h10), channel_id=1, source_target_pairs={{0,64},{64,128},{128,192},{192,0},{1,65},{65,129},{129,193},{193,1... | collective-permute-start | bytes 786440 | tf_op jit(solution)/shard_map/ppermute | solution.py:35

commit v5 on v4

--- a/solution.py
+++ b/solution.py
@@ -12,7 +12,6 @@
 STEP_LENGTH = 0.5
 PENALTY = 0.5
 DIGIT = 64
-HALVES = 2
 VAR = ("var_0", "var_1", "var_2")
 ALL = ("samp", "var_0", "var_1", "var_2")
 F32 = jnp.float32
@@ -35,12 +34,15 @@
     return lax.ppermute(x, axis, [(i, (i + k) % n) for i in range(n)])
 
 
-def cut_kernel(cols, at_ref, pattern_ref, data_ref, out_ref):
+def cut_kernel(cols, chunks, at_ref, pattern_ref, data_ref, out_ref, held, cutting, in_sems, out_sems):
     tiles, _, halves, rows, width = data_ref.shape
-    for t in range(tiles):
-        for b in range(cols):
-            for h in range(halves):
-                out_ref[t, h, b] = data_ref[t, b, h]
+    each = tiles // chunks
+    loads = [
+        pltpu.make_async_copy(data_ref.at[pl.ds(i * each, each)], held.at[pl.ds(i * each, each)], in_sems.at[i])
+        for i in range(chunks)
+    ]
+    for load in loads:
+        load.start()
     first, second = pattern_ref[0:1, :], pattern_ref[1:2, :]
     lane = lax.broadcasted_iota(jnp.int32, first.shape, 1)
     block = jnp.where(first == at_ref[0] * cols + lane, second, first)
@@ -50,24 +52,41 @@
     wide = jnp.concatenate([wide, jnp.zeros((rows, width - cols), F32)], axis=1).astype(out_ref.dtype)
     for t in range(tiles):
         for h in range(halves):
-            out_ref[t, h, cols] = wide
+            cutting[t, h, cols] = wide
+    stores = []
+    for i, load in enumerate(loads):
+        load.wait()
+
+        @pl.loop(i * each, (i + 1) * each)
+        def _(t):
+            for b in range(cols):
+                for h in range(halves):
+                    cutting[t, h, b] = held[t, b, h]
+
+        store = pltpu.make_async_copy(cutting.at[pl.ds(i * each, each)], out_ref.at[pl.ds(i * each, each)], out_sems.at[i])
+        store.start()
+        stores.append(store)
+    for store in stores:
+        store.wait()
 
 
 def cut(var_index, pattern, data, devices, cols, width):
     rows = data.shape[0] // devices
     tiles = devices // 2
     view = data.reshape(tiles, 2 * rows, cols, width).transpose(0, 2, 1, 3).reshape(tiles, cols, 2, rows, width)
-    block = 4
+    chunks = 4
+    shape = (tiles, 2, cols + 1, rows, width)
     out = pl.pallas_call(
-        functools.partial(cut_kernel, cols),
-        grid=(tiles // block,),
-        in_specs=[
-            pl.BlockSpec(memory_space=pltpu.SMEM),
-            pl.BlockSpec((2, cols), lambda i: (0, 0)),
-            pl.BlockSpec((block, cols, 2, rows, width), lambda i: (i, 0, 0, 0, 0)),
+        functools.partial(cut_kernel, cols, chunks),
+        in_specs=[pl.BlockSpec(memory_space=pltpu.SMEM), VMEM, HBM],
+        out_specs=HBM,
+        out_shape=jax.ShapeDtypeStruct(shape, data.dtype),
+        scratch_shapes=[
+            pltpu.VMEM(view.shape, data.dtype),
+            pltpu.VMEM(shape, data.dtype),
+            pltpu.SemaphoreType.DMA((chunks,)),
+            pltpu.SemaphoreType.DMA((chunks,)),
         ],
-        out_specs=pl.BlockSpec((block, 2, cols + 1, rows, width), lambda i: (i, 0, 0, 0, 0)),
-        out_shape=jax.ShapeDtypeStruct((tiles, 2, cols + 1, rows, width), data.dtype),
         compiler_params=params(56),
     )(var_index[None], pattern.T, view)
     return out.reshape(devices, cols + 1, rows, width)
@@ -181,20 +200,20 @@
     return hi, mid, (rest - mid.astype(F32)).astype(BF16)
 
 
-def steps_kernel(first, info_ref, far_ref, near_ref, turned_ref, start_ref, diag_ref, out_ref, obj_ref):
+def steps_kernel(info_ref, far_ref, near_ref, turned_ref, start_ref, diag_ref, out_ref, obj_ref):
     count, total_rows, width = far_ref.shape
     eye = lax.broadcasted_iota(jnp.int32, (width, width), 0) == lax.broadcasted_iota(jnp.int32, (width, width), 1)
     each = range(count)
     grams = []
     for c in each:
         far = far_ref[c]
-        both = jnp.concatenate([near_ref[first + c], far], axis=1)
-        top = jnp.dot(turned_ref[first + c], both, preferred_element_type=F32)
+        both = jnp.concatenate([near_ref[c], far], axis=1)
+        top = jnp.dot(turned_ref[c], both, preferred_element_type=F32)
         low = lax.dot_general(far, both, (((0,), (0,)), ((), ())), preferred_element_type=F32)
         grams.append(split3(jnp.concatenate([top, low], axis=0)))
-    db = [jnp.where(eye, 0.0, start_ref[first + c, :width]) for c in each]
-    ob = [start_ref[first + c, width:] for c in each]
-    dv = [diag_ref[pl.ds(info_ref[1] + first + c, 1), :] for c in each]
+    db = [jnp.where(eye, 0.0, start_ref[c, :width]) for c in each]
+    ob = [start_ref[c, width:] for c in each]
+    dv = [diag_ref[pl.ds(info_ref[1] + c, 1), :] for c in each]
     lane = lax.broadcasted_iota(jnp.int32, (1, width), 1)
     total = jnp.zeros((1, width), F32)
     for i in range(STEPS):
@@ -218,95 +237,93 @@
             dv[c] = 0.5 * (m + jnp.sqrt(m * m + 4.0 * STEP_LENGTH))
     obj_ref[...] = total
     for c in each:
-        where_diag = info_ref[2 + first + c]
+        where_diag = info_ref[2 + c]
         full = jnp.where(eye, jnp.broadcast_to(dv[c], (width, width)), db[c])
         out_ref[c, where_diag] = full.astype(out_ref.dtype)
         out_ref[c, 1 - where_diag] = ob[c].astype(out_ref.dtype)
 
 
-def iterate(first, info, far, near, turned, start, diag_rows):
+def iterate(info, far, near, turned, start, diag_rows):
     count, width = far.shape[0], far.shape[2]
     return pl.pallas_call(
-        functools.partial(steps_kernel, first),
+        steps_kernel,
         in_specs=[pl.BlockSpec(memory_space=pltpu.SMEM)] + [VMEM] * 5,
         out_specs=[VMEM] * 2,
         out_shape=[
             jax.ShapeDtypeStruct((count, 2, width, width), BF16),
             jax.ShapeDtypeStruct((1, width), F32),
         ],
-        compiler_params=params(16),
+        compiler_params=params(24),
         cost_estimate=cost(count << 29, 4 << 20),
     )(info, far, near, turned, start, diag_rows)
 
 
-def put(which_ref, out_ref, diag_ref, share, half, count, at, ref):
-    j = pl.program_id(0)
-    column = (share * HALVES + half) * count + j
+def put(which_ref, out_ref, diag_ref, at, column, ref):
     width = ref.shape[-1]
     eye = lax.broadcasted_iota(jnp.int32, (width, width), 0) == lax.broadcasted_iota(jnp.int32, (width, width), 1)
     where_diag = which_ref[column]
     full = ref[0, where_diag].astype(F32)
     diag_ref[pl.ds(column, 1), :] = jnp.sum(jnp.where(eye, full, 0.0), axis=0, keepdims=True)
-    out_ref[at, half, 0, where_diag] = jnp.where(eye, 0.0, full)
-    out_ref[at, half, 0, 1 - where_diag] = ref[0, 1 - where_diag].astype(F32)
-
-
-def first_places_kernel(count, samp_ref, which_ref, h00, h01, h10, h11, h30, h31, out_ref, diag_ref):
-    for k, refs in ((0, (h00, h01)), (1, (h10, h11)), (3, (h30, h31))):
+    out_ref[at, 0, where_diag] = jnp.where(eye, 0.0, full)
+    out_ref[at, 0, 1 - where_diag] = ref[0, 1 - where_diag].astype(F32)
+
+
+def first_places_kernel(samp_ref, which_ref, own_ref, one_ref, three_ref, out_ref, diag_ref):
+    for k, ref in ((0, own_ref), (1, one_ref), (3, three_ref)):
         q = lax.rem(samp_ref[0] + 4 - k, 4)
-        for h, ref in enumerate(refs):
-            put(which_ref, out_ref, diag_ref, q, h, count, q, ref)
-
-
-def last_places_kernel(count, samp_ref, which_ref, h20, h21, _, old_diag_ref, out_ref, diag_ref):
-    q = lax.rem(samp_ref[0] + 2, 4)
-
-    @pl.when(pl.program_id(0) == 0)
+        put(which_ref, out_ref, diag_ref, q, q * pl.num_programs(0) + pl.program_id(0), ref)
+
+
+def last_places_kernel(samp_ref, which_ref, low_ref, high_ref, _, old_diag_ref, out_ref, diag_ref):
+    j, half = pl.program_id(0), pl.num_programs(0)
+    column = lax.rem(samp_ref[0] + 2, 4) * 2 * half + j
+
+    @pl.when(j == 0)
     def _():
         diag_ref[...] = old_diag_ref[...]
 
-    for h, ref in enumerate((h20, h21)):
-        put(which_ref, out_ref, diag_ref, q, h, count, 0, ref)
+    for h, ref in enumerate((low_ref, high_ref)):
+        put(which_ref, out_ref.at[0], diag_ref, h, column + h * half, ref)
 
 
 def place_blocks(samp, which, own, one, three, two):
-    count, tail = own[0].shape[0], own[0].shape[1:]
+    count, tail = own.shape[0], own.shape[1:]
+    half = count // 2
     zeros = (0,) * len(tail)
     part = pl.BlockSpec((1,) + tail, lambda j, f, w: (j,) + zeros)
-    diag = pl.BlockSpec((4 * HALVES * count, tail[-1]), lambda j, f, w: (0, 0))
-    shapes = [
-        jax.ShapeDtypeStruct((4, HALVES, count) + tail, F32),
-        jax.ShapeDtypeStruct((4 * HALVES * count, tail[-1]), F32),
-    ]
+    diag = pl.BlockSpec((4 * count, tail[-1]), lambda j, f, w: (0, 0))
+    shape = (4, count) + tail
+    diag_shape = jax.ShapeDtypeStruct((4 * count, tail[-1]), F32)
     out, diagonal = pl.pallas_call(
-        functools.partial(first_places_kernel, count),
+        first_places_kernel,
         grid_spec=pltpu.PrefetchScalarGridSpec(
             num_scalar_prefetch=2,
             grid=(count,),
-            in_specs=[part] * 6,
-            out_specs=[pl.BlockSpec((4, HALVES, 1) + tail, lambda j, f, w: (0, 0, j) + zeros), diag],
+            in_specs=[part] * 3,
+            out_specs=[pl.BlockSpec((4, 1) + tail, lambda j, f, w: (0, j) + zeros), diag],
         ),
-        out_shape=shapes,
+        out_shape=[jax.ShapeDtypeStruct(shape, F32), diag_shape],
         compiler_params=params(24),
         cost_estimate=cost(1 << 20, 6 << 20),
-    )(samp[None], which, *own, *one, *three)
+    )(samp[None], which, own, one, three)
+    shape = (4, 2, half) + tail
     out, diagonal = pl.pallas_call(
-        functools.partial(last_places_kernel, count),
+        last_places_kernel,
         grid_spec=pltpu.PrefetchScalarGridSpec(
             num_scalar_prefetch=2,
-            grid=(count,),
+            grid=(half,),
             in_specs=[part, part, ANY, diag],
             out_specs=[
-                pl.BlockSpec((1, HALVES, 1) + tail, lambda j, f, w: (lax.rem(f[0] + 2, 4), 0, j) + zeros),
+                pl.BlockSpec((1, 2, 1) + tail, lambda j, f, w: (lax.rem(f[0] + 2, 4), 0, j) + zeros),
                 diag,
             ],
         ),
-        out_shape=shapes,
+        out_shape=[jax.ShapeDtypeStruct(shape, F32), diag_shape],
         input_output_aliases={4: 0},
         compiler_params=params(16),
         cost_estimate=cost(1 << 20, 2 << 20),
-    )(samp[None], which, *two, out, diagonal)
-    return out.reshape((4 * HALVES * count,) + tail), diagonal.reshape(-1)
+    )(samp[None], which, *two, out.reshape(shape), diagonal)
+    return out.reshape((4 * count,) + tail), diagonal.reshape(-1)
 
 
 def body(observed, blocks, diagonal, pattern):
@@ -315,7 +332,6 @@
     devices = lax.axis_size(VAR)
     shares = lax.axis_size("samp")
     each = cols // shares
-    half = each // HALVES
     total_rows = rows * shares
     samp = lax.axis_index("samp").astype(jnp.int32)
     var_index = lax.axis_index(VAR).astype(jnp.int32)
@@ -333,21 +349,15 @@
     far = lax.all_to_all(outgoing, ALL, split_axis=0, concat_axis=0, tiled=True)
 
     diag_rows = diagonal.reshape(cols, width)
-    new, objs = [], []
-    for h in range(HALVES):
-        far_h = far[:, h * half : (h + 1) * half].transpose(1, 0, 2, 3).reshape(half, total_rows, width)
-        done = iterate(h * half, info, far_h, near, turned, begin, diag_rows)
-        new.append(done[0])
-        objs.append(done[1])
-
-    one = [shift(x, "samp", 1) for x in new]
-    three = [shift(x, "samp", 3) for x in new]
-    two = [shift(one[0], "samp", 1), shift(three[1], "samp", 3)]
+    far = far.transpose(1, 0, 2, 3).reshape(each, total_rows, width)
+    new, obj = iterate(info, far, near, turned, begin, diag_rows)
+    one, three = shift(new, "samp", 1), shift(new, "samp", 3)
+    two = [shift(one[: each // 2], "samp", 1), shift(three[each // 2 :], "samp", 3)]
     new_blocks, new_diagonal = place_blocks(samp, which, new, one, three, two)
 
-    later = jnp.minimum(jnp.abs(three[1][0, 0, 0].astype(F32)), 0.0)
-    mine = jnp.broadcast_to(objs[0] + objs[1] + later, (shares * devices, width))
-    objective = jnp.sum(lax.all_to_all(mine, ALL, split_axis=0, concat_axis=0, tiled=True), axis=0)
+    obj = jnp.broadcast_to(obj, (devices, width))
+    obj = jnp.sum(lax.all_to_all(obj, VAR, split_axis=0, concat_axis=0, tiled=True), axis=0, keepdims=True)
+    objective = ((obj + shift(obj, "samp", 2)) + (shift(obj, "samp", 1) + shift(obj, "samp", 3)))[0]
     return (new_blocks, new_diagonal, objective[:STEPS] / (cols * devices * width))
 
 

time: 177 us -> 174 us (0.983)
  blocking collectives: 63.4 us -> 77 us
  starting transfers between devices: 31.3 us -> 23.4 us
  waiting for transfers between devices: 45.6 us -> 40.7 us
  Pallas kernels: 28.6 us -> 26.2 us
    all_to_all x0 -> x1, blocking collectives: none -> 13.6 us  [body(): lax.all_to_all(obj, VAR, split_axis=0, concat_axis=0, tiled=True)]
    all_to_all x1 -> x0, starting transfers between devices: 7.88 us -> none  [body(): lax.all_to_all(mine, ALL, split_axis=0, concat_axis=0, tiled=True)]
    all_to_all x1 -> x0, waiting for transfers between devices: 6.96 us -> none  [body(): lax.all_to_all(mine, ALL, split_axis=0, concat_axis=0, tiled=True)]
    pallas_call x5 -> x4, Pallas kernels: 15.9 us -> 13.4 us  [the longest x1 4.15 us: place_blocks(): pl.pallas_call(first_places_kernel, grid_spec=pltpu.PrefetchScalarGridSpe...]
    ppermute x9 -> x10, waiting for transfers between devices: 25 us -> 27.1 us  [shift(): return lax.ppermute(x, axis, [(i, (i + k) % n) for i in range(n)])]
    ppermute x9 -> x10, starting transfers between devices: 10.2 us -> 10.1 us  [shift(): return lax.ppermute(x, axis, [(i, (i + k) % n) for i in range(n)])]
  transfers between devices with their start and end apart: 11 -> 11, of which waited for: 4 -> 5; matrix products, arithmetic and copies ran while one was open for 2% -> 1% of each run, Pallas kernels for 7% -> 7%
where the time goes in v5:
time: 174 us; the launch traced here: 173 us
  blocking collectives  77 us (44%)
  waiting for transfers between devices  40.7 us (23%)
  Pallas kernels  26.2 us (15%)
  starting transfers between devices  23.4 us (13%)
  local copies, waits for them, and re-layouts  4.15 us (2%)
    all_to_all x1, blocking collectives, body(): far = lax.all_to_all(outgoing, ALL, split_axis=0, concat_axis=0, tiled=True)  63.4 us
    ppermute x10, waiting for transfers between devices, shift(): return lax.ppermute(x, axis, [(i, (i + k) % n) for i in range(n)])  27.1 us
    all_to_all x1, waiting for transfers between devices, body(): table = lax.all_to_all(pieces, VAR, split_axis=0, concat_axis=0, tiled=True)  13.7 us
    all_to_all x1, blocking collectives, body(): lax.all_to_all(obj, VAR, split_axis=0, concat_axis=0, tiled=True)  13.6 us
    all_to_all x1, starting transfers between devices, body(): table = lax.all_to_all(pieces, VAR, split_axis=0, concat_axis=0, tiled=True)  13.3 us
    ppermute x10, starting transfers between devices, shift(): return lax.ppermute(x, axis, [(i, (i + k) % n) for i in range(n)])  10.1 us
    pallas_call x1, Pallas kernels, near_panels(): pl.pallas_call(near_kernel, grid_spec=pltpu.PrefetchScalarGridSpec(num_sc...  7.55 us
    pallas_call x1, Pallas kernels, pick(): pl.pallas_call(functools.partial(pick_kernel, cols, shares), in_specs=[HB...  5.18 us
  transfers between devices with their start and end apart: 11, of which 5 were waited for; matrix products, arithmetic and copies ran while one was open for 1% of the time, Pallas kernels for 7%

profile of v5, /device:TPU:1, one launch (start us, length us, event | category | flops | bytes accessed | tf_op | source)
XLA Modules:
  0.0 173.4 jit_solution(7315858223328056697)
XLA Ops:
  0.6 3.4 %shard_map.67 = bf16[32,2,33,4,128]{4,3,2,1,0:T(4,128)(2,1)} custom-call(s32[1]{0:T(128)} %bitcast.3.at_ref, s32[2,32]{1,0:T(2,128)} %bitcast.36, bf16[32,32,2,4,128]{4,3,2,1,0:T(4,128)(2,1)} %bitcast.27), custom_call_target="tpu_custom_call" | custom-call | tf_op jit(solution)/shard_map/pallas_call | solution.py:79
  4.1 13.3 %all-to-all-start = ((bf16[64,33,4,128]{3,2,1,0:T(4,128)(2,1)}), bf16[64,33,4,128]{3,2,1,0:T(4,128)(2,1)}, u32[]{:S(2)}, u32[]{:S(2)}) async-start(bf16[64,33,4,128]{3,2,1,0:T(4,128)(2,1)} %bitcast.28), calls=%async_computation | async-start | bytes 4325376 | tf_op jit(solution)/shard_map/all_to_all | solution.py:342
  17.5 1.0 constant_dynamic-slice_fusion
  18.4 2.7 %collective-permute-start.2 = (bf16[256,1024]{1,0:T(8,128)(2,1)}, bf16[256,1024]{1,0:T(8,128)(2,1)S(1)}, u32[]{:S(2)}, u32[]{:S(2)}) collective-permute-start(bf16[256,1024]{1,0:T(8,128)(2,1)} %get-tuple-element.21), channel_id=1, source_target_pairs={{0,192},{64,0},{128,64},{192,128},{1,193},{65,1},{129,65},{193,129... | collective-permute-start | bytes 1572872 | tf_op jit(solution)/shard_map/ppermute | solution.py:34
  21.5 0.7 collective-permute-start
  22.9 20.5 %collective-permute-done.2.p3_ref = bf16[256,1024]{1,0:T(8,128)(2,1)S(1)} collective-permute-done((bf16[256,1024]{1,0:T(8,128)(2,1)}, bf16[256,1024]{1,0:T(8,128)(2,1)S(1)}, u32[]{:S(2)}, u32[]{:S(2)}) %collective-permute-start.2) | collective-permute-done | bytes 524320 | tf_op jit(solution)/shard_map/ppermute | solution.py:34
  43.3 4.5 %collective-permute-done.p1_ref = bf16[256,1024]{1,0:T(8,128)(2,1)S(1)} collective-permute-done((bf16[256,1024]{1,0:T(8,128)(2,1)S(1)}, bf16[256,1024]{1,0:T(8,128)(2,1)S(1)}, u32[]{:S(2)}, u32[]{:S(2)}) %collective-permute-start) | collective-permute-done | bytes 524320 | tf_op jit(solution)/shard_map/ppermute | solution.py:34
  47.9 0.8 copy-done.8
  48.7 7.6 %shard_map.68 = (bf16[8,1024,128]{2,1,0:T(8,128)(2,1)}, bf16[8,128,1024]{2,1,0:T(8,128)(2,1)}, f32[8,256,128]{2,1,0:T(8,128)}) custom-call(s32[10]{0:T(128)} %pad_add_fusion.info_ref, bf16[256,4096]{1,0:T(8,128)(2,1)} %own_ref.1, bf16[256,1024]{1,0:T(8,128)(2,1)} %copy-done.8, bf16[256,1024]{1,0:T(8,128)(2,1)} %copy-done.7, bf16[256,1024]{1,0:T(8,128)(2,1)} %copy-done.6, ...), custom_call_target="tpu_custom_call" | custom-call | flops 1048576 | bytes 10485760 | tf_op jit(solution)/shard_map/pallas_call | solution.py:164
  56.2 13.7 %all-to-all-done.table_ref = bf16[64,33,4,128]{3,2,1,0:T(4,128)(2,1)} async-done(((bf16[64,33,4,128]{3,2,1,0:T(4,128)(2,1)}), bf16[64,33,4,128]{3,2,1,0:T(4,128)(2,1)}, u32[]{:S(2)}, u32[]{:S(2)}) %all-to-all-start) | async-done | bytes 2162720 | tf_op jit(solution)/shard_map/all_to_all | solution.py:342
  69.9 5.2 %shard_map.69 = bf16[256,8,4,128]{3,2,1,0:T(4,128)(2,1)} custom-call(bf16[64,33,4,128]{3,2,1,0:T(4,128)(2,1)} %all-to-all-done.table_ref, bf16[8,1024,128]{2,1,0:T(8,128)(2,1)} %get-tuple-element.12.rest_0_.near_ref, bf16[8,128,1024]{2,1,0:T(8,128)(2,1)} %get-tuple-element.13.rest_1_.turned_ref, f32[8,256,128]{2,1,0:T(8,128)} %get-tuple-element.14.rest_2_.start_ref), custom_call_target="tpu_custom_call" | custom-call | tf_op jit(solution)/shard_map/pallas_call | solution.py:130
  75.1 63.4 %all_to_all.16 = bf16[256,8,4,128]{3,2,1,0:T(4,128)(2,1)S(1)} all-to-all(bf16[256,8,4,128]{3,2,1,0:T(4,128)(2,1)} %shard_map.69), channel_id=1, replica_groups=mesh['samp'=4,'var_0'=4,'var_1'=8,'var_2'=2] {'samp','var_0','var_1','va..., dimensions={0} | all-to-all | bytes 4194304 | tf_op jit(solution)/shard_map/all_to_all | solution.py:349
  138.5 0.7 copy.10
  139.3 0.8 copy-done
  140.1 0.6 copy-done.1
  140.8 3.7 %shard_map.70 = (bf16[8,2,128,128]{3,2,1,0:T(8,128)(2,1)S(1)}, f32[1,128]{1,0:T(1,128)S(1)}) custom-call(s32[10]{0:T(128)S(1)} %copy-done.3, bf16[8,1024,128]{2,1,0:T(8,128)(2,1)S(1)} %bitcast.24, bf16[8,1024,128]{2,1,0:T(8,128)(2,1)S(1)} %copy-done, bf16[8,128,1024]{2,1,0:T(8,128)(2,1)S(1)} %copy-done.1, f32[8,256,128]{2,1,0:T(8,128)S(1)} %copy-done.2, ...), custom_call_target="tpu_custom_call" | custom-call | flops 4294967296 | bytes 4194304 | tf_op jit(solution)/shard_map/pallas_call | solution.py:248
  144.5 0.8 collective-permute-start.5
  145.3 0.7 collective-permute-start.3
  146.0 13.6 %all_to_all.17 = f32[64,1,128]{2,1,0:T(1,128)S(1)} all-to-all(f32[64,1,128]{2,1,0:T(1,128)S(1)} %broadcast_in_dim.27), channel_id=1, replica_groups=mesh['samp'=4,'var_0'=4,'var_1'=8,'var_2'=2] {'var_0','var_1','var_2'}, dimensions={0} | all-to-all | bytes 65536 | tf_op jit(solution)/shard_map/all_to_all | solution.py:359
  159.9 2.3 %collective-permute-start.9 = (f32[1,128]{1,0:T(1,128)S(1)}, f32[1,128]{1,0:T(1,128)S(1)}, u32[]{:S(2)}, u32[]{:S(2)}) collective-permute-start(f32[1,128]{1,0:T(1,128)S(1)} %bitcast.34), channel_id=1, source_target_pairs={{0,192},{64,0},{128,64},{192,128},{1,193},{65,1},{129,65},{193,129... | collective-permute-start | bytes 1544 | tf_op jit(solution)/shard_map/ppermute | solution.py:34
  162.8 1.1 collective-permute-start.6
  164.5 1.7 collective-permute-done.7
  166.7 4.1 %shard_map.71 = (f32[4,8,2,128,128]{4,3,2,1,0:T(8,128)}, f32[32,128]{1,0:T(8,128)S(1)}) custom-call(s32[1]{0:T(128)} %bitcast.samp_ref, s32[32]{0:T(128)S(1)} %compare_select_fusion.which_ref, bf16[8,2,128,128]{3,2,1,0:T(8,128)(2,1)S(1)} %get-tuple-element.15.own_ref, bf16[8,2,128,128]{3,2,1,0:T(8,128)(2,1)S(1)} %collective-permute-done.3.one_ref, ...), custom_call_target="tpu_custom_call" | custom-call | flops 1048576 | bytes 6291456 | tf_op jit(solution)/shard_map/pallas_call | solution.py:297
  171.2 2.1 %shard_map.72 = (f32[4,2,4,2,128,128]{5,4,3,2,1,0:T(8,128)}, f32[32,128]{1,0:T(8,128)}) custom-call(s32[1]{0:T(128)} %bitcast.samp_ref, s32[32]{0:T(128)S(1)} %compare_select_fusion.which_ref, bf16[4,2,128,128]{3,2,1,0:T(8,128)(2,1)S(1)} %collective-permute-done.4.low_ref, ...), custom_call_target="tpu_custom_call", output_to_operand_aliasing={{0}: (4, {})} | custom-call | flops 1048576 | bytes 2097152 | tf_op jit(solution)/shard_map/pallas_call | solution.py:310
  (37 shorter events, 3.6 us)
Async XLA Ops:
  4.1 13.4 %copy-start.5 = (bf16[256,4096]{1,0:T(8,128)(2,1)S(1)}, bf16[256,4096]{1,0:T(8,128)(2,1)}, u32[]{:S(2)}) copy-start(bf16[256,4096]{1,0:T(8,128)(2,1)} %own_ref.1) | copy-start | bytes 6291460
  4.1 65.8 %all-to-all-start = ((bf16[64,33,4,128]{3,2,1,0:T(4,128)(2,1)}), bf16[64,33,4,128]{3,2,1,0:T(4,128)(2,1)}, u32[]{:S(2)}, u32[]{:S(2)}) async-start(bf16[64,33,4,128]{3,2,1,0:T(4,128)(2,1)} %bitcast.28), calls=%async_computation | async-start | bytes 4325376 | tf_op jit(solution)/shard_map/all_to_all | solution.py:342
  17.4 4.8 %copy-start.9 = (s32[32,2]{0,1:T(2,128)S(1)}, s32[32,2]{0,1:T(2,128)}, u32[]{:S(2)}) copy-start(s32[32,2]{0,1:T(2,128)} %param.7) | copy-start | bytes 772
  18.4 24.9 %collective-permute-start.2 = (bf16[256,1024]{1,0:T(8,128)(2,1)}, bf16[256,1024]{1,0:T(8,128)(2,1)S(1)}, u32[]{:S(2)}, u32[]{:S(2)}) collective-permute-start(bf16[256,1024]{1,0:T(8,128)(2,1)} %get-tuple-element.21), channel_id=1, source_target_pairs={{0,192},{64,0},{128,64},{192,128},{1,193},{65,1},{129,65},{193,129... | collective-permute-start | bytes 1572872 | tf_op jit(solution)/shard_map/ppermute | solution.py:34
  21.2 22.2 %collective-permute-start.1 = (bf16[256,1024]{1,0:T(8,128)(2,1)S(1)}, bf16[256,1024]{1,0:T(8,128)(2,1)S(1)}, u32[]{:S(2)}, u32[]{:S(2)}) collective-permute-start(bf16[256,1024]{1,0:T(8,128)(2,1)S(1)} %get-tuple-element.22), channel_id=1, source_target_pairs={{0,128},{64,192},{128,0},{192,64},{1,129},{65,193},{129,1},{193,65... | collective-permute-start | bytes 1572872 | tf_op jit(solution)/shard_map/ppermute | solution.py:34
  21.5 26.3 %collective-permute-start = (bf16[256,1024]{1,0:T(8,128)(2,1)S(1)}, bf16[256,1024]{1,0:T(8,128)(2,1)S(1)}, u32[]{:S(2)}, u32[]{:S(2)}) collective-permute-start(bf16[256,1024]{1,0:T(8,128)(2,1)S(1)} %get-tuple-element.23), channel_id=1, source_target_pairs={{0,64},{64,128},{128,192},{192,0},{1,65},{65,129},{129,193},{193,1... | collective-permute-start | bytes 1572872 | tf_op jit(solution)/shard_map/ppermute | solution.py:34
  43.3 4.5 %copy-start.6 = (bf16[256,1024]{1,0:T(8,128)(2,1)}, bf16[256,1024]{1,0:T(8,128)(2,1)S(1)}, u32[]{:S(2)}) copy-start(bf16[256,1024]{1,0:T(8,128)(2,1)S(1)} %collective-permute-done.2.p3_ref) | copy-start | bytes 1572868
  43.3 4.5 %copy-start.7 = (bf16[256,1024]{1,0:T(8,128)(2,1)}, bf16[256,1024]{1,0:T(8,128)(2,1)S(1)}, u32[]{:S(2)}) copy-start(bf16[256,1024]{1,0:T(8,128)(2,1)S(1)} %collective-permute-done.1.p2_ref) | copy-start | bytes 1572868
  47.9 0.8 copy-start.8
  75.1 64.2 %copy-start.2 = (f32[8,256,128]{2,1,0:T(8,128)S(1)}, f32[8,256,128]{2,1,0:T(8,128)}, u32[]{:S(2)}) copy-start(f32[8,256,128]{2,1,0:T(8,128)} %get-tuple-element.14.rest_2_.start_ref) | copy-start | bytes 3145732
  75.1 64.2 %copy-start.4 = (f32[4096]{0:T(1024)S(1)}, f32[4096]{0:T(1024)}, u32[]{:S(2)}) copy-start(f32[4096]{0:T(1024)} %param.6) | copy-start | bytes 49156
  138.5 1.6 copy-start
  138.5 2.2 %copy-start.1 = (bf16[8,128,1024]{2,1,0:T(8,128)(2,1)S(1)}, bf16[8,128,1024]{2,1,0:T(8,128)(2,1)}, u32[]{:S(2)}) copy-start(bf16[8,128,1024]{2,1,0:T(8,128)(2,1)} %get-tuple-element.13.rest_1_.turned_ref) | copy-start | bytes 6291460
  138.5 2.2 %copy-start.3 = (s32[10]{0:T(128)S(1)}, s32[10]{0:T(128)}, u32[]{:S(2)}) copy-start(s32[10]{0:T(128)} %pad_add_fusion.info_ref) | copy-start | bytes 124
  144.5 18.3 %collective-permute-start.5 = (bf16[8,2,128,128]{3,2,1,0:T(8,128)(2,1)S(1)}, bf16[8,2,128,128]{3,2,1,0:T(8,128)(2,1)S(1)}, u32[]{:S(2)}, u32[]{:S(2)}) collective-permute-start(bf16[8,2,128,128]{3,2,1,0:T(8,128)(2,1)S(1)} %get-tuple-element.15.own_ref), channel_id=1, source_target_pairs={{0,192},{64,0},{128,64},{192,128},{1,193},{65,1},{129,65},{193,129... | collective-permute-start | bytes 1572872 | tf_op jit(solution)/shard_map/ppermute | solution.py:34
  145.3 18.6 %collective-permute-start.3 = (bf16[8,2,128,128]{3,2,1,0:T(8,128)(2,1)S(1)}, bf16[8,2,128,128]{3,2,1,0:T(8,128)(2,1)S(1)}, u32[]{:S(2)}, u32[]{:S(2)}) collective-permute-start(bf16[8,2,128,128]{3,2,1,0:T(8,128)(2,1)S(1)} %get-tuple-element.15.own_ref), channel_id=1, source_target_pairs={{0,64},{64,128},{128,192},{192,0},{1,65},{65,129},{129,193},{193,1... | collective-permute-start | bytes 1572872 | tf_op jit(solution)/shard_map/ppermute | solution.py:34
  159.5 4.9 %collective-permute-start.8 = (f32[1,128]{1,0:T(1,128)S(1)}, f32[1,128]{1,0:T(1,128)S(1)}, u32[]{:S(2)}, u32[]{:S(2)}) collective-permute-start(f32[1,128]{1,0:T(1,128)S(1)} %bitcast.33), channel_id=1, source_target_pairs={{0,64},{64,128},{128,192},{192,0},{1,65},{65,129},{129,193},{193,1... | collective-permute-start | bytes 1544 | tf_op jit(solution)/shard_map/ppermute | solution.py:34
  159.9 4.5 %collective-permute-start.9 = (f32[1,128]{1,0:T(1,128)S(1)}, f32[1,128]{1,0:T(1,128)S(1)}, u32[]{:S(2)}, u32[]{:S(2)}) collective-permute-start(f32[1,128]{1,0:T(1,128)S(1)} %bitcast.34), channel_id=1, source_target_pairs={{0,192},{64,0},{128,64},{192,128},{1,193},{65,1},{129,65},{193,129... | collective-permute-start | bytes 1544 | tf_op jit(solution)/shard_map/ppermute | solution.py:34
  162.3 3.9 %collective-permute-start.7 = (f32[1,128]{1,0:T(1,128)S(1)}, f32[1,128]{1,0:T(1,128)S(1)}, u32[]{:S(2)}, u32[]{:S(2)}) collective-permute-start(f32[1,128]{1,0:T(1,128)S(1)} %bitcast.35), channel_id=1, source_target_pairs={{0,128},{64,192},{128,0},{192,64},{1,129},{65,193},{129,1},{193,65... | collective-permute-start | bytes 1544 | tf_op jit(solution)/shard_map/ppermute | solution.py:34
  162.8 8.0 %collective-permute-start.6 = (bf16[4,2,128,128]{3,2,1,0:T(8,128)(2,1)S(1)}, bf16[4,2,128,128]{3,2,1,0:T(8,128)(2,1)S(1)}, u32[]{:S(2)}, u32[]{:S(2)}) collective-permute-start(bf16[4,2,128,128]{3,2,1,0:T(8,128)(2,1)S(1)} %slice.18), channel_id=1, source_target_pairs={{0,192},{64,0},{128,64},{192,128},{1,193},{65,1},{129,65},{193,129... | collective-permute-start | bytes 786440 | tf_op jit(solution)/shard_map/ppermute | solution.py:34
  163.9 7.3 %collective-permute-start.4 = (bf16[4,2,128,128]{3,2,1,0:T(8,128)(2,1)S(1)}, bf16[4,2,128,128]{3,2,1,0:T(8,128)(2,1)S(1)}, u32[]{:S(2)}, u32[]{:S(2)}) collective-permute-start(bf16[4,2,128,128]{3,2,1,0:T(8,128)(2,1)S(1)} %slice.17), channel_id=1, source_target_pairs={{0,64},{64,128},{128,192},{192,0},{1,65},{65,129},{129,193},{193,1... | collective-permute-start | bytes 786440 | tf_op jit(solution)/shard_map/ppermute | solution.py:34

commit v6 on v5

--- a/solution.py
+++ b/solution.py
@@ -258,72 +258,90 @@
     )(info, far, near, turned, start, diag_rows)
 
 
-def put(which_ref, out_ref, diag_ref, at, column, ref):
-    width = ref.shape[-1]
+def put(which_ref, out_ref, diag_ref, at, column, block):
+    width = block.shape[-1]
     eye = lax.broadcasted_iota(jnp.int32, (width, width), 0) == lax.broadcasted_iota(jnp.int32, (width, width), 1)
     where_diag = which_ref[column]
-    full = ref[0, where_diag].astype(F32)
+    full = block[where_diag].astype(F32)
     diag_ref[pl.ds(column, 1), :] = jnp.sum(jnp.where(eye, full, 0.0), axis=0, keepdims=True)
-    out_ref[at, 0, where_diag] = jnp.where(eye, 0.0, full)
-    out_ref[at, 0, 1 - where_diag] = ref[0, 1 - where_diag].astype(F32)
+    out_ref[at + (where_diag,)] = jnp.where(eye, 0.0, full)
+    out_ref[at + (1 - where_diag,)] = block[1 - where_diag].astype(F32)
 
 
 def first_places_kernel(samp_ref, which_ref, own_ref, one_ref, three_ref, out_ref, diag_ref):
+    @pl.when(pl.program_id(0) == 0)
+    def _():
+        diag_ref[...] = jnp.zeros_like(diag_ref)
+
+    block = own_ref.shape[0]
     for k, ref in ((0, own_ref), (1, one_ref), (3, three_ref)):
         q = lax.rem(samp_ref[0] + 4 - k, 4)
-        put(which_ref, out_ref, diag_ref, q, q * pl.num_programs(0) + pl.program_id(0), ref)
+        for c in range(block):
+            put(which_ref, out_ref, diag_ref, (q, c), (q * pl.num_programs(0) + pl.program_id(0)) * block + c, ref.at[c])
 
 
 def last_places_kernel(samp_ref, which_ref, low_ref, high_ref, _, old_diag_ref, out_ref, diag_ref):
-    j, half = pl.program_id(0), pl.num_programs(0)
-    column = lax.rem(samp_ref[0] + 2, 4) * 2 * half + j
-
-    @pl.when(j == 0)
+    @pl.when(pl.program_id(0) == 0)
     def _():
         diag_ref[...] = old_diag_ref[...]
 
+    block = low_ref.shape[0]
+    half = pl.num_programs(0) * block
     for h, ref in enumerate((low_ref, high_ref)):
-        put(which_ref, out_ref.at[0], diag_ref, h, column + h * half, ref)
-
-
-def place_blocks(samp, which, own, one, three, two):
+        for c in range(block):
+            column = (lax.rem(samp_ref[0] + 2, 4) * 2 + h) * half + pl.program_id(0) * block + c
+            put(which_ref, out_ref, diag_ref, (0, h, c), column, ref.at[c])
+
+
+def place_first(samp, which, own, one, three):
     count, tail = own.shape[0], own.shape[1:]
-    half = count // 2
     zeros = (0,) * len(tail)
-    part = pl.BlockSpec((1,) + tail, lambda j, f, w: (j,) + zeros)
-    diag = pl.BlockSpec((4 * count, tail[-1]), lambda j, f, w: (0, 0))
-    shape = (4, count) + tail
-    diag_shape = jax.ShapeDtypeStruct((4 * count, tail[-1]), F32)
-    out, diagonal = pl.pallas_call(
+    block = 2
+    part = pl.BlockSpec((block,) + tail, lambda j, f, w: (j,) + zeros)
+    return pl.pallas_call(
         first_places_kernel,
         grid_spec=pltpu.PrefetchScalarGridSpec(
             num_scalar_prefetch=2,
-            grid=(count,),
+            grid=(count // block,),
             in_specs=[part] * 3,
-            out_specs=[pl.BlockSpec((4, 1) + tail, lambda j, f, w: (0, j) + zeros), diag],
+            out_specs=[
+                pl.BlockSpec((4, block) + tail, lambda j, f, w: (0, j) + zeros),
+                pl.BlockSpec((4 * count, tail[-1]), lambda j, f, w: (0, 0)),
+            ],
         ),
-        out_shape=[jax.ShapeDtypeStruct(shape, F32), diag_shape],
+        out_shape=[jax.ShapeDtypeStruct((4, count) + tail, F32), jax.ShapeDtypeStruct((4 * count, tail[-1]), F32)],
         compiler_params=params(24),
         cost_estimate=cost(1 << 20, 6 << 20),
     )(samp[None], which, own, one, three)
+
+
+def place_last(samp, which, low, high, out, diagonal):
+    half, tail = low.shape[0], low.shape[1:]
+    zeros = (0,) * len(tail)
+    block = 2
     shape = (4, 2, half) + tail
+    part = pl.BlockSpec((block,) + tail, lambda j, f, w: (j,) + zeros)
+    diag = pl.BlockSpec(diagonal.shape, lambda j, f, w: (0, 0))
     out, diagonal = pl.pallas_call(
         last_places_kernel,
         grid_spec=pltpu.PrefetchScalarGridSpec(
             num_scalar_prefetch=2,
-            grid=(half,),
+            grid=(half // block,),
             in_specs=[part, part, ANY, diag],
             out_specs=[
-                pl.BlockSpec((1, 2, 1) + tail, lambda j, f, w: (lax.rem(f[0] + 2, 4), 0, j) + zeros),
+                pl.BlockSpec((1, 2, block) + tail, lambda j, f, w: (lax.rem(f[0] + 2, 4), 0, j) + zeros),
                 diag,
             ],
         ),
-        out_shape=[jax.ShapeDtypeStruct(shape, F32), diag_shape],
+        out_shape=[
+            jax.ShapeDtypeStruct(shape, F32),
+            jax.ShapeDtypeStruct(diagonal.shape, F32),
+        ],
         input_output_aliases={4: 0},
         compiler_params=params(16),
         cost_estimate=cost(1 << 20, 2 << 20),
-    )(samp[None], which, *two, out.reshape(shape), diagonal)
-    return out.reshape((4 * count,) + tail), diagonal.reshape(-1)
+    )(samp[None], which, low, high, out.reshape(shape), diagonal)
+    return out.reshape((8 * half,) + tail), diagonal.reshape(-1)
 
 
 def body(observed, blocks, diagonal, pattern):
@@ -353,12 +371,11 @@
     new, obj = iterate(info, far, near, turned, begin, diag_rows)
     one, three = shift(new, "samp", 1), shift(new, "samp", 3)
     two = [shift(one[: each // 2], "samp", 1), shift(three[each // 2 :], "samp", 3)]
-    new_blocks, new_diagonal = place_blocks(samp, which, new, one, three, two)
-
-    obj = jnp.broadcast_to(obj, (devices, width))
-    obj = jnp.sum(lax.all_to_all(obj, VAR, split_axis=0, concat_axis=0, tiled=True), axis=0, keepdims=True)
-    objective = ((obj + shift(obj, "samp", 2)) + (shift(obj, "samp", 1) + shift(obj, "samp", 3)))[0]
-    return (new_blocks, new_diagonal, objective[:STEPS] / (cols * devices * width))
+    terms = jnp.broadcast_to(obj[None], (shares * devices, 1, width))
+    terms = jnp.sum(lax.all_to_all(terms, ALL, split_axis=0, concat_axis=0, tiled=True), axis=(0, 1))
+    placed, diag = place_first(samp, which, new, one, three)
+    new_blocks, new_diagonal = place_last(samp, which, *two, placed, diag)
+    return (new_blocks, new_diagonal, terms[:STEPS] / (cols * devices * width))
 
 
 def solution(mesh):

time: 174 us -> 172 us (0.989)
  blocking collectives: 77 us -> 63.4 us
  waiting for transfers between devices: 40.7 us -> 49.2 us
  starting transfers between devices: 23.4 us -> 27 us
    all_to_all x1 -> x0, blocking collectives: 13.6 us -> none  [body(): lax.all_to_all(obj, VAR, split_axis=0, concat_axis=0, tiled=True)]
    all_to_all x0 -> x1, waiting for transfers between devices: none -> 7.42 us  [body(): lax.all_to_all(terms, ALL, split_axis=0, concat_axis=0, tiled=True)]
    all_to_all x0 -> x1, starting transfers between devices: none -> 6.23 us  [body(): lax.all_to_all(terms, ALL, split_axis=0, concat_axis=0, tiled=True)]
    ppermute x10 -> x7, starting transfers between devices: 10.1 us -> 7.47 us  [shift(): return lax.ppermute(x, axis, [(i, (i + k) % n) for i in range(n)])]
    ppermute x10 -> x7, waiting for transfers between devices: 27.1 us -> 28.1 us  [shift(): return lax.ppermute(x, axis, [(i, (i + k) % n) for i in range(n)])]
  transfers between devices with their start and end apart: 11 -> 9, of which waited for: 5 -> 6; matrix products, arithmetic and copies ran while one was open for 1% -> 2% of each run, Pallas kernels for 7% -> 6%
where the time goes in v6:
time: 172 us; the launch traced here: 171 us
  blocking collectives  63.4 us (37%)
  waiting for transfers between devices  49.2 us (29%)
  starting transfers between devices  27 us (16%)
  Pallas kernels  24.6 us (14%)
  local copies, waits for them, and re-layouts  4.82 us (3%)
    all_to_all x1, blocking collectives, body(): far = lax.all_to_all(outgoing, ALL, split_axis=0, concat_axis=0, tiled=True)  63.4 us
    ppermute x7, waiting for transfers between devices, shift(): return lax.ppermute(x, axis, [(i, (i + k) % n) for i in range(n)])  28.1 us
    all_to_all x1, waiting for transfers between devices, body(): table = lax.all_to_all(pieces, VAR, split_axis=0, concat_axis=0, tiled=True)  13.7 us
    all_to_all x1, starting transfers between devices, body(): table = lax.all_to_all(pieces, VAR, split_axis=0, concat_axis=0, tiled=True)  13.3 us
    pallas_call x1, Pallas kernels, near_panels(): pl.pallas_call(near_kernel, grid_spec=pltpu.PrefetchScalarGridSpec(num_sc...  7.53 us
    ppermute x7, starting transfers between devices, shift(): return lax.ppermute(x, axis, [(i, (i + k) % n) for i in range(n)])  7.47 us
    all_to_all x1, waiting for transfers between devices, body(): lax.all_to_all(terms, ALL, split_axis=0, concat_axis=0, tiled=True)  7.42 us
    all_to_all x1, starting transfers between devices, body(): lax.all_to_all(terms, ALL, split_axis=0, concat_axis=0, tiled=True)  6.23 us
  transfers between devices with their start and end apart: 9, of which 6 were waited for; matrix products, arithmetic and copies ran while one was open for 2% of the time, Pallas kernels for 6%

profile of v6, /device:TPU:1, one launch (start us, length us, event | category | flops | bytes accessed | tf_op | source)
XLA Modules:
  0.0 171.0 jit_solution(9668655260682138757)
XLA Ops:
  0.6 3.4 %shard_map.67 = bf16[32,2,33,4,128]{4,3,2,1,0:T(4,128)(2,1)} custom-call(s32[1]{0:T(128)} %bitcast.3.at_ref, s32[2,32]{1,0:T(2,128)} %bitcast.29, bf16[32,32,2,4,128]{4,3,2,1,0:T(4,128)(2,1)} %bitcast.23), custom_call_target="tpu_custom_call" | custom-call | tf_op jit(solution)/shard_map/pallas_call | solution.py:79
  4.1 13.3 %all-to-all-start = ((bf16[64,33,4,128]{3,2,1,0:T(4,128)(2,1)}), bf16[64,33,4,128]{3,2,1,0:T(4,128)(2,1)}, u32[]{:S(2)}, u32[]{:S(2)}) async-start(bf16[64,33,4,128]{3,2,1,0:T(4,128)(2,1)} %bitcast.24), calls=%async_computation | async-start | bytes 4325376 | tf_op jit(solution)/shard_map/all_to_all | solution.py:360
  17.5 1.0 constant_dynamic-slice_fusion
  18.4 2.7 %collective-permute-start.2 = (bf16[256,1024]{1,0:T(8,128)(2,1)}, bf16[256,1024]{1,0:T(8,128)(2,1)S(1)}, u32[]{:S(2)}, u32[]{:S(2)}) collective-permute-start(bf16[256,1024]{1,0:T(8,128)(2,1)} %get-tuple-element.21), channel_id=1, source_target_pairs={{0,192},{64,0},{128,64},{192,128},{1,193},{65,1},{129,65},{193,129... | collective-permute-start | bytes 1572872 | tf_op jit(solution)/shard_map/ppermute | solution.py:34
  21.5 0.7 collective-permute-start
  22.9 20.5 %collective-permute-done.2.p3_ref = bf16[256,1024]{1,0:T(8,128)(2,1)S(1)} collective-permute-done((bf16[256,1024]{1,0:T(8,128)(2,1)}, bf16[256,1024]{1,0:T(8,128)(2,1)S(1)}, u32[]{:S(2)}, u32[]{:S(2)}) %collective-permute-start.2) | collective-permute-done | bytes 524320 | tf_op jit(solution)/shard_map/ppermute | solution.py:34
  43.3 4.5 %collective-permute-done.p1_ref = bf16[256,1024]{1,0:T(8,128)(2,1)S(1)} collective-permute-done((bf16[256,1024]{1,0:T(8,128)(2,1)S(1)}, bf16[256,1024]{1,0:T(8,128)(2,1)S(1)}, u32[]{:S(2)}, u32[]{:S(2)}) %collective-permute-start) | collective-permute-done | bytes 524320 | tf_op jit(solution)/shard_map/ppermute | solution.py:34
  47.8 0.8 copy-done.8
  48.6 7.5 %shard_map.68 = (bf16[8,1024,128]{2,1,0:T(8,128)(2,1)}, bf16[8,128,1024]{2,1,0:T(8,128)(2,1)}, f32[8,256,128]{2,1,0:T(8,128)}) custom-call(s32[10]{0:T(128)} %pad_add_fusion.info_ref, bf16[256,4096]{1,0:T(8,128)(2,1)} %own_ref.1, bf16[256,1024]{1,0:T(8,128)(2,1)} %copy-done.8, bf16[256,1024]{1,0:T(8,128)(2,1)} %copy-done.7, bf16[256,1024]{1,0:T(8,128)(2,1)} %copy-done.6, ...), custom_call_target="tpu_custom_call" | custom-call | flops 1048576 | bytes 10485760 | tf_op jit(solution)/shard_map/pallas_call | solution.py:164
  56.2 13.7 %all-to-all-done.table_ref = bf16[64,33,4,128]{3,2,1,0:T(4,128)(2,1)} async-done(((bf16[64,33,4,128]{3,2,1,0:T(4,128)(2,1)}), bf16[64,33,4,128]{3,2,1,0:T(4,128)(2,1)}, u32[]{:S(2)}, u32[]{:S(2)}) %all-to-all-start) | async-done | bytes 2162720 | tf_op jit(solution)/shard_map/all_to_all | solution.py:360
  69.9 5.2 %shard_map.69 = bf16[256,8,4,128]{3,2,1,0:T(4,128)(2,1)} custom-call(bf16[64,33,4,128]{3,2,1,0:T(4,128)(2,1)} %all-to-all-done.table_ref, bf16[8,1024,128]{2,1,0:T(8,128)(2,1)} %get-tuple-element.12.rest_0_.near_ref, bf16[8,128,1024]{2,1,0:T(8,128)(2,1)} %get-tuple-element.13.rest_1_.turned_ref, f32[8,256,128]{2,1,0:T(8,128)} %get-tuple-element.14.rest_2_.start_ref), custom_call_target="tpu_custom_call" | custom-call | tf_op jit(solution)/shard_map/pallas_call | solution.py:130
  75.1 63.4 %all_to_all.15 = bf16[256,8,4,128]{3,2,1,0:T(4,128)(2,1)S(1)} all-to-all(bf16[256,8,4,128]{3,2,1,0:T(4,128)(2,1)} %shard_map.69), channel_id=1, replica_groups=mesh['samp'=4,'var_0'=4,'var_1'=8,'var_2'=2] {'samp','var_0','var_1','va..., dimensions={0} | all-to-all | bytes 4194304 | tf_op jit(solution)/shard_map/all_to_all | solution.py:367
  138.5 0.7 copy.10
  139.3 0.8 copy-done
  140.8 3.7 %shard_map.70 = (bf16[8,2,128,128]{3,2,1,0:T(8,128)(2,1)S(1)}, f32[1,128]{1,0:T(1,128)S(1)}) custom-call(s32[10]{0:T(128)S(1)} %copy-done.3, bf16[8,1024,128]{2,1,0:T(8,128)(2,1)S(1)} %bitcast.20, bf16[8,1024,128]{2,1,0:T(8,128)(2,1)S(1)} %copy-done, bf16[8,128,1024]{2,1,0:T(8,128)(2,1)S(1)} %copy-done.1, f32[8,256,128]{2,1,0:T(8,128)S(1)} %copy-done.2, ...), custom_call_target="tpu_custom_call" | custom-call | flops 4294967296 | bytes 4194304 | tf_op jit(solution)/shard_map/pallas_call | solution.py:248
  144.5 0.8 collective-permute-start.5
  145.3 0.7 collective-permute-start.3
  145.9 0.7 broadcast_in_dim.28
  146.7 6.2 %all-to-all-start.2 = ((f32[256,1,128]{2,1,0:T(1,128)}), f32[256,1,128]{2,1,0:T(1,128)S(1)}, u32[]{:S(2)}, u32[]{:S(2)}) async-start(f32[256,1,128]{2,1,0:T(1,128)} %broadcast_in_dim.28), calls=%async_computation.2 | async-start | bytes 262144 | tf_op jit(solution)/shard_map/all_to_all | solution.py:375
  152.9 2.8 %collective-permute-done.5.three_ref = bf16[8,2,128,128]{3,2,1,0:T(8,128)(2,1)S(1)} collective-permute-done((bf16[8,2,128,128]{3,2,1,0:T(8,128)(2,1)S(1)}, bf16[8,2,128,128]{3,2,1,0:T(8,128)(2,1)S(1)}, u32[]{:S(2)}, u32[]{:S(2)}) %collective-permute-start.5) | collective-permute-done | bytes 524320 | tf_op jit(solution)/shard_map/ppermute | solution.py:34
  155.7 2.1 %collective-permute-start.6 = (bf16[4,2,128,128]{3,2,1,0:T(8,128)(2,1)S(1)}, bf16[4,2,128,128]{3,2,1,0:T(8,128)(2,1)S(1)}, u32[]{:S(2)}, u32[]{:S(2)}) collective-permute-start(bf16[4,2,128,128]{3,2,1,0:T(8,128)(2,1)S(1)} %slice.17), channel_id=1, source_target_pairs={{0,192},{64,0},{128,64},{192,128},{1,193},{65,1},{129,65},{193,129... | collective-permute-start | bytes 786440 | tf_op jit(solution)/shard_map/ppermute | solution.py:34
  158.3 7.4 %all-to-all-done.2 = f32[256,1,128]{2,1,0:T(1,128)S(1)} async-done(((f32[256,1,128]{2,1,0:T(1,128)}), f32[256,1,128]{2,1,0:T(1,128)S(1)}, u32[]{:S(2)}, u32[]{:S(2)}) %all-to-all-start.2) | async-done | bytes 131104 | tf_op jit(solution)/shard_map/all_to_all | solution.py:375
  166.3 3.1 %shard_map.71 = (f32[4,8,2,128,128]{4,3,2,1,0:T(8,128)}, f32[32,128]{1,0:T(8,128)S(1)}) custom-call(s32[1]{0:T(128)} %bitcast.samp_ref, s32[32]{0:T(128)S(1)} %compare_select_fusion.which_ref, bf16[8,2,128,128]{3,2,1,0:T(8,128)(2,1)S(1)} %get-tuple-element.15.own_ref, bf16[8,2,128,128]{3,2,1,0:T(8,128)(2,1)S(1)} %collective-permute-done.3.one_ref, ...), custom_call_target="tpu_custom_call" | custom-call | flops 1048576 | bytes 6291456 | tf_op jit(solution)/shard_map/pallas_call | solution.py:301
  169.4 1.6 shard_map.72
  (31 shorter events, 2.7 us)
Async XLA Ops:
  4.1 13.4 %copy-start.5 = (bf16[256,4096]{1,0:T(8,128)(2,1)S(1)}, bf16[256,4096]{1,0:T(8,128)(2,1)}, u32[]{:S(2)}) copy-start(bf16[256,4096]{1,0:T(8,128)(2,1)} %own_ref.1) | copy-start | bytes 6291460
  4.1 65.8 %all-to-all-start = ((bf16[64,33,4,128]{3,2,1,0:T(4,128)(2,1)}), bf16[64,33,4,128]{3,2,1,0:T(4,128)(2,1)}, u32[]{:S(2)}, u32[]{:S(2)}) async-start(bf16[64,33,4,128]{3,2,1,0:T(4,128)(2,1)} %bitcast.24), calls=%async_computation | async-start | bytes 4325376 | tf_op jit(solution)/shard_map/all_to_all | solution.py:360
  17.4 4.8 %copy-start.9 = (s32[32,2]{0,1:T(2,128)S(1)}, s32[32,2]{0,1:T(2,128)}, u32[]{:S(2)}) copy-start(s32[32,2]{0,1:T(2,128)} %param.7) | copy-start | bytes 772
  18.4 24.9 %collective-permute-start.2 = (bf16[256,1024]{1,0:T(8,128)(2,1)}, bf16[256,1024]{1,0:T(8,128)(2,1)S(1)}, u32[]{:S(2)}, u32[]{:S(2)}) collective-permute-start(bf16[256,1024]{1,0:T(8,128)(2,1)} %get-tuple-element.21), channel_id=1, source_target_pairs={{0,192},{64,0},{128,64},{192,128},{1,193},{65,1},{129,65},{193,129... | collective-permute-start | bytes 1572872 | tf_op jit(solution)/shard_map/ppermute | solution.py:34
  21.2 22.2 %collective-permute-start.1 = (bf16[256,1024]{1,0:T(8,128)(2,1)S(1)}, bf16[256,1024]{1,0:T(8,128)(2,1)S(1)}, u32[]{:S(2)}, u32[]{:S(2)}) collective-permute-start(bf16[256,1024]{1,0:T(8,128)(2,1)S(1)} %get-tuple-element.22), channel_id=1, source_target_pairs={{0,128},{64,192},{128,0},{192,64},{1,129},{65,193},{129,1},{193,65... | collective-permute-start | bytes 1572872 | tf_op jit(solution)/shard_map/ppermute | solution.py:34
  21.5 26.3 %collective-permute-start = (bf16[256,1024]{1,0:T(8,128)(2,1)S(1)}, bf16[256,1024]{1,0:T(8,128)(2,1)S(1)}, u32[]{:S(2)}, u32[]{:S(2)}) collective-permute-start(bf16[256,1024]{1,0:T(8,128)(2,1)S(1)} %get-tuple-element.23), channel_id=1, source_target_pairs={{0,64},{64,128},{128,192},{192,0},{1,65},{65,129},{129,193},{193,1... | collective-permute-start | bytes 1572872 | tf_op jit(solution)/shard_map/ppermute | solution.py:34
  43.3 4.5 %copy-start.6 = (bf16[256,1024]{1,0:T(8,128)(2,1)}, bf16[256,1024]{1,0:T(8,128)(2,1)S(1)}, u32[]{:S(2)}) copy-start(bf16[256,1024]{1,0:T(8,128)(2,1)S(1)} %collective-permute-done.2.p3_ref) | copy-start | bytes 1572868
  43.3 4.5 %copy-start.7 = (bf16[256,1024]{1,0:T(8,128)(2,1)}, bf16[256,1024]{1,0:T(8,128)(2,1)S(1)}, u32[]{:S(2)}) copy-start(bf16[256,1024]{1,0:T(8,128)(2,1)S(1)} %collective-permute-done.1.p2_ref) | copy-start | bytes 1572868
  47.8 0.8 copy-start.8
  75.1 64.2 %copy-start.2 = (f32[8,256,128]{2,1,0:T(8,128)S(1)}, f32[8,256,128]{2,1,0:T(8,128)}, u32[]{:S(2)}) copy-start(f32[8,256,128]{2,1,0:T(8,128)} %get-tuple-element.14.rest_2_.start_ref) | copy-start | bytes 3145732
  75.1 64.2 %copy-start.4 = (f32[4096]{0:T(1024)S(1)}, f32[4096]{0:T(1024)}, u32[]{:S(2)}) copy-start(f32[4096]{0:T(1024)} %param.6) | copy-start | bytes 49156
  138.5 1.6 copy-start
  138.5 2.2 %copy-start.1 = (bf16[8,128,1024]{2,1,0:T(8,128)(2,1)S(1)}, bf16[8,128,1024]{2,1,0:T(8,128)(2,1)}, u32[]{:S(2)}) copy-start(bf16[8,128,1024]{2,1,0:T(8,128)(2,1)} %get-tuple-element.13.rest_1_.turned_ref) | copy-start | bytes 6291460
  138.5 2.2 %copy-start.3 = (s32[10]{0:T(128)S(1)}, s32[10]{0:T(128)}, u32[]{:S(2)}) copy-start(s32[10]{0:T(128)} %pad_add_fusion.info_ref) | copy-start | bytes 124
  144.5 11.3 %collective-permute-start.5 = (bf16[8,2,128,128]{3,2,1,0:T(8,128)(2,1)S(1)}, bf16[8,2,128,128]{3,2,1,0:T(8,128)(2,1)S(1)}, u32[]{:S(2)}, u32[]{:S(2)}) collective-permute-start(bf16[8,2,128,128]{3,2,1,0:T(8,128)(2,1)S(1)} %get-tuple-element.15.own_ref), channel_id=1, source_target_pairs={{0,192},{64,0},{128,64},{192,128},{1,193},{65,1},{129,65},{193,129... | collective-permute-start | bytes 1572872 | tf_op jit(solution)/shard_map/ppermute | solution.py:34
  145.3 12.9 %collective-permute-start.3 = (bf16[8,2,128,128]{3,2,1,0:T(8,128)(2,1)S(1)}, bf16[8,2,128,128]{3,2,1,0:T(8,128)(2,1)S(1)}, u32[]{:S(2)}, u32[]{:S(2)}) collective-permute-start(bf16[8,2,128,128]{3,2,1,0:T(8,128)(2,1)S(1)} %get-tuple-element.15.own_ref), channel_id=1, source_target_pairs={{0,64},{64,128},{128,192},{192,0},{1,65},{65,129},{129,193},{193,1... | collective-permute-start | bytes 1572872 | tf_op jit(solution)/shard_map/ppermute | solution.py:34
  146.7 19.1 %all-to-all-start.2 = ((f32[256,1,128]{2,1,0:T(1,128)}), f32[256,1,128]{2,1,0:T(1,128)S(1)}, u32[]{:S(2)}, u32[]{:S(2)}) async-start(f32[256,1,128]{2,1,0:T(1,128)} %broadcast_in_dim.28), calls=%async_computation.2 | async-start | bytes 262144 | tf_op jit(solution)/shard_map/all_to_all | solution.py:375
  155.7 13.7 %collective-permute-start.6 = (bf16[4,2,128,128]{3,2,1,0:T(8,128)(2,1)S(1)}, bf16[4,2,128,128]{3,2,1,0:T(8,128)(2,1)S(1)}, u32[]{:S(2)}, u32[]{:S(2)}) collective-permute-start(bf16[4,2,128,128]{3,2,1,0:T(8,128)(2,1)S(1)} %slice.17), channel_id=1, source_target_pairs={{0,192},{64,0},{128,64},{192,128},{1,193},{65,1},{129,65},{193,129... | collective-permute-start | bytes 786440 | tf_op jit(solution)/shard_map/ppermute | solution.py:34
  158.2 11.2 %collective-permute-start.4 = (bf16[4,2,128,128]{3,2,1,0:T(8,128)(2,1)S(1)}, bf16[4,2,128,128]{3,2,1,0:T(8,128)(2,1)S(1)}, u32[]{:S(2)}, u32[]{:S(2)}) collective-permute-start(bf16[4,2,128,128]{3,2,1,0:T(8,128)(2,1)S(1)} %slice.16), channel_id=1, source_target_pairs={{0,64},{64,128},{128,192},{192,0},{1,65},{65,129},{129,193},{193,1... | collective-permute-start | bytes 786440 | tf_op jit(solution)/shard_map/ppermute | solution.py:34

commit v7 on v6

--- a/solution.py
+++ b/solution.py
@@ -372,8 +372,10 @@
     one, three = shift(new, "samp", 1), shift(new, "samp", 3)
     two = [shift(one[: each // 2], "samp", 1), shift(three[each // 2 :], "samp", 3)]
     terms = jnp.broadcast_to(obj[None], (shares * devices, 1, width))
-    terms = jnp.sum(lax.all_to_all(terms, ALL, split_axis=0, concat_axis=0, tiled=True), axis=(0, 1))
+    terms = lax.all_to_all(terms, ALL, split_axis=0, concat_axis=0, tiled=True)
     placed, diag = place_first(samp, which, new, one, three)
+    terms, diag = lax.optimization_barrier((terms, diag))
+    terms = jnp.sum(terms, axis=(0, 1))
     new_blocks, new_diagonal = place_last(samp, which, *two, placed, diag)
     return (new_blocks, new_diagonal, terms[:STEPS] / (cols * devices * width))
 

time: 172 us -> 171 us (level)
  waiting for transfers between devices: 49.2 us -> 46.5 us
    all_to_all x1, waiting for transfers between devices: 7.42 us -> 4.34 us  [body(): terms = lax.all_to_all(terms, ALL, split_axis=0, concat_axis=0, tiled=True)]
  transfers between devices with their start and end apart: 9 -> 9, of which waited for: 6 -> 7; matrix products, arithmetic and copies ran while one was open for 2% -> 2% of each run, Pallas kernels for 6% -> 6%
where the time goes in v7:
time: 171 us; the launch traced here: 169 us
  blocking collectives  63.4 us (37%)
  waiting for transfers between devices  46.5 us (27%)
  starting transfers between devices  27 us (16%)
  Pallas kernels  24.6 us (14%)
  local copies, waits for them, and re-layouts  4.82 us (3%)
    all_to_all x1, blocking collectives, body(): far = lax.all_to_all(outgoing, ALL, split_axis=0, concat_axis=0, tiled=True)  63.4 us
    ppermute x7, waiting for transfers between devices, shift(): return lax.ppermute(x, axis, [(i, (i + k) % n) for i in range(n)])  28.5 us
    all_to_all x1, waiting for transfers between devices, body(): table = lax.all_to_all(pieces, VAR, split_axis=0, concat_axis=0, tiled=True)  13.7 us
    all_to_all x1, starting transfers between devices, body(): table = lax.all_to_all(pieces, VAR, split_axis=0, concat_axis=0, tiled=True)  13.3 us
    pallas_call x1, Pallas kernels, near_panels(): pl.pallas_call(near_kernel, grid_spec=pltpu.PrefetchScalarGridSpec(num_sc...  7.53 us
    ppermute x7, starting transfers between devices, shift(): return lax.ppermute(x, axis, [(i, (i + k) % n) for i in range(n)])  7.47 us
    all_to_all x1, starting transfers between devices, body(): terms = lax.all_to_all(terms, ALL, split_axis=0, concat_axis=0, tiled=True)  6.23 us
    pallas_call x1, Pallas kernels, pick(): pl.pallas_call(functools.partial(pick_kernel, cols, shares), in_specs=[HB...  5.18 us
  transfers between devices with their start and end apart: 9, of which 7 were waited for; matrix products, arithmetic and copies ran while one was open for 2% of the time, Pallas kernels for 6%

profile of v7, /device:TPU:1, one launch (start us, length us, event | category | flops | bytes accessed | tf_op | source)
XLA Modules:
  0.0 168.6 jit_solution(11289231530455360999)
XLA Ops:
  0.6 3.4 %shard_map.67 = bf16[32,2,33,4,128]{4,3,2,1,0:T(4,128)(2,1)} custom-call(s32[1]{0:T(128)} %bitcast.3.at_ref, s32[2,32]{1,0:T(2,128)} %bitcast.27, bf16[32,32,2,4,128]{4,3,2,1,0:T(4,128)(2,1)} %bitcast.22), custom_call_target="tpu_custom_call" | custom-call | tf_op jit(solution)/shard_map/pallas_call | solution.py:79
  4.1 13.3 %all-to-all-start = ((bf16[64,33,4,128]{3,2,1,0:T(4,128)(2,1)}), bf16[64,33,4,128]{3,2,1,0:T(4,128)(2,1)}, u32[]{:S(2)}, u32[]{:S(2)}) async-start(bf16[64,33,4,128]{3,2,1,0:T(4,128)(2,1)} %bitcast.23), calls=%async_computation | async-start | bytes 4325376 | tf_op jit(solution)/shard_map/all_to_all | solution.py:360
  17.5 1.0 constant_dynamic-slice_fusion
  18.4 2.7 %collective-permute-start.2 = (bf16[256,1024]{1,0:T(8,128)(2,1)}, bf16[256,1024]{1,0:T(8,128)(2,1)S(1)}, u32[]{:S(2)}, u32[]{:S(2)}) collective-permute-start(bf16[256,1024]{1,0:T(8,128)(2,1)} %get-tuple-element.25), channel_id=1, source_target_pairs={{0,192},{64,0},{128,64},{192,128},{1,193},{65,1},{129,65},{193,129... | collective-permute-start | bytes 1572872 | tf_op jit(solution)/shard_map/ppermute | solution.py:34
  21.5 0.7 collective-permute-start
  22.9 20.5 %collective-permute-done.2.p3_ref = bf16[256,1024]{1,0:T(8,128)(2,1)S(1)} collective-permute-done((bf16[256,1024]{1,0:T(8,128)(2,1)}, bf16[256,1024]{1,0:T(8,128)(2,1)S(1)}, u32[]{:S(2)}, u32[]{:S(2)}) %collective-permute-start.2) | collective-permute-done | bytes 524320 | tf_op jit(solution)/shard_map/ppermute | solution.py:34
  43.3 4.5 %collective-permute-done.p1_ref = bf16[256,1024]{1,0:T(8,128)(2,1)S(1)} collective-permute-done((bf16[256,1024]{1,0:T(8,128)(2,1)S(1)}, bf16[256,1024]{1,0:T(8,128)(2,1)S(1)}, u32[]{:S(2)}, u32[]{:S(2)}) %collective-permute-start) | collective-permute-done | bytes 524320 | tf_op jit(solution)/shard_map/ppermute | solution.py:34
  47.8 0.8 copy-done.8
  48.6 7.5 %shard_map.68 = (bf16[8,1024,128]{2,1,0:T(8,128)(2,1)}, bf16[8,128,1024]{2,1,0:T(8,128)(2,1)}, f32[8,256,128]{2,1,0:T(8,128)}) custom-call(s32[10]{0:T(128)} %pad_add_fusion.info_ref, bf16[256,4096]{1,0:T(8,128)(2,1)} %own_ref.1, bf16[256,1024]{1,0:T(8,128)(2,1)} %copy-done.8, bf16[256,1024]{1,0:T(8,128)(2,1)} %copy-done.7, bf16[256,1024]{1,0:T(8,128)(2,1)} %copy-done.6, ...), custom_call_target="tpu_custom_call" | custom-call | flops 1048576 | bytes 10485760 | tf_op jit(solution)/shard_map/pallas_call | solution.py:164
  56.2 13.7 %all-to-all-done.table_ref = bf16[64,33,4,128]{3,2,1,0:T(4,128)(2,1)} async-done(((bf16[64,33,4,128]{3,2,1,0:T(4,128)(2,1)}), bf16[64,33,4,128]{3,2,1,0:T(4,128)(2,1)}, u32[]{:S(2)}, u32[]{:S(2)}) %all-to-all-start) | async-done | bytes 2162720 | tf_op jit(solution)/shard_map/all_to_all | solution.py:360
  69.9 5.2 %shard_map.69 = bf16[256,8,4,128]{3,2,1,0:T(4,128)(2,1)} custom-call(bf16[64,33,4,128]{3,2,1,0:T(4,128)(2,1)} %all-to-all-done.table_ref, bf16[8,1024,128]{2,1,0:T(8,128)(2,1)} %get-tuple-element.14.rest_0_.near_ref, bf16[8,128,1024]{2,1,0:T(8,128)(2,1)} %get-tuple-element.15.rest_1_.turned_ref, f32[8,256,128]{2,1,0:T(8,128)} %get-tuple-element.16.rest_2_.start_ref), custom_call_target="tpu_custom_call" | custom-call | tf_op jit(solution)/shard_map/pallas_call | solution.py:130
  75.1 63.4 %all_to_all.15 = bf16[256,8,4,128]{3,2,1,0:T(4,128)(2,1)S(1)} all-to-all(bf16[256,8,4,128]{3,2,1,0:T(4,128)(2,1)} %shard_map.69), channel_id=1, replica_groups=mesh['samp'=4,'var_0'=4,'var_1'=8,'var_2'=2] {'samp','var_0','var_1','va..., dimensions={0} | all-to-all | bytes 4194304 | tf_op jit(solution)/shard_map/all_to_all | solution.py:367
  138.5 0.7 copy.8
  139.3 0.8 copy-done
  140.8 3.7 %shard_map.70 = (bf16[8,2,128,128]{3,2,1,0:T(8,128)(2,1)S(1)}, f32[1,128]{1,0:T(1,128)S(1)}) custom-call(s32[10]{0:T(128)S(1)} %copy-done.3, bf16[8,1024,128]{2,1,0:T(8,128)(2,1)S(1)} %bitcast.19, bf16[8,1024,128]{2,1,0:T(8,128)(2,1)S(1)} %copy-done, bf16[8,128,1024]{2,1,0:T(8,128)(2,1)S(1)} %copy-done.1, f32[8,256,128]{2,1,0:T(8,128)S(1)} %copy-done.2, ...), custom_call_target="tpu_custom_call" | custom-call | flops 4294967296 | bytes 4194304 | tf_op jit(solution)/shard_map/pallas_call | solution.py:248
  144.5 0.8 collective-permute-start.5
  145.3 0.7 collective-permute-start.3
  145.9 0.7 broadcast_in_dim.28
  146.6 6.2 %all-to-all-start.2 = ((f32[256,1,128]{2,1,0:T(1,128)}), f32[256,1,128]{2,1,0:T(1,128)S(1)}, u32[]{:S(2)}, u32[]{:S(2)}) async-start(f32[256,1,128]{2,1,0:T(1,128)} %broadcast_in_dim.28), calls=%async_computation.2 | async-start | bytes 262144 | tf_op jit(solution)/shard_map/all_to_all | solution.py:375
  152.9 2.8 %collective-permute-done.5.three_ref = bf16[8,2,128,128]{3,2,1,0:T(8,128)(2,1)S(1)} collective-permute-done((bf16[8,2,128,128]{3,2,1,0:T(8,128)(2,1)S(1)}, bf16[8,2,128,128]{3,2,1,0:T(8,128)(2,1)S(1)}, u32[]{:S(2)}, u32[]{:S(2)}) %collective-permute-start.5) | collective-permute-done | bytes 524320 | tf_op jit(solution)/shard_map/ppermute | solution.py:34
  155.7 2.1 %collective-permute-start.6 = (bf16[4,2,128,128]{3,2,1,0:T(8,128)(2,1)S(1)}, bf16[4,2,128,128]{3,2,1,0:T(8,128)(2,1)S(1)}, u32[]{:S(2)}, u32[]{:S(2)}) collective-permute-start(bf16[4,2,128,128]{3,2,1,0:T(8,128)(2,1)S(1)} %slice.17), channel_id=1, source_target_pairs={{0,192},{64,0},{128,64},{192,128},{1,193},{65,1},{129,65},{193,129... | collective-permute-start | bytes 786440 | tf_op jit(solution)/shard_map/ppermute | solution.py:34
  158.3 3.1 %shard_map.71 = (f32[4,8,2,128,128]{4,3,2,1,0:T(8,128)}, f32[32,128]{1,0:T(8,128)S(1)}) custom-call(s32[1]{0:T(128)} %bitcast.samp_ref, s32[32]{0:T(128)S(1)} %compare_select_fusion.which_ref, bf16[8,2,128,128]{3,2,1,0:T(8,128)(2,1)S(1)} %get-tuple-element.17.own_ref, bf16[8,2,128,128]{3,2,1,0:T(8,128)(2,1)S(1)} %collective-permute-done.3.one_ref, ...), custom_call_target="tpu_custom_call" | custom-call | flops 1048576 | bytes 6291456 | tf_op jit(solution)/shard_map/pallas_call | solution.py:301
  161.4 4.3 %all-to-all-done.2 = f32[256,1,128]{2,1,0:T(1,128)S(1)} async-done(((f32[256,1,128]{2,1,0:T(1,128)}), f32[256,1,128]{2,1,0:T(1,128)S(1)}, u32[]{:S(2)}, u32[]{:S(2)}) %all-to-all-start.2) | async-done | bytes 131104 | tf_op jit(solution)/shard_map/all_to_all | solution.py:375
  166.9 1.6 shard_map.72
  (31 shorter events, 3.3 us)
Async XLA Ops:
  4.1 13.4 %copy-start.5 = (bf16[256,4096]{1,0:T(8,128)(2,1)S(1)}, bf16[256,4096]{1,0:T(8,128)(2,1)}, u32[]{:S(2)}) copy-start(bf16[256,4096]{1,0:T(8,128)(2,1)} %own_ref.1) | copy-start | bytes 6291460
  4.1 65.8 %all-to-all-start = ((bf16[64,33,4,128]{3,2,1,0:T(4,128)(2,1)}), bf16[64,33,4,128]{3,2,1,0:T(4,128)(2,1)}, u32[]{:S(2)}, u32[]{:S(2)}) async-start(bf16[64,33,4,128]{3,2,1,0:T(4,128)(2,1)} %bitcast.23), calls=%async_computation | async-start | bytes 4325376 | tf_op jit(solution)/shard_map/all_to_all | solution.py:360
  17.4 4.8 %copy-start.9 = (s32[32,2]{0,1:T(2,128)S(1)}, s32[32,2]{0,1:T(2,128)}, u32[]{:S(2)}) copy-start(s32[32,2]{0,1:T(2,128)} %param.7) | copy-start | bytes 772
  18.4 24.9 %collective-permute-start.2 = (bf16[256,1024]{1,0:T(8,128)(2,1)}, bf16[256,1024]{1,0:T(8,128)(2,1)S(1)}, u32[]{:S(2)}, u32[]{:S(2)}) collective-permute-start(bf16[256,1024]{1,0:T(8,128)(2,1)} %get-tuple-element.25), channel_id=1, source_target_pairs={{0,192},{64,0},{128,64},{192,128},{1,193},{65,1},{129,65},{193,129... | collective-permute-start | bytes 1572872 | tf_op jit(solution)/shard_map/ppermute | solution.py:34
  21.2 22.2 %collective-permute-start.1 = (bf16[256,1024]{1,0:T(8,128)(2,1)S(1)}, bf16[256,1024]{1,0:T(8,128)(2,1)S(1)}, u32[]{:S(2)}, u32[]{:S(2)}) collective-permute-start(bf16[256,1024]{1,0:T(8,128)(2,1)S(1)} %get-tuple-element.26), channel_id=1, source_target_pairs={{0,128},{64,192},{128,0},{192,64},{1,129},{65,193},{129,1},{193,65... | collective-permute-start | bytes 1572872 | tf_op jit(solution)/shard_map/ppermute | solution.py:34
  21.5 26.3 %collective-permute-start = (bf16[256,1024]{1,0:T(8,128)(2,1)S(1)}, bf16[256,1024]{1,0:T(8,128)(2,1)S(1)}, u32[]{:S(2)}, u32[]{:S(2)}) collective-permute-start(bf16[256,1024]{1,0:T(8,128)(2,1)S(1)} %get-tuple-element.27), channel_id=1, source_target_pairs={{0,64},{64,128},{128,192},{192,0},{1,65},{65,129},{129,193},{193,1... | collective-permute-start | bytes 1572872 | tf_op jit(solution)/shard_map/ppermute | solution.py:34
  43.3 4.5 %copy-start.6 = (bf16[256,1024]{1,0:T(8,128)(2,1)}, bf16[256,1024]{1,0:T(8,128)(2,1)S(1)}, u32[]{:S(2)}) copy-start(bf16[256,1024]{1,0:T(8,128)(2,1)S(1)} %collective-permute-done.2.p3_ref) | copy-start | bytes 1572868
  43.3 4.5 %copy-start.7 = (bf16[256,1024]{1,0:T(8,128)(2,1)}, bf16[256,1024]{1,0:T(8,128)(2,1)S(1)}, u32[]{:S(2)}) copy-start(bf16[256,1024]{1,0:T(8,128)(2,1)S(1)} %collective-permute-done.1.p2_ref) | copy-start | bytes 1572868
  47.8 0.8 copy-start.8
  75.1 64.2 %copy-start.2 = (f32[8,256,128]{2,1,0:T(8,128)S(1)}, f32[8,256,128]{2,1,0:T(8,128)}, u32[]{:S(2)}) copy-start(f32[8,256,128]{2,1,0:T(8,128)} %get-tuple-element.16.rest_2_.start_ref) | copy-start | bytes 3145732
  75.1 64.2 %copy-start.4 = (f32[4096]{0:T(1024)S(1)}, f32[4096]{0:T(1024)}, u32[]{:S(2)}) copy-start(f32[4096]{0:T(1024)} %param.6) | copy-start | bytes 49156
  138.5 1.6 copy-start
  138.5 2.2 %copy-start.1 = (bf16[8,128,1024]{2,1,0:T(8,128)(2,1)S(1)}, bf16[8,128,1024]{2,1,0:T(8,128)(2,1)}, u32[]{:S(2)}) copy-start(bf16[8,128,1024]{2,1,0:T(8,128)(2,1)} %get-tuple-element.15.rest_1_.turned_ref) | copy-start | bytes 6291460
  138.5 2.2 %copy-start.3 = (s32[10]{0:T(128)S(1)}, s32[10]{0:T(128)}, u32[]{:S(2)}) copy-start(s32[10]{0:T(128)} %pad_add_fusion.info_ref) | copy-start | bytes 124
  144.5 11.3 %collective-permute-start.5 = (bf16[8,2,128,128]{3,2,1,0:T(8,128)(2,1)S(1)}, bf16[8,2,128,128]{3,2,1,0:T(8,128)(2,1)S(1)}, u32[]{:S(2)}, u32[]{:S(2)}) collective-permute-start(bf16[8,2,128,128]{3,2,1,0:T(8,128)(2,1)S(1)} %get-tuple-element.17.own_ref), channel_id=1, source_target_pairs={{0,192},{64,0},{128,64},{192,128},{1,193},{65,1},{129,65},{193,129... | collective-permute-start | bytes 1572872 | tf_op jit(solution)/shard_map/ppermute | solution.py:34
  145.3 12.9 %collective-permute-start.3 = (bf16[8,2,128,128]{3,2,1,0:T(8,128)(2,1)S(1)}, bf16[8,2,128,128]{3,2,1,0:T(8,128)(2,1)S(1)}, u32[]{:S(2)}, u32[]{:S(2)}) collective-permute-start(bf16[8,2,128,128]{3,2,1,0:T(8,128)(2,1)S(1)} %get-tuple-element.17.own_ref), channel_id=1, source_target_pairs={{0,64},{64,128},{128,192},{192,0},{1,65},{65,129},{129,193},{193,1... | collective-permute-start | bytes 1572872 | tf_op jit(solution)/shard_map/ppermute | solution.py:34
  146.6 19.1 %all-to-all-start.2 = ((f32[256,1,128]{2,1,0:T(1,128)}), f32[256,1,128]{2,1,0:T(1,128)S(1)}, u32[]{:S(2)}, u32[]{:S(2)}) async-start(f32[256,1,128]{2,1,0:T(1,128)} %broadcast_in_dim.28), calls=%async_computation.2 | async-start | bytes 262144 | tf_op jit(solution)/shard_map/all_to_all | solution.py:375
  155.7 10.8 %collective-permute-start.6 = (bf16[4,2,128,128]{3,2,1,0:T(8,128)(2,1)S(1)}, bf16[4,2,128,128]{3,2,1,0:T(8,128)(2,1)S(1)}, u32[]{:S(2)}, u32[]{:S(2)}) collective-permute-start(bf16[4,2,128,128]{3,2,1,0:T(8,128)(2,1)S(1)} %slice.17), channel_id=1, source_target_pairs={{0,192},{64,0},{128,64},{192,128},{1,193},{65,1},{129,65},{193,129... | collective-permute-start | bytes 786440 | tf_op jit(solution)/shard_map/ppermute | solution.py:34
  158.2 8.8 %collective-permute-start.4 = (bf16[4,2,128,128]{3,2,1,0:T(8,128)(2,1)S(1)}, bf16[4,2,128,128]{3,2,1,0:T(8,128)(2,1)S(1)}, u32[]{:S(2)}, u32[]{:S(2)}) collective-permute-start(bf16[4,2,128,128]{3,2,1,0:T(8,128)(2,1)S(1)} %slice.16), channel_id=1, source_target_pairs={{0,64},{64,128},{128,192},{192,0},{1,65},{65,129},{129,193},{193,1... | collective-permute-start | bytes 786440 | tf_op jit(solution)/shard_map/ppermute | solution.py:34

commit v8 on v7

--- a/solution.py
+++ b/solution.py
@@ -74,7 +74,7 @@
     rows = data.shape[0] // devices
     tiles = devices // 2
     view = data.reshape(tiles, 2 * rows, cols, width).transpose(0, 2, 1, 3).reshape(tiles, cols, 2, rows, width)
-    chunks = 4
+    chunks = 8
     shape = (tiles, 2, cols + 1, rows, width)
     out = pl.pallas_call(
         functools.partial(cut_kernel, cols, chunks),
@@ -200,7 +200,7 @@
     return hi, mid, (rest - mid.astype(F32)).astype(BF16)
 
 
-def steps_kernel(info_ref, far_ref, near_ref, turned_ref, start_ref, diag_ref, out_ref, obj_ref):
+def steps_kernel(info_ref, far_ref, near_ref, turned_ref, start_ref, diag_ref, out0_ref, out1_ref, obj_ref):
     count, total_rows, width = far_ref.shape
     eye = lax.broadcasted_iota(jnp.int32, (width, width), 0) == lax.broadcasted_iota(jnp.int32, (width, width), 1)
     each = range(count)
@@ -239,8 +239,10 @@
     for c in each:
         where_diag = info_ref[2 + c]
         full = jnp.where(eye, jnp.broadcast_to(dv[c], (width, width)), db[c])
-        out_ref[c, where_diag] = full.astype(out_ref.dtype)
-        out_ref[c, 1 - where_diag] = ob[c].astype(out_ref.dtype)
+        half = count // 2
+        out_ref = out0_ref if c < half else out1_ref
+        out_ref[c % half, where_diag] = full.astype(out_ref.dtype)
+        out_ref[c % half, 1 - where_diag] = ob[c].astype(out_ref.dtype)
 
 
 def iterate(info, far, near, turned, start, diag_rows):
@@ -248,9 +250,10 @@
     return pl.pallas_call(
         steps_kernel,
         in_specs=[pl.BlockSpec(memory_space=pltpu.SMEM)] + [VMEM] * 5,
-        out_specs=[VMEM] * 2,
+        out_specs=[VMEM] * 3,
         out_shape=[
-            jax.ShapeDtypeStruct((count, 2, width, width), BF16),
+            jax.ShapeDtypeStruct((count // 2, 2, width, width), BF16),
+            jax.ShapeDtypeStruct((count // 2, 2, width, width), BF16),
             jax.ShapeDtypeStruct((1, width), F32),
         ],
         compiler_params=params(24),
@@ -268,22 +271,28 @@
     out_ref[at + (1 - where_diag,)] = block[1 - where_diag].astype(F32)
 
 
-def first_places_kernel(samp_ref, which_ref, own_ref, one_ref, three_ref, out_ref, diag_ref):
+def first_places_kernel(samp_ref, which_ref, own0, own1, one0, one1, three0, three1, out_ref, diag_ref):
     @pl.when(pl.program_id(0) == 0)
     def _():
         diag_ref[...] = jnp.zeros_like(diag_ref)
 
-    block = own_ref.shape[0]
-    for k, ref in ((0, own_ref), (1, one_ref), (3, three_ref)):
+    block = own0.shape[0]
+    half = pl.num_programs(0) * block
+    for k, refs in ((0, (own0, own1)), (1, (one0, one1)), (3, (three0, three1))):
         q = lax.rem(samp_ref[0] + 4 - k, 4)
-        for c in range(block):
-            put(which_ref, out_ref, diag_ref, (q, c), (q * pl.num_programs(0) + pl.program_id(0)) * block + c, ref.at[c])
-
-
-def last_places_kernel(samp_ref, which_ref, low_ref, high_ref, _, old_diag_ref, out_ref, diag_ref):
+        for h, ref in enumerate(refs):
+            for c in range(block):
+                put(which_ref, out_ref, diag_ref, (q, h, c), (q * 2 + h) * half + pl.program_id(0) * block + c, ref.at[c])
+
+
+def last_places_kernel(scale, samp_ref, which_ref, low_ref, high_ref, _, old_diag_ref, terms_ref, out_ref, diag_ref, objective_ref):
     @pl.when(pl.program_id(0) == 0)
     def _():
         diag_ref[...] = old_diag_ref[...]
+        total = jnp.sum(terms_ref[...], axis=0)
+        lane = lax.broadcasted_iota(jnp.int32, total.shape, 1)
+        for i in range(STEPS):
+            objective_ref[i] = jnp.sum(jnp.where(lane == i, total, 0.0)) * scale
 
     block = low_ref.shape[0]
     half = pl.num_programs(0) * block
@@ -294,7 +303,7 @@
 
 
 def place_first(samp, which, own, one, three):
-    count, tail = own.shape[0], own.shape[1:]
+    half, tail = own[0].shape[0], own[0].shape[1:]
     zeros = (0,) * len(tail)
     block = 2
     part = pl.BlockSpec((block,) + tail, lambda j, f, w: (j,) + zeros)
@@ -302,46 +311,48 @@
         first_places_kernel,
         grid_spec=pltpu.PrefetchScalarGridSpec(
             num_scalar_prefetch=2,
-            grid=(count // block,),
-            in_specs=[part] * 3,
+            grid=(half // block,),
+            in_specs=[part] * 6,
             out_specs=[
-                pl.BlockSpec((4, block) + tail, lambda j, f, w: (0, j) + zeros),
-                pl.BlockSpec((4 * count, tail[-1]), lambda j, f, w: (0, 0)),
+                pl.BlockSpec((4, 2, block) + tail, lambda j, f, w: (0, 0, j) + zeros),
+                pl.BlockSpec((8 * half, tail[-1]), lambda j, f, w: (0, 0)),
             ],
         ),
-        out_shape=[jax.ShapeDtypeStruct((4, count) + tail, F32), jax.ShapeDtypeStruct((4 * count, tail[-1]), F32)],
+        out_shape=[jax.ShapeDtypeStruct((4, 2, half) + tail, F32), jax.ShapeDtypeStruct((8 * half, tail[-1]), F32)],
         compiler_params=params(24),
         cost_estimate=cost(1 << 20, 6 << 20),
-    )(samp[None], which, own, one, three)
-
-
-def place_last(samp, which, low, high, out, diagonal):
+    )(samp[None], which, *own, *one, *three)
+
+
+def place_last(samp, which, low, high, out, diagonal, terms, scale):
     half, tail = low.shape[0], low.shape[1:]
     zeros = (0,) * len(tail)
     block = 2
     shape = (4, 2, half) + tail
     part = pl.BlockSpec((block,) + tail, lambda j, f, w: (j,) + zeros)
     diag = pl.BlockSpec(diagonal.shape, lambda j, f, w: (0, 0))
-    out, diagonal = pl.pallas_call(
-        last_places_kernel,
+    out, diagonal, objective = pl.pallas_call(
+        functools.partial(last_places_kernel, scale),
         grid_spec=pltpu.PrefetchScalarGridSpec(
             num_scalar_prefetch=2,
             grid=(half // block,),
-            in_specs=[part, part, ANY, diag],
+            in_specs=[part, part, ANY, diag, pl.BlockSpec(terms.shape, lambda j, f, w: (0, 0, 0))],
             out_specs=[
                 pl.BlockSpec((1, 2, block) + tail, lambda j, f, w: (lax.rem(f[0] + 2, 4), 0, j) + zeros),
                 diag,
+                pl.BlockSpec(memory_space=pltpu.SMEM),
             ],
         ),
         out_shape=[
             jax.ShapeDtypeStruct(shape, F32),
             jax.ShapeDtypeStruct(diagonal.shape, F32),
+            jax.ShapeDtypeStruct((STEPS,), F32),
         ],
         input_output_aliases={4: 0},
         compiler_params=params(16),
         cost_estimate=cost(1 << 20, 2 << 20),
-    )(samp[None], which, low, high, out.reshape(shape), diagonal)
-    return out.reshape((8 * half,) + tail), diagonal.reshape(-1)
+    )(samp[None], which, low, high, out.reshape(shape), diagonal, terms)
+    return out.reshape((8 * half,) + tail), diagonal.reshape(-1), objective
 
 
 def body(observed, blocks, diagonal, pattern):
@@ -368,16 +379,14 @@
 
     diag_rows = diagonal.reshape(cols, width)
     far = far.transpose(1, 0, 2, 3).reshape(each, total_rows, width)
-    new, obj = iterate(info, far, near, turned, begin, diag_rows)
-    one, three = shift(new, "samp", 1), shift(new, "samp", 3)
-    two = [shift(one[: each // 2], "samp", 1), shift(three[each // 2 :], "samp", 3)]
+    *new, obj = iterate(info, far, near, turned, begin, diag_rows)
+    one = [shift(x, "samp", 1) for x in new]
+    three = [shift(x, "samp", 3) for x in new]
+    two = [shift(one[0], "samp", 1), shift(three[1], "samp", 3)]
     terms = jnp.broadcast_to(obj[None], (shares * devices, 1, width))
     terms = lax.all_to_all(terms, ALL, split_axis=0, concat_axis=0, tiled=True)
     placed, diag = place_first(samp, which, new, one, three)
-    terms, diag = lax.optimization_barrier((terms, diag))
-    terms = jnp.sum(terms, axis=(0, 1))
-    new_blocks, new_diagonal = place_last(samp, which, *two, placed, diag)
-    return (new_blocks, new_diagonal, terms[:STEPS] / (cols * devices * width))
+    return place_last(samp, which, *two, placed, diag, terms, 1.0 / (cols * devices * width))
 
 
 def solution(mesh):

time: 171 us -> 178 us (1.041); the launches traced: 169 us -> 178 us
  waiting for transfers between devices: 46.5 us -> 53.7 us
  starting transfers between devices: 27 us -> 29.6 us
    all_to_all x1, waiting for transfers between devices: 4.34 us -> 9.97 us  [body(): terms = lax.all_to_all(terms, ALL, split_axis=0, concat_axis=0, tiled=True)]
    ppermute x7 -> x9, starting transfers between devices: 7.47 us -> 11 us  [shift(): return lax.ppermute(x, axis, [(i, (i + k) % n) for i in range(n)])]
    ppermute x7 -> x9, waiting for transfers between devices: 28.5 us -> 30 us  [shift(): return lax.ppermute(x, axis, [(i, (i + k) % n) for i in range(n)])]
  transfers between devices with their start and end apart: 9 -> 11, of which waited for: 7 -> 5; matrix products, arithmetic and copies ran while one was open for 2% -> 1% of each run, Pallas kernels for 6% -> 6%
where the time goes in v8:
time: 178 us
  blocking collectives  63.4 us (36%)
  waiting for transfers between devices  53.7 us (30%)
  starting transfers between devices  29.6 us (17%)
  Pallas kernels  24.7 us (14%)
  local copies, waits for them, and re-layouts  4.81 us (3%)
    all_to_all x1, blocking collectives, body(): far = lax.all_to_all(outgoing, ALL, split_axis=0, concat_axis=0, tiled=True)  63.4 us
    ppermute x9, waiting for transfers between devices, shift(): return lax.ppermute(x, axis, [(i, (i + k) % n) for i in range(n)])  30 us
    all_to_all x1, waiting for transfers between devices, body(): table = lax.all_to_all(pieces, VAR, split_axis=0, concat_axis=0, tiled=True)  13.7 us
    all_to_all x1, starting transfers between devices, body(): table = lax.all_to_all(pieces, VAR, split_axis=0, concat_axis=0, tiled=True)  13.3 us
    ppermute x9, starting transfers between devices, shift(): return lax.ppermute(x, axis, [(i, (i + k) % n) for i in range(n)])  11 us
    all_to_all x1, waiting for transfers between devices, body(): terms = lax.all_to_all(terms, ALL, split_axis=0, concat_axis=0, tiled=True)  9.97 us
    pallas_call x1, Pallas kernels, near_panels(): pl.pallas_call(near_kernel, grid_spec=pltpu.PrefetchScalarGridSpec(num_sc...  7.56 us
    all_to_all x1, starting transfers between devices, body(): terms = lax.all_to_all(terms, ALL, split_axis=0, concat_axis=0, tiled=True)  5.36 us
  transfers between devices with their start and end apart: 11, of which 5 were waited for; matrix products, arithmetic and copies ran while one was open for 1% of the time, Pallas kernels for 6%

profile of v8, /device:TPU:1, one launch (start us, length us, event | category | flops | bytes accessed | tf_op | source)
XLA Modules:
  0.0 177.8 jit_solution(17757409495691477768)
XLA Ops:
  0.6 3.3 %shard_map.67 = bf16[32,2,33,4,128]{4,3,2,1,0:T(4,128)(2,1)} custom-call(s32[1]{0:T(128)} %bitcast.3.at_ref, s32[2,32]{1,0:T(2,128)} %bitcast.25, bf16[32,32,2,4,128]{4,3,2,1,0:T(4,128)(2,1)} %bitcast.21), custom_call_target="tpu_custom_call" | custom-call | tf_op jit(solution)/shard_map/pallas_call | solution.py:79
  4.0 13.3 %all-to-all-start = ((bf16[64,33,4,128]{3,2,1,0:T(4,128)(2,1)}), bf16[64,33,4,128]{3,2,1,0:T(4,128)(2,1)}, u32[]{:S(2)}, u32[]{:S(2)}) async-start(bf16[64,33,4,128]{3,2,1,0:T(4,128)(2,1)} %bitcast.22), calls=%async_computation | async-start | bytes 4325376 | tf_op jit(solution)/shard_map/all_to_all | solution.py:371
  17.3 1.0 constant_dynamic-slice_fusion
  18.3 2.7 %collective-permute-start.2 = (bf16[256,1024]{1,0:T(8,128)(2,1)}, bf16[256,1024]{1,0:T(8,128)(2,1)S(1)}, u32[]{:S(2)}, u32[]{:S(2)}) collective-permute-start(bf16[256,1024]{1,0:T(8,128)(2,1)} %get-tuple-element.25), channel_id=1, source_target_pairs={{0,192},{64,0},{128,64},{192,128},{1,193},{65,1},{129,65},{193,129... | collective-permute-start | bytes 1572872 | tf_op jit(solution)/shard_map/ppermute | solution.py:34
  21.4 0.7 collective-permute-start
  22.8 20.5 %collective-permute-done.2.p3_ref = bf16[256,1024]{1,0:T(8,128)(2,1)S(1)} collective-permute-done((bf16[256,1024]{1,0:T(8,128)(2,1)}, bf16[256,1024]{1,0:T(8,128)(2,1)S(1)}, u32[]{:S(2)}, u32[]{:S(2)}) %collective-permute-start.2) | collective-permute-done | bytes 524320 | tf_op jit(solution)/shard_map/ppermute | solution.py:34
  43.2 4.5 %collective-permute-done.p1_ref = bf16[256,1024]{1,0:T(8,128)(2,1)S(1)} collective-permute-done((bf16[256,1024]{1,0:T(8,128)(2,1)S(1)}, bf16[256,1024]{1,0:T(8,128)(2,1)S(1)}, u32[]{:S(2)}, u32[]{:S(2)}) %collective-permute-start) | collective-permute-done | bytes 524320 | tf_op jit(solution)/shard_map/ppermute | solution.py:34
  47.7 0.8 copy-done.8
  48.6 7.6 %shard_map.68 = (bf16[8,1024,128]{2,1,0:T(8,128)(2,1)}, bf16[8,128,1024]{2,1,0:T(8,128)(2,1)}, f32[8,256,128]{2,1,0:T(8,128)}) custom-call(s32[10]{0:T(128)} %pad_add_fusion.info_ref, bf16[256,4096]{1,0:T(8,128)(2,1)} %own_ref.1, bf16[256,1024]{1,0:T(8,128)(2,1)} %copy-done.8, bf16[256,1024]{1,0:T(8,128)(2,1)} %copy-done.7, bf16[256,1024]{1,0:T(8,128)(2,1)} %copy-done.6, ...), custom_call_target="tpu_custom_call" | custom-call | flops 1048576 | bytes 10485760 | tf_op jit(solution)/shard_map/pallas_call | solution.py:164
  56.1 13.7 %all-to-all-done.table_ref = bf16[64,33,4,128]{3,2,1,0:T(4,128)(2,1)} async-done(((bf16[64,33,4,128]{3,2,1,0:T(4,128)(2,1)}), bf16[64,33,4,128]{3,2,1,0:T(4,128)(2,1)}, u32[]{:S(2)}, u32[]{:S(2)}) %all-to-all-start) | async-done | bytes 2162720 | tf_op jit(solution)/shard_map/all_to_all | solution.py:371
  69.8 5.2 %shard_map.69 = bf16[256,8,4,128]{3,2,1,0:T(4,128)(2,1)} custom-call(bf16[64,33,4,128]{3,2,1,0:T(4,128)(2,1)} %all-to-all-done.table_ref, bf16[8,1024,128]{2,1,0:T(8,128)(2,1)} %get-tuple-element.14.rest_0_.near_ref, bf16[8,128,1024]{2,1,0:T(8,128)(2,1)} %get-tuple-element.15.rest_1_.turned_ref, f32[8,256,128]{2,1,0:T(8,128)} %get-tuple-element.16.rest_2_.start_ref), custom_call_target="tpu_custom_call" | custom-call | tf_op jit(solution)/shard_map/pallas_call | solution.py:130
  75.0 63.4 %all_to_all.15 = bf16[256,8,4,128]{3,2,1,0:T(4,128)(2,1)S(1)} all-to-all(bf16[256,8,4,128]{3,2,1,0:T(4,128)(2,1)} %shard_map.69), channel_id=1, replica_groups=mesh['samp'=4,'var_0'=4,'var_1'=8,'var_2'=2] {'samp','var_0','var_1','va..., dimensions={0} | all-to-all | bytes 4194304 | tf_op jit(solution)/shard_map/all_to_all | solution.py:378
  138.4 0.7 copy.8
  139.2 0.8 copy-done
  140.6 3.7 %shard_map.70 = (bf16[4,2,128,128]{3,2,1,0:T(8,128)(2,1)S(1)}, bf16[4,2,128,128]{3,2,1,0:T(8,128)(2,1)S(1)}, f32[1,128]{1,0:T(1,128)S(1)}) custom-call(s32[10]{0:T(128)S(1)} %copy-done.3, bf16[8,1024,128]{2,1,0:T(8,128)(2,1)S(1)} %bitcast.18, bf16[8,1024,128]{2,1,0:T(8,128)(2,1)S(1)} %copy-done, bf16[8,128,1024]{2,1,0:T(8,128)(2,1)S(1)} %copy-done.1, ...), custom_call_target="tpu_custom_call" | custom-call | flops 4294967296 | bytes 4194304 | tf_op jit(solution)/shard_map/pallas_call | solution.py:250
  144.7 2.3 %collective-permute-start.5 = (bf16[4,2,128,128]{3,2,1,0:T(8,128)(2,1)S(1)}, bf16[4,2,128,128]{3,2,1,0:T(8,128)(2,1)S(1)}, u32[]{:S(2)}, u32[]{:S(2)}) collective-permute-start(bf16[4,2,128,128]{3,2,1,0:T(8,128)(2,1)S(1)} %get-tuple-element.18.own1), channel_id=1, source_target_pairs={{0,192},{64,0},{128,64},{192,128},{1,193},{65,1},{129,65},{193,129... | collective-permute-start | bytes 786440 | tf_op jit(solution)/shard_map/ppermute | solution.py:34
  147.1 1.4 collective-permute-start.7
  148.5 5.1 %collective-permute-done.3.one0 = bf16[4,2,128,128]{3,2,1,0:T(8,128)(2,1)S(1)} collective-permute-done((bf16[4,2,128,128]{3,2,1,0:T(8,128)(2,1)S(1)}, bf16[4,2,128,128]{3,2,1,0:T(8,128)(2,1)S(1)}, u32[]{:S(2)}, u32[]{:S(2)}) %collective-permute-start.3) | collective-permute-done | bytes 262176 | tf_op jit(solution)/shard_map/ppermute | solution.py:34
  153.6 3.1 %collective-permute-start.6 = (bf16[4,2,128,128]{3,2,1,0:T(8,128)(2,1)S(1)}, bf16[4,2,128,128]{3,2,1,0:T(8,128)(2,1)S(1)}, u32[]{:S(2)}, u32[]{:S(2)}) collective-permute-start(bf16[4,2,128,128]{3,2,1,0:T(8,128)(2,1)S(1)} %collective-permute-done.5.three1), channel_id=1, source_target_pairs={{0,192},{64,0},{128,64},{192,128},{1,193},{65,1},{129,65},{193,129... | collective-permute-start | bytes 786440 | tf_op jit(solution)/shard_map/ppermute | solution.py:34
  156.6 0.7 broadcast_in_dim.28
  157.3 5.4 %all-to-all-start.2 = ((f32[256,1,128]{2,1,0:T(1,128)}), f32[256,1,128]{2,1,0:T(1,128)S(1)}, u32[]{:S(2)}, u32[]{:S(2)}) async-start(f32[256,1,128]{2,1,0:T(1,128)} %broadcast_in_dim.28), calls=%async_computation.2 | async-start | bytes 262144 | tf_op jit(solution)/shard_map/all_to_all | solution.py:387
  162.7 2.9 %shard_map.71 = (f32[4,2,4,2,128,128]{5,4,3,2,1,0:T(8,128)}, f32[32,128]{1,0:T(8,128)S(1)}) custom-call(s32[1]{0:T(128)} %bitcast.samp_ref, s32[32]{0:T(128)S(1)} %compare_select_fusion.which_ref, bf16[4,2,128,128]{3,2,1,0:T(8,128)(2,1)S(1)} %get-tuple-element.17.own0, bf16[4,2,128,128]{3,2,1,0:T(8,128)(2,1)S(1)} %get-tuple-element.18.own1, ...), custom_call_target="tpu_custom_call" | custom-call | flops 1048576 | bytes 6291456 | tf_op jit(solution)/shard_map/pallas_call | solution.py:310
  165.6 10.0 %all-to-all-done.2.terms_ref = f32[256,1,128]{2,1,0:T(1,128)S(1)} async-done(((f32[256,1,128]{2,1,0:T(1,128)}), f32[256,1,128]{2,1,0:T(1,128)S(1)}, u32[]{:S(2)}, u32[]{:S(2)}) %all-to-all-start.2) | async-done | bytes 131104 | tf_op jit(solution)/shard_map/all_to_all | solution.py:387
  175.6 2.0 %shard_map.72 = (f32[4,2,4,2,128,128]{5,4,3,2,1,0:T(8,128)}, f32[32,128]{1,0:T(8,128)}, f32[2]{0:T(128)}) custom-call(s32[1]{0:T(128)} %bitcast.samp_ref, s32[32]{0:T(128)S(1)} %compare_select_fusion.which_ref, bf16[4,2,128,128]{3,2,1,0:T(8,128)(2,1)S(1)} %collective-permute-done.4.low_ref, ...), custom_call_target="tpu_custom_call", output_to_operand_aliasing={{0}: (4, {})} | custom-call | flops 1048576 | bytes 2097152 | tf_op jit(solution)/shard_map/pallas_call | solution.py:334
  (31 shorter events, 2.1 us)
Async XLA Ops:
  4.0 13.4 %copy-start.5 = (bf16[256,4096]{1,0:T(8,128)(2,1)S(1)}, bf16[256,4096]{1,0:T(8,128)(2,1)}, u32[]{:S(2)}) copy-start(bf16[256,4096]{1,0:T(8,128)(2,1)} %own_ref.1) | copy-start | bytes 6291460
  4.0 65.8 %all-to-all-start = ((bf16[64,33,4,128]{3,2,1,0:T(4,128)(2,1)}), bf16[64,33,4,128]{3,2,1,0:T(4,128)(2,1)}, u32[]{:S(2)}, u32[]{:S(2)}) async-start(bf16[64,33,4,128]{3,2,1,0:T(4,128)(2,1)} %bitcast.22), calls=%async_computation | async-start | bytes 4325376 | tf_op jit(solution)/shard_map/all_to_all | solution.py:371
  17.3 4.8 %copy-start.9 = (s32[32,2]{0,1:T(2,128)S(1)}, s32[32,2]{0,1:T(2,128)}, u32[]{:S(2)}) copy-start(s32[32,2]{0,1:T(2,128)} %param.7) | copy-start | bytes 772
  18.3 24.9 %collective-permute-start.2 = (bf16[256,1024]{1,0:T(8,128)(2,1)}, bf16[256,1024]{1,0:T(8,128)(2,1)S(1)}, u32[]{:S(2)}, u32[]{:S(2)}) collective-permute-start(bf16[256,1024]{1,0:T(8,128)(2,1)} %get-tuple-element.25), channel_id=1, source_target_pairs={{0,192},{64,0},{128,64},{192,128},{1,193},{65,1},{129,65},{193,129... | collective-permute-start | bytes 1572872 | tf_op jit(solution)/shard_map/ppermute | solution.py:34
  21.0 22.2 %collective-permute-start.1 = (bf16[256,1024]{1,0:T(8,128)(2,1)S(1)}, bf16[256,1024]{1,0:T(8,128)(2,1)S(1)}, u32[]{:S(2)}, u32[]{:S(2)}) collective-permute-start(bf16[256,1024]{1,0:T(8,128)(2,1)S(1)} %get-tuple-element.26), channel_id=1, source_target_pairs={{0,128},{64,192},{128,0},{192,64},{1,129},{65,193},{129,1},{193,65... | collective-permute-start | bytes 1572872 | tf_op jit(solution)/shard_map/ppermute | solution.py:34
  21.4 26.3 %collective-permute-start = (bf16[256,1024]{1,0:T(8,128)(2,1)S(1)}, bf16[256,1024]{1,0:T(8,128)(2,1)S(1)}, u32[]{:S(2)}, u32[]{:S(2)}) collective-permute-start(bf16[256,1024]{1,0:T(8,128)(2,1)S(1)} %get-tuple-element.27), channel_id=1, source_target_pairs={{0,64},{64,128},{128,192},{192,0},{1,65},{65,129},{129,193},{193,1... | collective-permute-start | bytes 1572872 | tf_op jit(solution)/shard_map/ppermute | solution.py:34
  43.2 4.5 %copy-start.6 = (bf16[256,1024]{1,0:T(8,128)(2,1)}, bf16[256,1024]{1,0:T(8,128)(2,1)S(1)}, u32[]{:S(2)}) copy-start(bf16[256,1024]{1,0:T(8,128)(2,1)S(1)} %collective-permute-done.2.p3_ref) | copy-start | bytes 1572868
  43.2 4.5 %copy-start.7 = (bf16[256,1024]{1,0:T(8,128)(2,1)}, bf16[256,1024]{1,0:T(8,128)(2,1)S(1)}, u32[]{:S(2)}) copy-start(bf16[256,1024]{1,0:T(8,128)(2,1)S(1)} %collective-permute-done.1.p2_ref) | copy-start | bytes 1572868
  47.7 0.8 copy-start.8
  75.0 64.2 %copy-start.2 = (f32[8,256,128]{2,1,0:T(8,128)S(1)}, f32[8,256,128]{2,1,0:T(8,128)}, u32[]{:S(2)}) copy-start(f32[8,256,128]{2,1,0:T(8,128)} %get-tuple-element.16.rest_2_.start_ref) | copy-start | bytes 3145732
  75.0 64.2 %copy-start.4 = (f32[4096]{0:T(1024)S(1)}, f32[4096]{0:T(1024)}, u32[]{:S(2)}) copy-start(f32[4096]{0:T(1024)} %param.6) | copy-start | bytes 49156
  138.4 1.6 copy-start
  138.4 2.2 %copy-start.1 = (bf16[8,128,1024]{2,1,0:T(8,128)(2,1)S(1)}, bf16[8,128,1024]{2,1,0:T(8,128)(2,1)}, u32[]{:S(2)}) copy-start(bf16[8,128,1024]{2,1,0:T(8,128)(2,1)} %get-tuple-element.15.rest_1_.turned_ref) | copy-start | bytes 6291460
  138.4 2.2 %copy-start.3 = (s32[10]{0:T(128)S(1)}, s32[10]{0:T(128)}, u32[]{:S(2)}) copy-start(s32[10]{0:T(128)} %pad_add_fusion.info_ref) | copy-start | bytes 124
  144.3 9.2 %collective-permute-start.3 = (bf16[4,2,128,128]{3,2,1,0:T(8,128)(2,1)S(1)}, bf16[4,2,128,128]{3,2,1,0:T(8,128)(2,1)S(1)}, u32[]{:S(2)}, u32[]{:S(2)}) collective-permute-start(bf16[4,2,128,128]{3,2,1,0:T(8,128)(2,1)S(1)} %get-tuple-element.17.own0), channel_id=1, source_target_pairs={{0,64},{64,128},{128,192},{192,0},{1,65},{65,129},{129,193},{193,1... | collective-permute-start | bytes 786440 | tf_op jit(solution)/shard_map/ppermute | solution.py:34
  144.7 8.9 %collective-permute-start.5 = (bf16[4,2,128,128]{3,2,1,0:T(8,128)(2,1)S(1)}, bf16[4,2,128,128]{3,2,1,0:T(8,128)(2,1)S(1)}, u32[]{:S(2)}, u32[]{:S(2)}) collective-permute-start(bf16[4,2,128,128]{3,2,1,0:T(8,128)(2,1)S(1)} %get-tuple-element.18.own1), channel_id=1, source_target_pairs={{0,192},{64,0},{128,64},{192,128},{1,193},{65,1},{129,65},{193,129... | collective-permute-start | bytes 786440 | tf_op jit(solution)/shard_map/ppermute | solution.py:34
  147.0 15.7 %collective-permute-start.8 = (bf16[4,2,128,128]{3,2,1,0:T(8,128)(2,1)S(1)}, bf16[4,2,128,128]{3,2,1,0:T(8,128)(2,1)S(1)}, u32[]{:S(2)}, u32[]{:S(2)}) collective-permute-start(bf16[4,2,128,128]{3,2,1,0:T(8,128)(2,1)S(1)} %get-tuple-element.17.own0), channel_id=1, source_target_pairs={{0,192},{64,0},{128,64},{192,128},{1,193},{65,1},{129,65},{193,129... | collective-permute-start | bytes 786440 | tf_op jit(solution)/shard_map/ppermute | solution.py:34
  147.1 15.7 %collective-permute-start.7 = (bf16[4,2,128,128]{3,2,1,0:T(8,128)(2,1)S(1)}, bf16[4,2,128,128]{3,2,1,0:T(8,128)(2,1)S(1)}, u32[]{:S(2)}, u32[]{:S(2)}) collective-permute-start(bf16[4,2,128,128]{3,2,1,0:T(8,128)(2,1)S(1)} %get-tuple-element.18.own1), channel_id=1, source_target_pairs={{0,64},{64,128},{128,192},{192,0},{1,65},{65,129},{129,193},{193,1... | collective-permute-start | bytes 786440 | tf_op jit(solution)/shard_map/ppermute | solution.py:34
  153.6 22.0 %collective-permute-start.4 = (bf16[4,2,128,128]{3,2,1,0:T(8,128)(2,1)S(1)}, bf16[4,2,128,128]{3,2,1,0:T(8,128)(2,1)S(1)}, u32[]{:S(2)}, u32[]{:S(2)}) collective-permute-start(bf16[4,2,128,128]{3,2,1,0:T(8,128)(2,1)S(1)} %collective-permute-done.3.one0), channel_id=1, source_target_pairs={{0,64},{64,128},{128,192},{192,0},{1,65},{65,129},{129,193},{193,1... | collective-permute-start | bytes 786440 | tf_op jit(solution)/shard_map/ppermute | solution.py:34
  153.6 22.0 %collective-permute-start.6 = (bf16[4,2,128,128]{3,2,1,0:T(8,128)(2,1)S(1)}, bf16[4,2,128,128]{3,2,1,0:T(8,128)(2,1)S(1)}, u32[]{:S(2)}, u32[]{:S(2)}) collective-permute-start(bf16[4,2,128,128]{3,2,1,0:T(8,128)(2,1)S(1)} %collective-permute-done.5.three1), channel_id=1, source_target_pairs={{0,192},{64,0},{128,64},{192,128},{1,193},{65,1},{129,65},{193,129... | collective-permute-start | bytes 786440 | tf_op jit(solution)/shard_map/ppermute | solution.py:34
  157.3 18.2 %all-to-all-start.2 = ((f32[256,1,128]{2,1,0:T(1,128)}), f32[256,1,128]{2,1,0:T(1,128)S(1)}, u32[]{:S(2)}, u32[]{:S(2)}) async-start(f32[256,1,128]{2,1,0:T(1,128)} %broadcast_in_dim.28), calls=%async_computation.2 | async-start | bytes 262144 | tf_op jit(solution)/shard_map/all_to_all | solution.py:387

commit v9 on v8

--- a/solution.py
+++ b/solution.py
@@ -285,14 +285,10 @@
                 put(which_ref, out_ref, diag_ref, (q, h, c), (q * 2 + h) * half + pl.program_id(0) * block + c, ref.at[c])
 
 
-def last_places_kernel(scale, samp_ref, which_ref, low_ref, high_ref, _, old_diag_ref, terms_ref, out_ref, diag_ref, objective_ref):
+def last_places_kernel(samp_ref, which_ref, low_ref, high_ref, _, old_diag_ref, out_ref, diag_ref):
     @pl.when(pl.program_id(0) == 0)
     def _():
         diag_ref[...] = old_diag_ref[...]
-        total = jnp.sum(terms_ref[...], axis=0)
-        lane = lax.broadcasted_iota(jnp.int32, total.shape, 1)
-        for i in range(STEPS):
-            objective_ref[i] = jnp.sum(jnp.where(lane == i, total, 0.0)) * scale
 
     block = low_ref.shape[0]
     half = pl.num_programs(0) * block
@@ -324,35 +320,33 @@
     )(samp[None], which, *own, *one, *three)
 
 
-def place_last(samp, which, low, high, out, diagonal, terms, scale):
+def place_last(samp, which, low, high, out, diagonal):
     half, tail = low.shape[0], low.shape[1:]
     zeros = (0,) * len(tail)
     block = 2
     shape = (4, 2, half) + tail
     part = pl.BlockSpec((block,) + tail, lambda j, f, w: (j,) + zeros)
     diag = pl.BlockSpec(diagonal.shape, lambda j, f, w: (0, 0))
-    out, diagonal, objective = pl.pallas_call(
-        functools.partial(last_places_kernel, scale),
+    out, diagonal = pl.pallas_call(
+        last_places_kernel,
         grid_spec=pltpu.PrefetchScalarGridSpec(
             num_scalar_prefetch=2,
             grid=(half // block,),
-            in_specs=[part, part, ANY, diag, pl.BlockSpec(terms.shape, lambda j, f, w: (0, 0, 0))],
+            in_specs=[part, part, ANY, diag],
             out_specs=[
                 pl.BlockSpec((1, 2, block) + tail, lambda j, f, w: (lax.rem(f[0] + 2, 4), 0, j) + zeros),
                 diag,
-                pl.BlockSpec(memory_space=pltpu.SMEM),
             ],
         ),
         out_shape=[
             jax.ShapeDtypeStruct(shape, F32),
             jax.ShapeDtypeStruct(diagonal.shape, F32),
-            jax.ShapeDtypeStruct((STEPS,), F32),
         ],
         input_output_aliases={4: 0},
         compiler_params=params(16),
         cost_estimate=cost(1 << 20, 2 << 20),
-    )(samp[None], which, low, high, out.reshape(shape), diagonal, terms)
-    return out.reshape((8 * half,) + tail), diagonal.reshape(-1), objective
+    )(samp[None], which, low, high, out.reshape(shape), diagonal)
+    return out.reshape((8 * half,) + tail), diagonal.reshape(-1)
 
 
 def body(observed, blocks, diagonal, pattern):
@@ -386,7 +380,10 @@
     terms = jnp.broadcast_to(obj[None], (shares * devices, 1, width))
     terms = lax.all_to_all(terms, ALL, split_axis=0, concat_axis=0, tiled=True)
     placed, diag = place_first(samp, which, new, one, three)
-    return place_last(samp, which, *two, placed, diag, terms, 1.0 / (cols * devices * width))
+    terms, diag = lax.optimization_barrier((terms, diag))
+    terms = jnp.sum(terms, axis=(0, 1))
+    new_blocks, new_diagonal = place_last(samp, which, *two, placed, diag)
+    return (new_blocks, new_diagonal, terms[:STEPS] / (cols * devices * width))
 
 
 def solution(mesh):

time: 178 us -> 171 us (0.961)
  waiting for transfers between devices: 53.7 us -> 45.8 us
    ppermute x9, waiting for transfers between devices: 30 us -> 25 us  [shift(): return lax.ppermute(x, axis, [(i, (i + k) % n) for i in range(n)])]
    all_to_all x1, waiting for transfers between devices: 9.97 us -> 7.15 us  [body(): terms = lax.all_to_all(terms, ALL, split_axis=0, concat_axis=0, tiled=True)]
  transfers between devices with their start and end apart: 11 -> 11, of which waited for: 5 -> 4; matrix products, arithmetic and copies ran while one was open for 1% -> 2% of each run, Pallas kernels for 6% -> 6%
where the time goes in v9:
time: 171 us; the launch traced here: 170 us
  blocking collectives  63.4 us (37%)
  waiting for transfers between devices  45.8 us (27%)
  starting transfers between devices  29.8 us (17%)
  Pallas kernels  24.2 us (14%)
  local copies, waits for them, and re-layouts  4.79 us (3%)
    all_to_all x1, blocking collectives, body(): far = lax.all_to_all(outgoing, ALL, split_axis=0, concat_axis=0, tiled=True)  63.4 us
    ppermute x9, waiting for transfers between devices, shift(): return lax.ppermute(x, axis, [(i, (i + k) % n) for i in range(n)])  25 us
    all_to_all x1, waiting for transfers between devices, body(): table = lax.all_to_all(pieces, VAR, split_axis=0, concat_axis=0, tiled=True)  13.7 us
    all_to_all x1, starting transfers between devices, body(): table = lax.all_to_all(pieces, VAR, split_axis=0, concat_axis=0, tiled=True)  13.3 us
    ppermute x9, starting transfers between devices, shift(): return lax.ppermute(x, axis, [(i, (i + k) % n) for i in range(n)])  10.8 us
    pallas_call x1, Pallas kernels, near_panels(): pl.pallas_call(near_kernel, grid_spec=pltpu.PrefetchScalarGridSpec(num_sc...  7.53 us
    all_to_all x1, waiting for transfers between devices, body(): terms = lax.all_to_all(terms, ALL, split_axis=0, concat_axis=0, tiled=True)  7.15 us
    all_to_all x1, starting transfers between devices, body(): terms = lax.all_to_all(terms, ALL, split_axis=0, concat_axis=0, tiled=True)  5.74 us
  transfers between devices with their start and end apart: 11, of which 4 were waited for; matrix products, arithmetic and copies ran while one was open for 2% of the time, Pallas kernels for 6%

profile of v9, /device:TPU:1, one launch (start us, length us, event | category | flops | bytes accessed | tf_op | source)
XLA Modules:
  0.0 170.3 jit_solution(6925466959807669225)
XLA Ops:
  0.6 3.3 %shard_map.67 = bf16[32,2,33,4,128]{4,3,2,1,0:T(4,128)(2,1)} custom-call(s32[1]{0:T(128)} %bitcast.3.at_ref, s32[2,32]{1,0:T(2,128)} %bitcast.25, bf16[32,32,2,4,128]{4,3,2,1,0:T(4,128)(2,1)} %bitcast.21), custom_call_target="tpu_custom_call" | custom-call | tf_op jit(solution)/shard_map/pallas_call | solution.py:79
  4.0 13.3 %all-to-all-start = ((bf16[64,33,4,128]{3,2,1,0:T(4,128)(2,1)}), bf16[64,33,4,128]{3,2,1,0:T(4,128)(2,1)}, u32[]{:S(2)}, u32[]{:S(2)}) async-start(bf16[64,33,4,128]{3,2,1,0:T(4,128)(2,1)} %bitcast.22), calls=%async_computation | async-start | bytes 4325376 | tf_op jit(solution)/shard_map/all_to_all | solution.py:365
  17.3 1.0 constant_dynamic-slice_fusion
  18.3 2.7 %collective-permute-start.2 = (bf16[256,1024]{1,0:T(8,128)(2,1)}, bf16[256,1024]{1,0:T(8,128)(2,1)S(1)}, u32[]{:S(2)}, u32[]{:S(2)}) collective-permute-start(bf16[256,1024]{1,0:T(8,128)(2,1)} %get-tuple-element.27), channel_id=1, source_target_pairs={{0,192},{64,0},{128,64},{192,128},{1,193},{65,1},{129,65},{193,129... | collective-permute-start | bytes 1572872 | tf_op jit(solution)/shard_map/ppermute | solution.py:34
  21.4 0.7 collective-permute-start
  22.8 20.5 %collective-permute-done.2.p3_ref = bf16[256,1024]{1,0:T(8,128)(2,1)S(1)} collective-permute-done((bf16[256,1024]{1,0:T(8,128)(2,1)}, bf16[256,1024]{1,0:T(8,128)(2,1)S(1)}, u32[]{:S(2)}, u32[]{:S(2)}) %collective-permute-start.2) | collective-permute-done | bytes 524320 | tf_op jit(solution)/shard_map/ppermute | solution.py:34
  43.2 4.5 %collective-permute-done.p1_ref = bf16[256,1024]{1,0:T(8,128)(2,1)S(1)} collective-permute-done((bf16[256,1024]{1,0:T(8,128)(2,1)S(1)}, bf16[256,1024]{1,0:T(8,128)(2,1)S(1)}, u32[]{:S(2)}, u32[]{:S(2)}) %collective-permute-start) | collective-permute-done | bytes 524320 | tf_op jit(solution)/shard_map/ppermute | solution.py:34
  47.7 0.8 copy-done.8
  48.5 7.5 %shard_map.68 = (bf16[8,1024,128]{2,1,0:T(8,128)(2,1)}, bf16[8,128,1024]{2,1,0:T(8,128)(2,1)}, f32[8,256,128]{2,1,0:T(8,128)}) custom-call(s32[10]{0:T(128)} %pad_add_fusion.info_ref, bf16[256,4096]{1,0:T(8,128)(2,1)} %own_ref.1, bf16[256,1024]{1,0:T(8,128)(2,1)} %copy-done.8, bf16[256,1024]{1,0:T(8,128)(2,1)} %copy-done.7, bf16[256,1024]{1,0:T(8,128)(2,1)} %copy-done.6, ...), custom_call_target="tpu_custom_call" | custom-call | flops 1048576 | bytes 10485760 | tf_op jit(solution)/shard_map/pallas_call | solution.py:164
  56.1 13.7 %all-to-all-done.table_ref = bf16[64,33,4,128]{3,2,1,0:T(4,128)(2,1)} async-done(((bf16[64,33,4,128]{3,2,1,0:T(4,128)(2,1)}), bf16[64,33,4,128]{3,2,1,0:T(4,128)(2,1)}, u32[]{:S(2)}, u32[]{:S(2)}) %all-to-all-start) | async-done | bytes 2162720 | tf_op jit(solution)/shard_map/all_to_all | solution.py:365
  69.8 5.2 %shard_map.69 = bf16[256,8,4,128]{3,2,1,0:T(4,128)(2,1)} custom-call(bf16[64,33,4,128]{3,2,1,0:T(4,128)(2,1)} %all-to-all-done.table_ref, bf16[8,1024,128]{2,1,0:T(8,128)(2,1)} %get-tuple-element.15.rest_0_.near_ref, bf16[8,128,1024]{2,1,0:T(8,128)(2,1)} %get-tuple-element.16.rest_1_.turned_ref, f32[8,256,128]{2,1,0:T(8,128)} %get-tuple-element.17.rest_2_.start_ref), custom_call_target="tpu_custom_call" | custom-call | tf_op jit(solution)/shard_map/pallas_call | solution.py:130
  75.0 63.4 %all_to_all.15 = bf16[256,8,4,128]{3,2,1,0:T(4,128)(2,1)S(1)} all-to-all(bf16[256,8,4,128]{3,2,1,0:T(4,128)(2,1)} %shard_map.69), channel_id=1, replica_groups=mesh['samp'=4,'var_0'=4,'var_1'=8,'var_2'=2] {'samp','var_0','var_1','va..., dimensions={0} | all-to-all | bytes 4194304 | tf_op jit(solution)/shard_map/all_to_all | solution.py:372
  138.4 0.7 copy.8
  139.2 0.8 copy-done
  140.6 3.7 %shard_map.70 = (bf16[4,2,128,128]{3,2,1,0:T(8,128)(2,1)S(1)}, bf16[4,2,128,128]{3,2,1,0:T(8,128)(2,1)S(1)}, f32[1,128]{1,0:T(1,128)S(1)}) custom-call(s32[10]{0:T(128)S(1)} %copy-done.3, bf16[8,1024,128]{2,1,0:T(8,128)(2,1)S(1)} %bitcast.18, bf16[8,1024,128]{2,1,0:T(8,128)(2,1)S(1)} %copy-done, bf16[8,128,1024]{2,1,0:T(8,128)(2,1)S(1)} %copy-done.1, ...), custom_call_target="tpu_custom_call" | custom-call | flops 4294967296 | bytes 4194304 | tf_op jit(solution)/shard_map/pallas_call | solution.py:250
  144.7 2.3 %collective-permute-start.5 = (bf16[4,2,128,128]{3,2,1,0:T(8,128)(2,1)S(1)}, bf16[4,2,128,128]{3,2,1,0:T(8,128)(2,1)S(1)}, u32[]{:S(2)}, u32[]{:S(2)}) collective-permute-start(bf16[4,2,128,128]{3,2,1,0:T(8,128)(2,1)S(1)} %get-tuple-element.19.own1), channel_id=1, source_target_pairs={{0,192},{64,0},{128,64},{192,128},{1,193},{65,1},{129,65},{193,129... | collective-permute-start | bytes 786440 | tf_op jit(solution)/shard_map/ppermute | solution.py:34
  147.1 1.4 collective-permute-start.7
  148.5 0.7 broadcast_in_dim.28
  149.2 5.7 %all-to-all-start.2 = ((f32[256,1,128]{2,1,0:T(1,128)}), f32[256,1,128]{2,1,0:T(1,128)S(1)}, u32[]{:S(2)}, u32[]{:S(2)}) async-start(f32[256,1,128]{2,1,0:T(1,128)} %broadcast_in_dim.28), calls=%async_computation.2 | async-start | bytes 262144 | tf_op jit(solution)/shard_map/all_to_all | solution.py:381
  155.0 1.5 collective-permute-start.4
  156.4 1.4 collective-permute-start.6
  157.8 2.9 %shard_map.71 = (f32[4,2,4,2,128,128]{5,4,3,2,1,0:T(8,128)}, f32[32,128]{1,0:T(8,128)S(1)}) custom-call(s32[1]{0:T(128)} %bitcast.samp_ref, s32[32]{0:T(128)S(1)} %compare_select_fusion.which_ref, bf16[4,2,128,128]{3,2,1,0:T(8,128)(2,1)S(1)} %get-tuple-element.18.own0, bf16[4,2,128,128]{3,2,1,0:T(8,128)(2,1)S(1)} %get-tuple-element.19.own1, ...), custom_call_target="tpu_custom_call" | custom-call | flops 1048576 | bytes 6291456 | tf_op jit(solution)/shard_map/pallas_call | solution.py:306
  160.7 7.2 %all-to-all-done.2 = f32[256,1,128]{2,1,0:T(1,128)S(1)} async-done(((f32[256,1,128]{2,1,0:T(1,128)}), f32[256,1,128]{2,1,0:T(1,128)S(1)}, u32[]{:S(2)}, u32[]{:S(2)}) %all-to-all-start.2) | async-done | bytes 131104 | tf_op jit(solution)/shard_map/all_to_all | solution.py:381
  168.6 1.6 shard_map.72
  (33 shorter events, 2.9 us)
Async XLA Ops:
  4.0 13.4 %copy-start.5 = (bf16[256,4096]{1,0:T(8,128)(2,1)S(1)}, bf16[256,4096]{1,0:T(8,128)(2,1)}, u32[]{:S(2)}) copy-start(bf16[256,4096]{1,0:T(8,128)(2,1)} %own_ref.1) | copy-start | bytes 6291460
  4.0 65.8 %all-to-all-start = ((bf16[64,33,4,128]{3,2,1,0:T(4,128)(2,1)}), bf16[64,33,4,128]{3,2,1,0:T(4,128)(2,1)}, u32[]{:S(2)}, u32[]{:S(2)}) async-start(bf16[64,33,4,128]{3,2,1,0:T(4,128)(2,1)} %bitcast.22), calls=%async_computation | async-start | bytes 4325376 | tf_op jit(solution)/shard_map/all_to_all | solution.py:365
  17.3 4.8 %copy-start.9 = (s32[32,2]{0,1:T(2,128)S(1)}, s32[32,2]{0,1:T(2,128)}, u32[]{:S(2)}) copy-start(s32[32,2]{0,1:T(2,128)} %param.7) | copy-start | bytes 772
  18.3 24.9 %collective-permute-start.2 = (bf16[256,1024]{1,0:T(8,128)(2,1)}, bf16[256,1024]{1,0:T(8,128)(2,1)S(1)}, u32[]{:S(2)}, u32[]{:S(2)}) collective-permute-start(bf16[256,1024]{1,0:T(8,128)(2,1)} %get-tuple-element.27), channel_id=1, source_target_pairs={{0,192},{64,0},{128,64},{192,128},{1,193},{65,1},{129,65},{193,129... | collective-permute-start | bytes 1572872 | tf_op jit(solution)/shard_map/ppermute | solution.py:34
  21.0 22.2 %collective-permute-start.1 = (bf16[256,1024]{1,0:T(8,128)(2,1)S(1)}, bf16[256,1024]{1,0:T(8,128)(2,1)S(1)}, u32[]{:S(2)}, u32[]{:S(2)}) collective-permute-start(bf16[256,1024]{1,0:T(8,128)(2,1)S(1)} %get-tuple-element.28), channel_id=1, source_target_pairs={{0,128},{64,192},{128,0},{192,64},{1,129},{65,193},{129,1},{193,65... | collective-permute-start | bytes 1572872 | tf_op jit(solution)/shard_map/ppermute | solution.py:34
  21.4 26.3 %collective-permute-start = (bf16[256,1024]{1,0:T(8,128)(2,1)S(1)}, bf16[256,1024]{1,0:T(8,128)(2,1)S(1)}, u32[]{:S(2)}, u32[]{:S(2)}) collective-permute-start(bf16[256,1024]{1,0:T(8,128)(2,1)S(1)} %get-tuple-element.29), channel_id=1, source_target_pairs={{0,64},{64,128},{128,192},{192,0},{1,65},{65,129},{129,193},{193,1... | collective-permute-start | bytes 1572872 | tf_op jit(solution)/shard_map/ppermute | solution.py:34
  43.2 4.5 %copy-start.6 = (bf16[256,1024]{1,0:T(8,128)(2,1)}, bf16[256,1024]{1,0:T(8,128)(2,1)S(1)}, u32[]{:S(2)}) copy-start(bf16[256,1024]{1,0:T(8,128)(2,1)S(1)} %collective-permute-done.2.p3_ref) | copy-start | bytes 1572868
  43.2 4.5 %copy-start.7 = (bf16[256,1024]{1,0:T(8,128)(2,1)}, bf16[256,1024]{1,0:T(8,128)(2,1)S(1)}, u32[]{:S(2)}) copy-start(bf16[256,1024]{1,0:T(8,128)(2,1)S(1)} %collective-permute-done.1.p2_ref) | copy-start | bytes 1572868
  47.7 0.8 copy-start.8
  75.0 64.2 %copy-start.2 = (f32[8,256,128]{2,1,0:T(8,128)S(1)}, f32[8,256,128]{2,1,0:T(8,128)}, u32[]{:S(2)}) copy-start(f32[8,256,128]{2,1,0:T(8,128)} %get-tuple-element.17.rest_2_.start_ref) | copy-start | bytes 3145732
  75.0 64.2 %copy-start.4 = (f32[4096]{0:T(1024)S(1)}, f32[4096]{0:T(1024)}, u32[]{:S(2)}) copy-start(f32[4096]{0:T(1024)} %param.6) | copy-start | bytes 49156
  138.4 1.6 copy-start
  138.4 2.2 %copy-start.1 = (bf16[8,128,1024]{2,1,0:T(8,128)(2,1)S(1)}, bf16[8,128,1024]{2,1,0:T(8,128)(2,1)}, u32[]{:S(2)}) copy-start(bf16[8,128,1024]{2,1,0:T(8,128)(2,1)} %get-tuple-element.16.rest_1_.turned_ref) | copy-start | bytes 6291460
  138.4 2.2 %copy-start.3 = (s32[10]{0:T(128)S(1)}, s32[10]{0:T(128)}, u32[]{:S(2)}) copy-start(s32[10]{0:T(128)} %pad_add_fusion.info_ref) | copy-start | bytes 124
  144.3 10.6 %collective-permute-start.3 = (bf16[4,2,128,128]{3,2,1,0:T(8,128)(2,1)S(1)}, bf16[4,2,128,128]{3,2,1,0:T(8,128)(2,1)S(1)}, u32[]{:S(2)}, u32[]{:S(2)}) collective-permute-start(bf16[4,2,128,128]{3,2,1,0:T(8,128)(2,1)S(1)} %get-tuple-element.18.own0), channel_id=1, source_target_pairs={{0,64},{64,128},{128,192},{192,0},{1,65},{65,129},{129,193},{193,1... | collective-permute-start | bytes 786440 | tf_op jit(solution)/shard_map/ppermute | solution.py:34
  144.7 11.7 %collective-permute-start.5 = (bf16[4,2,128,128]{3,2,1,0:T(8,128)(2,1)S(1)}, bf16[4,2,128,128]{3,2,1,0:T(8,128)(2,1)S(1)}, u32[]{:S(2)}, u32[]{:S(2)}) collective-permute-start(bf16[4,2,128,128]{3,2,1,0:T(8,128)(2,1)S(1)} %get-tuple-element.19.own1), channel_id=1, source_target_pairs={{0,192},{64,0},{128,64},{192,128},{1,193},{65,1},{129,65},{193,129... | collective-permute-start | bytes 786440 | tf_op jit(solution)/shard_map/ppermute | solution.py:34
  147.0 10.8 %collective-permute-start.8 = (bf16[4,2,128,128]{3,2,1,0:T(8,128)(2,1)S(1)}, bf16[4,2,128,128]{3,2,1,0:T(8,128)(2,1)S(1)}, u32[]{:S(2)}, u32[]{:S(2)}) collective-permute-start(bf16[4,2,128,128]{3,2,1,0:T(8,128)(2,1)S(1)} %get-tuple-element.18.own0), channel_id=1, source_target_pairs={{0,192},{64,0},{128,64},{192,128},{1,193},{65,1},{129,65},{193,129... | collective-permute-start | bytes 786440 | tf_op jit(solution)/shard_map/ppermute | solution.py:34
  147.1 10.7 %collective-permute-start.7 = (bf16[4,2,128,128]{3,2,1,0:T(8,128)(2,1)S(1)}, bf16[4,2,128,128]{3,2,1,0:T(8,128)(2,1)S(1)}, u32[]{:S(2)}, u32[]{:S(2)}) collective-permute-start(bf16[4,2,128,128]{3,2,1,0:T(8,128)(2,1)S(1)} %get-tuple-element.19.own1), channel_id=1, source_target_pairs={{0,64},{64,128},{128,192},{192,0},{1,65},{65,129},{129,193},{193,1... | collective-permute-start | bytes 786440 | tf_op jit(solution)/shard_map/ppermute | solution.py:34
  149.2 18.6 %all-to-all-start.2 = ((f32[256,1,128]{2,1,0:T(1,128)}), f32[256,1,128]{2,1,0:T(1,128)S(1)}, u32[]{:S(2)}, u32[]{:S(2)}) async-start(f32[256,1,128]{2,1,0:T(1,128)} %broadcast_in_dim.28), calls=%async_computation.2 | async-start | bytes 262144 | tf_op jit(solution)/shard_map/all_to_all | solution.py:381
  155.0 13.7 %collective-permute-start.4 = (bf16[4,2,128,128]{3,2,1,0:T(8,128)(2,1)S(1)}, bf16[4,2,128,128]{3,2,1,0:T(8,128)(2,1)S(1)}, u32[]{:S(2)}, u32[]{:S(2)}) collective-permute-start(bf16[4,2,128,128]{3,2,1,0:T(8,128)(2,1)S(1)} %collective-permute-done.3.one0), channel_id=1, source_target_pairs={{0,64},{64,128},{128,192},{192,0},{1,65},{65,129},{129,193},{193,1... | collective-permute-start | bytes 786440 | tf_op jit(solution)/shard_map/ppermute | solution.py:34
  156.4 12.2 %collective-permute-start.6 = (bf16[4,2,128,128]{3,2,1,0:T(8,128)(2,1)S(1)}, bf16[4,2,128,128]{3,2,1,0:T(8,128)(2,1)S(1)}, u32[]{:S(2)}, u32[]{:S(2)}) collective-permute-start(bf16[4,2,128,128]{3,2,1,0:T(8,128)(2,1)S(1)} %collective-permute-done.5.three1), channel_id=1, source_target_pairs={{0,192},{64,0},{128,64},{192,128},{1,193},{65,1},{129,65},{193,129... | collective-permute-start | bytes 786440 | tf_op jit(solution)/shard_map/ppermute | solution.py:34

commit v10 on v7

--- a/solution.py
+++ b/solution.py
@@ -145,14 +145,15 @@
     )(table, *after)
 
 
-def near_kernel(info_ref, own_ref, p1_ref, p2_ref, p3_ref, blocks_ref, near_ref, turned_ref, start_ref):
+def near_kernel(info_ref, own_ref, p1_ref, p2_ref, p3_ref, blocks_ref, gram_ref, turned_ref, start_ref, near):
     samp, rows, width = info_ref[0], own_ref.shape[0], own_ref.shape[1]
     for k, ref in enumerate((own_ref, p1_ref, p2_ref, p3_ref)):
         q = lax.rem(samp + 4 - k, 4)
         at = pl.multiple_of(q * rows, rows)
         x = ref[...]
-        near_ref[0, pl.ds(at, rows), :] = x
+        near[pl.ds(at, rows), :] = x
         turned_ref[0, :, pl.ds(at, rows)] = x.T
+    gram_ref[0] = jnp.dot(turned_ref[0], near[...], preferred_element_type=F32)
     where_diag = info_ref[2 + pl.program_id(0)]
     start_ref[0, :width] = blocks_ref[0, where_diag]
     start_ref[0, width:] = blocks_ref[0, 1 - where_diag]
@@ -174,13 +175,14 @@
                 pl.BlockSpec((1, 2, width, width), lambda j, f: (f[1] + j, 0, 0, 0)),
             ],
             out_specs=[
-                pl.BlockSpec((1, 4 * rows, width), lambda j, f: (j, 0, 0)),
+                pl.BlockSpec((1, width, width), lambda j, f: (j, 0, 0)),
                 pl.BlockSpec((1, width, 4 * rows), lambda j, f: (j, 0, 0)),
                 pl.BlockSpec((1, 2 * width, width), lambda j, f: (j, 0, 0)),
             ],
+            scratch_shapes=[pltpu.VMEM((4 * rows, width), BF16)],
         ),
         out_shape=[
-            jax.ShapeDtypeStruct((each, 4 * rows, width), BF16),
+            jax.ShapeDtypeStruct((each, width, width), F32),
             jax.ShapeDtypeStruct((each, width, 4 * rows), BF16),
             jax.ShapeDtypeStruct((each, 2 * width, width), F32),
         ],
@@ -207,9 +209,10 @@
     grams = []
     for c in each:
         far = far_ref[c]
-        both = jnp.concatenate([near_ref[c], far], axis=1)
-        top = jnp.dot(turned_ref[c], both, preferred_element_type=F32)
-        low = lax.dot_general(far, both, (((0,), (0,)), ((), ())), preferred_element_type=F32)
+        cross = jnp.dot(turned_ref[c], far, preferred_element_type=F32)
+        own = lax.dot_general(far, far, (((0,), (0,)), ((), ())), preferred_element_type=F32)
+        top = jnp.concatenate([near_ref[c], cross], axis=1)
+        low = jnp.concatenate([cross.T, own], axis=1)
         grams.append(split3(jnp.concatenate([top, low], axis=0)))
     db = [jnp.where(eye, 0.0, start_ref[c, :width]) for c in each]
     ob = [start_ref[c, width:] for c in each]

time: 171 us -> 171 us (level)
  no operation moved by 1% of the time
where the time goes in v10:
time: 171 us; the launch traced here: 168 us
  blocking collectives  63.4 us (37%)
  waiting for transfers between devices  46.4 us (27%)
  starting transfers between devices  27 us (16%)
  Pallas kernels  24.8 us (15%)
  local copies, waits for them, and re-layouts  4.58 us (3%)
    all_to_all x1, blocking collectives, body(): far = lax.all_to_all(outgoing, ALL, split_axis=0, concat_axis=0, tiled=True)  63.4 us
    ppermute x7, waiting for transfers between devices, shift(): return lax.ppermute(x, axis, [(i, (i + k) % n) for i in range(n)])  28.5 us
    all_to_all x1, waiting for transfers between devices, body(): table = lax.all_to_all(pieces, VAR, split_axis=0, concat_axis=0, tiled=True)  13.6 us
    all_to_all x1, starting transfers between devices, body(): table = lax.all_to_all(pieces, VAR, split_axis=0, concat_axis=0, tiled=True)  13.3 us
    pallas_call x1, Pallas kernels, near_panels(): pl.pallas_call(near_kernel, grid_spec=pltpu.PrefetchScalarGridSpec(num_sc...  7.66 us
    ppermute x7, starting transfers between devices, shift(): return lax.ppermute(x, axis, [(i, (i + k) % n) for i in range(n)])  7.47 us
    all_to_all x1, starting transfers between devices, body(): terms = lax.all_to_all(terms, ALL, split_axis=0, concat_axis=0, tiled=True)  6.23 us
    pallas_call x1, Pallas kernels, pick(): pl.pallas_call(functools.partial(pick_kernel, cols, shares), in_specs=[HB...  5.18 us
  transfers between devices with their start and end apart: 9, of which 7 were waited for; matrix products, arithmetic and copies ran while one was open for 2% of the time, Pallas kernels for 6%

profile of v10, /device:TPU:1, one launch (start us, length us, event | category | flops | bytes accessed | tf_op | source)
XLA Modules:
  0.0 168.4 jit_solution(15395474882296005507)
XLA Ops:
  0.6 3.4 %shard_map.67 = bf16[32,2,33,4,128]{4,3,2,1,0:T(4,128)(2,1)} custom-call(s32[1]{0:T(128)} %bitcast.3.at_ref, s32[2,32]{1,0:T(2,128)} %bitcast.27, bf16[32,32,2,4,128]{4,3,2,1,0:T(4,128)(2,1)} %bitcast.22), custom_call_target="tpu_custom_call" | custom-call | tf_op jit(solution)/shard_map/pallas_call | solution.py:79
  4.1 13.3 %all-to-all-start = ((bf16[64,33,4,128]{3,2,1,0:T(4,128)(2,1)}), bf16[64,33,4,128]{3,2,1,0:T(4,128)(2,1)}, u32[]{:S(2)}, u32[]{:S(2)}) async-start(bf16[64,33,4,128]{3,2,1,0:T(4,128)(2,1)} %bitcast.23), calls=%async_computation | async-start | bytes 4325376 | tf_op jit(solution)/shard_map/all_to_all | solution.py:363
  17.5 1.0 constant_dynamic-slice_fusion
  18.4 2.7 %collective-permute-start.2 = (bf16[256,1024]{1,0:T(8,128)(2,1)}, bf16[256,1024]{1,0:T(8,128)(2,1)S(1)}, u32[]{:S(2)}, u32[]{:S(2)}) collective-permute-start(bf16[256,1024]{1,0:T(8,128)(2,1)} %get-tuple-element.25), channel_id=1, source_target_pairs={{0,192},{64,0},{128,64},{192,128},{1,193},{65,1},{129,65},{193,129... | collective-permute-start | bytes 1572872 | tf_op jit(solution)/shard_map/ppermute | solution.py:34
  21.5 0.7 collective-permute-start
  22.9 20.5 %collective-permute-done.2.p3_ref = bf16[256,1024]{1,0:T(8,128)(2,1)S(1)} collective-permute-done((bf16[256,1024]{1,0:T(8,128)(2,1)}, bf16[256,1024]{1,0:T(8,128)(2,1)S(1)}, u32[]{:S(2)}, u32[]{:S(2)}) %collective-permute-start.2) | collective-permute-done | bytes 524320 | tf_op jit(solution)/shard_map/ppermute | solution.py:34
  43.3 4.5 %collective-permute-done.p1_ref = bf16[256,1024]{1,0:T(8,128)(2,1)S(1)} collective-permute-done((bf16[256,1024]{1,0:T(8,128)(2,1)S(1)}, bf16[256,1024]{1,0:T(8,128)(2,1)S(1)}, u32[]{:S(2)}, u32[]{:S(2)}) %collective-permute-start) | collective-permute-done | bytes 524320 | tf_op jit(solution)/shard_map/ppermute | solution.py:34
  47.8 0.8 copy-done.8
  48.6 7.7 %shard_map.68 = (f32[8,128,128]{2,1,0:T(8,128)}, bf16[8,128,1024]{2,1,0:T(8,128)(2,1)}, f32[8,256,128]{2,1,0:T(8,128)}) custom-call(s32[10]{0:T(128)} %pad_add_fusion.info_ref, bf16[256,4096]{1,0:T(8,128)(2,1)} %own_ref.1, bf16[256,1024]{1,0:T(8,128)(2,1)} %copy-done.8, bf16[256,1024]{1,0:T(8,128)(2,1)} %copy-done.7, bf16[256,1024]{1,0:T(8,128)(2,1)} %copy-done.6, ...), custom_call_target="tpu_custom_call" | custom-call | flops 1048576 | bytes 10485760 | tf_op jit(solution)/shard_map/pallas_call | solution.py:165
  56.3 13.6 %all-to-all-done.table_ref = bf16[64,33,4,128]{3,2,1,0:T(4,128)(2,1)} async-done(((bf16[64,33,4,128]{3,2,1,0:T(4,128)(2,1)}), bf16[64,33,4,128]{3,2,1,0:T(4,128)(2,1)}, u32[]{:S(2)}, u32[]{:S(2)}) %all-to-all-start) | async-done | bytes 2162720 | tf_op jit(solution)/shard_map/all_to_all | solution.py:363
  69.9 5.2 %shard_map.69 = bf16[256,8,4,128]{3,2,1,0:T(4,128)(2,1)} custom-call(bf16[64,33,4,128]{3,2,1,0:T(4,128)(2,1)} %all-to-all-done.table_ref, f32[8,128,128]{2,1,0:T(8,128)} %get-tuple-element.14.rest_0_.near_ref, bf16[8,128,1024]{2,1,0:T(8,128)(2,1)} %get-tuple-element.15.rest_1_.turned_ref, f32[8,256,128]{2,1,0:T(8,128)} %get-tuple-element.16.rest_2_.start_ref), custom_call_target="tpu_custom_call" | custom-call | tf_op jit(solution)/shard_map/pallas_call | solution.py:130
  75.1 63.4 %all_to_all.15 = bf16[256,8,4,128]{3,2,1,0:T(4,128)(2,1)S(1)} all-to-all(bf16[256,8,4,128]{3,2,1,0:T(4,128)(2,1)} %shard_map.69), channel_id=1, replica_groups=mesh['samp'=4,'var_0'=4,'var_1'=8,'var_2'=2] {'samp','var_0','var_1','va..., dimensions={0} | all-to-all | bytes 4194304 | tf_op jit(solution)/shard_map/all_to_all | solution.py:370
  138.5 0.7 copy.8
  139.3 0.8 copy-done
  140.5 3.8 %shard_map.70 = (bf16[8,2,128,128]{3,2,1,0:T(8,128)(2,1)S(1)}, f32[1,128]{1,0:T(1,128)S(1)}) custom-call(s32[10]{0:T(128)S(1)} %copy-done.3, bf16[8,1024,128]{2,1,0:T(8,128)(2,1)S(1)} %bitcast.19, f32[8,128,128]{2,1,0:T(8,128)S(1)} %copy-done.2, bf16[8,128,1024]{2,1,0:T(8,128)(2,1)S(1)} %copy-done, f32[8,256,128]{2,1,0:T(8,128)S(1)} %copy-done.1, ...), custom_call_target="tpu_custom_call" | custom-call | flops 4294967296 | bytes 4194304 | tf_op jit(solution)/shard_map/pallas_call | solution.py:251
  144.3 0.8 collective-permute-start.5
  145.1 0.7 collective-permute-start.3
  145.7 0.7 broadcast_in_dim.28
  146.5 6.2 %all-to-all-start.2 = ((f32[256,1,128]{2,1,0:T(1,128)}), f32[256,1,128]{2,1,0:T(1,128)S(1)}, u32[]{:S(2)}, u32[]{:S(2)}) async-start(f32[256,1,128]{2,1,0:T(1,128)} %broadcast_in_dim.28), calls=%async_computation.2 | async-start | bytes 262144 | tf_op jit(solution)/shard_map/all_to_all | solution.py:378
  152.7 2.8 %collective-permute-done.5.three_ref = bf16[8,2,128,128]{3,2,1,0:T(8,128)(2,1)S(1)} collective-permute-done((bf16[8,2,128,128]{3,2,1,0:T(8,128)(2,1)S(1)}, bf16[8,2,128,128]{3,2,1,0:T(8,128)(2,1)S(1)}, u32[]{:S(2)}, u32[]{:S(2)}) %collective-permute-start.5) | collective-permute-done | bytes 524320 | tf_op jit(solution)/shard_map/ppermute | solution.py:34
  155.6 2.1 %collective-permute-start.6 = (bf16[4,2,128,128]{3,2,1,0:T(8,128)(2,1)S(1)}, bf16[4,2,128,128]{3,2,1,0:T(8,128)(2,1)S(1)}, u32[]{:S(2)}, u32[]{:S(2)}) collective-permute-start(bf16[4,2,128,128]{3,2,1,0:T(8,128)(2,1)S(1)} %slice.17), channel_id=1, source_target_pairs={{0,192},{64,0},{128,64},{192,128},{1,193},{65,1},{129,65},{193,129... | collective-permute-start | bytes 786440 | tf_op jit(solution)/shard_map/ppermute | solution.py:34
  158.1 3.1 %shard_map.71 = (f32[4,8,2,128,128]{4,3,2,1,0:T(8,128)}, f32[32,128]{1,0:T(8,128)S(1)}) custom-call(s32[1]{0:T(128)} %bitcast.samp_ref, s32[32]{0:T(128)S(1)} %compare_select_fusion.which_ref, bf16[8,2,128,128]{3,2,1,0:T(8,128)(2,1)S(1)} %get-tuple-element.17.own_ref, bf16[8,2,128,128]{3,2,1,0:T(8,128)(2,1)S(1)} %collective-permute-done.3.one_ref, ...), custom_call_target="tpu_custom_call" | custom-call | flops 1048576 | bytes 6291456 | tf_op jit(solution)/shard_map/pallas_call | solution.py:304
  161.2 4.3 %all-to-all-done.2 = f32[256,1,128]{2,1,0:T(1,128)S(1)} async-done(((f32[256,1,128]{2,1,0:T(1,128)}), f32[256,1,128]{2,1,0:T(1,128)S(1)}, u32[]{:S(2)}, u32[]{:S(2)}) %all-to-all-start.2) | async-done | bytes 131104 | tf_op jit(solution)/shard_map/all_to_all | solution.py:378
  166.8 1.6 shard_map.72
  (31 shorter events, 3.0 us)
Async XLA Ops:
  4.1 13.4 %copy-start.5 = (bf16[256,4096]{1,0:T(8,128)(2,1)S(1)}, bf16[256,4096]{1,0:T(8,128)(2,1)}, u32[]{:S(2)}) copy-start(bf16[256,4096]{1,0:T(8,128)(2,1)} %own_ref.1) | copy-start | bytes 6291460
  4.1 65.8 %all-to-all-start = ((bf16[64,33,4,128]{3,2,1,0:T(4,128)(2,1)}), bf16[64,33,4,128]{3,2,1,0:T(4,128)(2,1)}, u32[]{:S(2)}, u32[]{:S(2)}) async-start(bf16[64,33,4,128]{3,2,1,0:T(4,128)(2,1)} %bitcast.23), calls=%async_computation | async-start | bytes 4325376 | tf_op jit(solution)/shard_map/all_to_all | solution.py:363
  17.4 4.8 %copy-start.9 = (s32[32,2]{0,1:T(2,128)S(1)}, s32[32,2]{0,1:T(2,128)}, u32[]{:S(2)}) copy-start(s32[32,2]{0,1:T(2,128)} %param.7) | copy-start | bytes 772
  18.4 24.9 %collective-permute-start.2 = (bf16[256,1024]{1,0:T(8,128)(2,1)}, bf16[256,1024]{1,0:T(8,128)(2,1)S(1)}, u32[]{:S(2)}, u32[]{:S(2)}) collective-permute-start(bf16[256,1024]{1,0:T(8,128)(2,1)} %get-tuple-element.25), channel_id=1, source_target_pairs={{0,192},{64,0},{128,64},{192,128},{1,193},{65,1},{129,65},{193,129... | collective-permute-start | bytes 1572872 | tf_op jit(solution)/shard_map/ppermute | solution.py:34
  21.2 22.2 %collective-permute-start.1 = (bf16[256,1024]{1,0:T(8,128)(2,1)S(1)}, bf16[256,1024]{1,0:T(8,128)(2,1)S(1)}, u32[]{:S(2)}, u32[]{:S(2)}) collective-permute-start(bf16[256,1024]{1,0:T(8,128)(2,1)S(1)} %get-tuple-element.26), channel_id=1, source_target_pairs={{0,128},{64,192},{128,0},{192,64},{1,129},{65,193},{129,1},{193,65... | collective-permute-start | bytes 1572872 | tf_op jit(solution)/shard_map/ppermute | solution.py:34
  21.5 26.3 %collective-permute-start = (bf16[256,1024]{1,0:T(8,128)(2,1)S(1)}, bf16[256,1024]{1,0:T(8,128)(2,1)S(1)}, u32[]{:S(2)}, u32[]{:S(2)}) collective-permute-start(bf16[256,1024]{1,0:T(8,128)(2,1)S(1)} %get-tuple-element.27), channel_id=1, source_target_pairs={{0,64},{64,128},{128,192},{192,0},{1,65},{65,129},{129,193},{193,1... | collective-permute-start | bytes 1572872 | tf_op jit(solution)/shard_map/ppermute | solution.py:34
  43.3 4.5 %copy-start.6 = (bf16[256,1024]{1,0:T(8,128)(2,1)}, bf16[256,1024]{1,0:T(8,128)(2,1)S(1)}, u32[]{:S(2)}) copy-start(bf16[256,1024]{1,0:T(8,128)(2,1)S(1)} %collective-permute-done.2.p3_ref) | copy-start | bytes 1572868
  43.3 4.5 %copy-start.7 = (bf16[256,1024]{1,0:T(8,128)(2,1)}, bf16[256,1024]{1,0:T(8,128)(2,1)S(1)}, u32[]{:S(2)}) copy-start(bf16[256,1024]{1,0:T(8,128)(2,1)S(1)} %collective-permute-done.1.p2_ref) | copy-start | bytes 1572868
  47.8 0.8 copy-start.8
  138.5 1.6 copy-start
  138.5 1.9 %copy-start.1 = (f32[8,256,128]{2,1,0:T(8,128)S(1)}, f32[8,256,128]{2,1,0:T(8,128)}, u32[]{:S(2)}) copy-start(f32[8,256,128]{2,1,0:T(8,128)} %get-tuple-element.16.rest_2_.start_ref) | copy-start | bytes 3145732
  138.5 2.0 %copy-start.2 = (f32[8,128,128]{2,1,0:T(8,128)S(1)}, f32[8,128,128]{2,1,0:T(8,128)}, u32[]{:S(2)}) copy-start(f32[8,128,128]{2,1,0:T(8,128)} %get-tuple-element.14.rest_0_.near_ref) | copy-start | bytes 1572868
  138.5 2.0 %copy-start.3 = (s32[10]{0:T(128)S(1)}, s32[10]{0:T(128)}, u32[]{:S(2)}) copy-start(s32[10]{0:T(128)} %pad_add_fusion.info_ref) | copy-start | bytes 124
  138.5 2.0 %copy-start.4 = (f32[4096]{0:T(1024)S(1)}, f32[4096]{0:T(1024)}, u32[]{:S(2)}) copy-start(f32[4096]{0:T(1024)} %param.6) | copy-start | bytes 49156
  144.3 11.3 %collective-permute-start.5 = (bf16[8,2,128,128]{3,2,1,0:T(8,128)(2,1)S(1)}, bf16[8,2,128,128]{3,2,1,0:T(8,128)(2,1)S(1)}, u32[]{:S(2)}, u32[]{:S(2)}) collective-permute-start(bf16[8,2,128,128]{3,2,1,0:T(8,128)(2,1)S(1)} %get-tuple-element.17.own_ref), channel_id=1, source_target_pairs={{0,192},{64,0},{128,64},{192,128},{1,193},{65,1},{129,65},{193,129... | collective-permute-start | bytes 1572872 | tf_op jit(solution)/shard_map/ppermute | solution.py:34
  145.1 12.9 %collective-permute-start.3 = (bf16[8,2,128,128]{3,2,1,0:T(8,128)(2,1)S(1)}, bf16[8,2,128,128]{3,2,1,0:T(8,128)(2,1)S(1)}, u32[]{:S(2)}, u32[]{:S(2)}) collective-permute-start(bf16[8,2,128,128]{3,2,1,0:T(8,128)(2,1)S(1)} %get-tuple-element.17.own_ref), channel_id=1, source_target_pairs={{0,64},{64,128},{128,192},{192,0},{1,65},{65,129},{129,193},{193,1... | collective-permute-start | bytes 1572872 | tf_op jit(solution)/shard_map/ppermute | solution.py:34
  146.5 19.1 %all-to-all-start.2 = ((f32[256,1,128]{2,1,0:T(1,128)}), f32[256,1,128]{2,1,0:T(1,128)S(1)}, u32[]{:S(2)}, u32[]{:S(2)}) async-start(f32[256,1,128]{2,1,0:T(1,128)} %broadcast_in_dim.28), calls=%async_computation.2 | async-start | bytes 262144 | tf_op jit(solution)/shard_map/all_to_all | solution.py:378
  155.6 10.8 %collective-permute-start.6 = (bf16[4,2,128,128]{3,2,1,0:T(8,128)(2,1)S(1)}, bf16[4,2,128,128]{3,2,1,0:T(8,128)(2,1)S(1)}, u32[]{:S(2)}, u32[]{:S(2)}) collective-permute-start(bf16[4,2,128,128]{3,2,1,0:T(8,128)(2,1)S(1)} %slice.17), channel_id=1, source_target_pairs={{0,192},{64,0},{128,64},{192,128},{1,193},{65,1},{129,65},{193,129... | collective-permute-start | bytes 786440 | tf_op jit(solution)/shard_map/ppermute | solution.py:34
  158.0 8.8 %collective-permute-start.4 = (bf16[4,2,128,128]{3,2,1,0:T(8,128)(2,1)S(1)}, bf16[4,2,128,128]{3,2,1,0:T(8,128)(2,1)S(1)}, u32[]{:S(2)}, u32[]{:S(2)}) collective-permute-start(bf16[4,2,128,128]{3,2,1,0:T(8,128)(2,1)S(1)} %slice.16), channel_id=1, source_target_pairs={{0,64},{64,128},{128,192},{192,0},{1,65},{65,129},{129,193},{193,1... | collective-permute-start | bytes 786440 | tf_op jit(solution)/shard_map/ppermute | solution.py:34

commit v11 on v9

--- a/solution.py
+++ b/solution.py
@@ -145,14 +145,15 @@
     )(table, *after)
 
 
-def near_kernel(info_ref, own_ref, p1_ref, p2_ref, p3_ref, blocks_ref, near_ref, turned_ref, start_ref):
+def near_kernel(info_ref, own_ref, p1_ref, p2_ref, p3_ref, blocks_ref, gram_ref, turned_ref, start_ref, near):
     samp, rows, width = info_ref[0], own_ref.shape[0], own_ref.shape[1]
     for k, ref in enumerate((own_ref, p1_ref, p2_ref, p3_ref)):
         q = lax.rem(samp + 4 - k, 4)
         at = pl.multiple_of(q * rows, rows)
         x = ref[...]
-        near_ref[0, pl.ds(at, rows), :] = x
+        near[pl.ds(at, rows), :] = x
         turned_ref[0, :, pl.ds(at, rows)] = x.T
+    gram_ref[0] = jnp.dot(turned_ref[0], near[...], preferred_element_type=F32)
     where_diag = info_ref[2 + pl.program_id(0)]
     start_ref[0, :width] = blocks_ref[0, where_diag]
     start_ref[0, width:] = blocks_ref[0, 1 - where_diag]
@@ -174,13 +175,14 @@
                 pl.BlockSpec((1, 2, width, width), lambda j, f: (f[1] + j, 0, 0, 0)),
             ],
             out_specs=[
-                pl.BlockSpec((1, 4 * rows, width), lambda j, f: (j, 0, 0)),
+                pl.BlockSpec((1, width, width), lambda j, f: (j, 0, 0)),
                 pl.BlockSpec((1, width, 4 * rows), lambda j, f: (j, 0, 0)),
                 pl.BlockSpec((1, 2 * width, width), lambda j, f: (j, 0, 0)),
             ],
+            scratch_shapes=[pltpu.VMEM((4 * rows, width), BF16)],
         ),
         out_shape=[
-            jax.ShapeDtypeStruct((each, 4 * rows, width), BF16),
+            jax.ShapeDtypeStruct((each, width, width), F32),
             jax.ShapeDtypeStruct((each, width, 4 * rows), BF16),
             jax.ShapeDtypeStruct((each, 2 * width, width), F32),
         ],
@@ -207,9 +209,10 @@
     grams = []
     for c in each:
         far = far_ref[c]
-        both = jnp.concatenate([near_ref[c], far], axis=1)
-        top = jnp.dot(turned_ref[c], both, preferred_element_type=F32)
-        low = lax.dot_general(far, both, (((0,), (0,)), ((), ())), preferred_element_type=F32)
+        cross = jnp.dot(turned_ref[c], far, preferred_element_type=F32)
+        own = lax.dot_general(far, far, (((0,), (0,)), ((), ())), preferred_element_type=F32)
+        top = jnp.concatenate([near_ref[c], cross], axis=1)
+        low = jnp.concatenate([cross.T, own], axis=1)
         grams.append(split3(jnp.concatenate([top, low], axis=0)))
     db = [jnp.where(eye, 0.0, start_ref[c, :width]) for c in each]
     ob = [start_ref[c, width:] for c in each]

time: 171 us -> 171 us (level)
  no operation moved by 1% of the time
where the time goes in v11:
time: 171 us; the launch traced here: 170 us
  blocking collectives  63.4 us (37%)
  waiting for transfers between devices  45.7 us (27%)
  starting transfers between devices  29.8 us (17%)
  Pallas kernels  24.5 us (14%)
  local copies, waits for them, and re-layouts  4.55 us (3%)
    all_to_all x1, blocking collectives, body(): far = lax.all_to_all(outgoing, ALL, split_axis=0, concat_axis=0, tiled=True)  63.4 us
    ppermute x9, waiting for transfers between devices, shift(): return lax.ppermute(x, axis, [(i, (i + k) % n) for i in range(n)])  25 us
    all_to_all x1, waiting for transfers between devices, body(): table = lax.all_to_all(pieces, VAR, split_axis=0, concat_axis=0, tiled=True)  13.6 us
    all_to_all x1, starting transfers between devices, body(): table = lax.all_to_all(pieces, VAR, split_axis=0, concat_axis=0, tiled=True)  13.3 us
    ppermute x9, starting transfers between devices, shift(): return lax.ppermute(x, axis, [(i, (i + k) % n) for i in range(n)])  10.8 us
    pallas_call x1, Pallas kernels, near_panels(): pl.pallas_call(near_kernel, grid_spec=pltpu.PrefetchScalarGridSpec(num_sc...  7.67 us
    all_to_all x1, waiting for transfers between devices, body(): terms = lax.all_to_all(terms, ALL, split_axis=0, concat_axis=0, tiled=True)  7.15 us
    all_to_all x1, starting transfers between devices, body(): terms = lax.all_to_all(terms, ALL, split_axis=0, concat_axis=0, tiled=True)  5.74 us
  transfers between devices with their start and end apart: 11, of which 4 were waited for; matrix products, arithmetic and copies ran while one was open for 2% of the time, Pallas kernels for 6%

profile of v11, /device:TPU:1, one launch (start us, length us, event | category | flops | bytes accessed | tf_op | source)
XLA Modules:
  0.0 170.1 jit_solution(3439700973813342303)
XLA Ops:
  0.6 3.3 %shard_map.67 = bf16[32,2,33,4,128]{4,3,2,1,0:T(4,128)(2,1)} custom-call(s32[1]{0:T(128)} %bitcast.3.at_ref, s32[2,32]{1,0:T(2,128)} %bitcast.25, bf16[32,32,2,4,128]{4,3,2,1,0:T(4,128)(2,1)} %bitcast.21), custom_call_target="tpu_custom_call" | custom-call | tf_op jit(solution)/shard_map/pallas_call | solution.py:79
  4.0 13.3 %all-to-all-start = ((bf16[64,33,4,128]{3,2,1,0:T(4,128)(2,1)}), bf16[64,33,4,128]{3,2,1,0:T(4,128)(2,1)}, u32[]{:S(2)}, u32[]{:S(2)}) async-start(bf16[64,33,4,128]{3,2,1,0:T(4,128)(2,1)} %bitcast.22), calls=%async_computation | async-start | bytes 4325376 | tf_op jit(solution)/shard_map/all_to_all | solution.py:368
  17.3 1.0 constant_dynamic-slice_fusion
  18.3 2.7 %collective-permute-start.2 = (bf16[256,1024]{1,0:T(8,128)(2,1)}, bf16[256,1024]{1,0:T(8,128)(2,1)S(1)}, u32[]{:S(2)}, u32[]{:S(2)}) collective-permute-start(bf16[256,1024]{1,0:T(8,128)(2,1)} %get-tuple-element.27), channel_id=1, source_target_pairs={{0,192},{64,0},{128,64},{192,128},{1,193},{65,1},{129,65},{193,129... | collective-permute-start | bytes 1572872 | tf_op jit(solution)/shard_map/ppermute | solution.py:34
  21.4 0.7 collective-permute-start
  22.8 20.5 %collective-permute-done.2.p3_ref = bf16[256,1024]{1,0:T(8,128)(2,1)S(1)} collective-permute-done((bf16[256,1024]{1,0:T(8,128)(2,1)}, bf16[256,1024]{1,0:T(8,128)(2,1)S(1)}, u32[]{:S(2)}, u32[]{:S(2)}) %collective-permute-start.2) | collective-permute-done | bytes 524320 | tf_op jit(solution)/shard_map/ppermute | solution.py:34
  43.2 4.5 %collective-permute-done.p1_ref = bf16[256,1024]{1,0:T(8,128)(2,1)S(1)} collective-permute-done((bf16[256,1024]{1,0:T(8,128)(2,1)S(1)}, bf16[256,1024]{1,0:T(8,128)(2,1)S(1)}, u32[]{:S(2)}, u32[]{:S(2)}) %collective-permute-start) | collective-permute-done | bytes 524320 | tf_op jit(solution)/shard_map/ppermute | solution.py:34
  47.7 0.8 copy-done.8
  48.5 7.7 %shard_map.68 = (f32[8,128,128]{2,1,0:T(8,128)}, bf16[8,128,1024]{2,1,0:T(8,128)(2,1)}, f32[8,256,128]{2,1,0:T(8,128)}) custom-call(s32[10]{0:T(128)} %pad_add_fusion.info_ref, bf16[256,4096]{1,0:T(8,128)(2,1)} %own_ref.1, bf16[256,1024]{1,0:T(8,128)(2,1)} %copy-done.8, bf16[256,1024]{1,0:T(8,128)(2,1)} %copy-done.7, bf16[256,1024]{1,0:T(8,128)(2,1)} %copy-done.6, ...), custom_call_target="tpu_custom_call" | custom-call | flops 1048576 | bytes 10485760 | tf_op jit(solution)/shard_map/pallas_call | solution.py:165
  56.2 13.6 %all-to-all-done.table_ref = bf16[64,33,4,128]{3,2,1,0:T(4,128)(2,1)} async-done(((bf16[64,33,4,128]{3,2,1,0:T(4,128)(2,1)}), bf16[64,33,4,128]{3,2,1,0:T(4,128)(2,1)}, u32[]{:S(2)}, u32[]{:S(2)}) %all-to-all-start) | async-done | bytes 2162720 | tf_op jit(solution)/shard_map/all_to_all | solution.py:368
  69.8 5.2 %shard_map.69 = bf16[256,8,4,128]{3,2,1,0:T(4,128)(2,1)} custom-call(bf16[64,33,4,128]{3,2,1,0:T(4,128)(2,1)} %all-to-all-done.table_ref, f32[8,128,128]{2,1,0:T(8,128)} %get-tuple-element.15.rest_0_.near_ref, bf16[8,128,1024]{2,1,0:T(8,128)(2,1)} %get-tuple-element.16.rest_1_.turned_ref, f32[8,256,128]{2,1,0:T(8,128)} %get-tuple-element.17.rest_2_.start_ref), custom_call_target="tpu_custom_call" | custom-call | tf_op jit(solution)/shard_map/pallas_call | solution.py:130
  75.0 63.4 %all_to_all.15 = bf16[256,8,4,128]{3,2,1,0:T(4,128)(2,1)S(1)} all-to-all(bf16[256,8,4,128]{3,2,1,0:T(4,128)(2,1)} %shard_map.69), channel_id=1, replica_groups=mesh['samp'=4,'var_0'=4,'var_1'=8,'var_2'=2] {'samp','var_0','var_1','va..., dimensions={0} | all-to-all | bytes 4194304 | tf_op jit(solution)/shard_map/all_to_all | solution.py:375
  138.4 0.7 copy.8
  139.1 0.8 copy-done
  140.4 3.8 %shard_map.70 = (bf16[4,2,128,128]{3,2,1,0:T(8,128)(2,1)S(1)}, bf16[4,2,128,128]{3,2,1,0:T(8,128)(2,1)S(1)}, f32[1,128]{1,0:T(1,128)S(1)}) custom-call(s32[10]{0:T(128)S(1)} %copy-done.3, bf16[8,1024,128]{2,1,0:T(8,128)(2,1)S(1)} %bitcast.18, f32[8,128,128]{2,1,0:T(8,128)S(1)} %copy-done.2, bf16[8,128,1024]{2,1,0:T(8,128)(2,1)S(1)} %copy-done, ...), custom_call_target="tpu_custom_call" | custom-call | flops 4294967296 | bytes 4194304 | tf_op jit(solution)/shard_map/pallas_call | solution.py:253
  144.5 2.3 %collective-permute-start.5 = (bf16[4,2,128,128]{3,2,1,0:T(8,128)(2,1)S(1)}, bf16[4,2,128,128]{3,2,1,0:T(8,128)(2,1)S(1)}, u32[]{:S(2)}, u32[]{:S(2)}) collective-permute-start(bf16[4,2,128,128]{3,2,1,0:T(8,128)(2,1)S(1)} %get-tuple-element.19.own1), channel_id=1, source_target_pairs={{0,192},{64,0},{128,64},{192,128},{1,193},{65,1},{129,65},{193,129... | collective-permute-start | bytes 786440 | tf_op jit(solution)/shard_map/ppermute | solution.py:34
  146.9 1.4 collective-permute-start.7
  148.3 0.7 broadcast_in_dim.28
  149.0 5.7 %all-to-all-start.2 = ((f32[256,1,128]{2,1,0:T(1,128)}), f32[256,1,128]{2,1,0:T(1,128)S(1)}, u32[]{:S(2)}, u32[]{:S(2)}) async-start(f32[256,1,128]{2,1,0:T(1,128)} %broadcast_in_dim.28), calls=%async_computation.2 | async-start | bytes 262144 | tf_op jit(solution)/shard_map/all_to_all | solution.py:384
  154.8 1.5 collective-permute-start.4
  156.3 1.4 collective-permute-start.6
  157.6 2.9 %shard_map.71 = (f32[4,2,4,2,128,128]{5,4,3,2,1,0:T(8,128)}, f32[32,128]{1,0:T(8,128)S(1)}) custom-call(s32[1]{0:T(128)} %bitcast.samp_ref, s32[32]{0:T(128)S(1)} %compare_select_fusion.which_ref, bf16[4,2,128,128]{3,2,1,0:T(8,128)(2,1)S(1)} %get-tuple-element.18.own0, bf16[4,2,128,128]{3,2,1,0:T(8,128)(2,1)S(1)} %get-tuple-element.19.own1, ...), custom_call_target="tpu_custom_call" | custom-call | flops 1048576 | bytes 6291456 | tf_op jit(solution)/shard_map/pallas_call | solution.py:309
  160.5 7.2 %all-to-all-done.2 = f32[256,1,128]{2,1,0:T(1,128)S(1)} async-done(((f32[256,1,128]{2,1,0:T(1,128)}), f32[256,1,128]{2,1,0:T(1,128)S(1)}, u32[]{:S(2)}, u32[]{:S(2)}) %all-to-all-start.2) | async-done | bytes 131104 | tf_op jit(solution)/shard_map/all_to_all | solution.py:384
  168.4 1.6 shard_map.72
  (33 shorter events, 2.7 us)
Async XLA Ops:
  4.0 13.4 %copy-start.5 = (bf16[256,4096]{1,0:T(8,128)(2,1)S(1)}, bf16[256,4096]{1,0:T(8,128)(2,1)}, u32[]{:S(2)}) copy-start(bf16[256,4096]{1,0:T(8,128)(2,1)} %own_ref.1) | copy-start | bytes 6291460
  4.0 65.8 %all-to-all-start = ((bf16[64,33,4,128]{3,2,1,0:T(4,128)(2,1)}), bf16[64,33,4,128]{3,2,1,0:T(4,128)(2,1)}, u32[]{:S(2)}, u32[]{:S(2)}) async-start(bf16[64,33,4,128]{3,2,1,0:T(4,128)(2,1)} %bitcast.22), calls=%async_computation | async-start | bytes 4325376 | tf_op jit(solution)/shard_map/all_to_all | solution.py:368
  17.3 4.8 %copy-start.9 = (s32[32,2]{0,1:T(2,128)S(1)}, s32[32,2]{0,1:T(2,128)}, u32[]{:S(2)}) copy-start(s32[32,2]{0,1:T(2,128)} %param.7) | copy-start | bytes 772
  18.3 24.9 %collective-permute-start.2 = (bf16[256,1024]{1,0:T(8,128)(2,1)}, bf16[256,1024]{1,0:T(8,128)(2,1)S(1)}, u32[]{:S(2)}, u32[]{:S(2)}) collective-permute-start(bf16[256,1024]{1,0:T(8,128)(2,1)} %get-tuple-element.27), channel_id=1, source_target_pairs={{0,192},{64,0},{128,64},{192,128},{1,193},{65,1},{129,65},{193,129... | collective-permute-start | bytes 1572872 | tf_op jit(solution)/shard_map/ppermute | solution.py:34
  21.0 22.2 %collective-permute-start.1 = (bf16[256,1024]{1,0:T(8,128)(2,1)S(1)}, bf16[256,1024]{1,0:T(8,128)(2,1)S(1)}, u32[]{:S(2)}, u32[]{:S(2)}) collective-permute-start(bf16[256,1024]{1,0:T(8,128)(2,1)S(1)} %get-tuple-element.28), channel_id=1, source_target_pairs={{0,128},{64,192},{128,0},{192,64},{1,129},{65,193},{129,1},{193,65... | collective-permute-start | bytes 1572872 | tf_op jit(solution)/shard_map/ppermute | solution.py:34
  21.4 26.3 %collective-permute-start = (bf16[256,1024]{1,0:T(8,128)(2,1)S(1)}, bf16[256,1024]{1,0:T(8,128)(2,1)S(1)}, u32[]{:S(2)}, u32[]{:S(2)}) collective-permute-start(bf16[256,1024]{1,0:T(8,128)(2,1)S(1)} %get-tuple-element.29), channel_id=1, source_target_pairs={{0,64},{64,128},{128,192},{192,0},{1,65},{65,129},{129,193},{193,1... | collective-permute-start | bytes 1572872 | tf_op jit(solution)/shard_map/ppermute | solution.py:34
  43.2 4.5 %copy-start.6 = (bf16[256,1024]{1,0:T(8,128)(2,1)}, bf16[256,1024]{1,0:T(8,128)(2,1)S(1)}, u32[]{:S(2)}) copy-start(bf16[256,1024]{1,0:T(8,128)(2,1)S(1)} %collective-permute-done.2.p3_ref) | copy-start | bytes 1572868
  43.2 4.5 %copy-start.7 = (bf16[256,1024]{1,0:T(8,128)(2,1)}, bf16[256,1024]{1,0:T(8,128)(2,1)S(1)}, u32[]{:S(2)}) copy-start(bf16[256,1024]{1,0:T(8,128)(2,1)S(1)} %collective-permute-done.1.p2_ref) | copy-start | bytes 1572868
  47.7 0.8 copy-start.8
  138.4 1.6 copy-start
  138.4 1.9 %copy-start.1 = (f32[8,256,128]{2,1,0:T(8,128)S(1)}, f32[8,256,128]{2,1,0:T(8,128)}, u32[]{:S(2)}) copy-start(f32[8,256,128]{2,1,0:T(8,128)} %get-tuple-element.17.rest_2_.start_ref) | copy-start | bytes 3145732
  138.4 2.0 %copy-start.2 = (f32[8,128,128]{2,1,0:T(8,128)S(1)}, f32[8,128,128]{2,1,0:T(8,128)}, u32[]{:S(2)}) copy-start(f32[8,128,128]{2,1,0:T(8,128)} %get-tuple-element.15.rest_0_.near_ref) | copy-start | bytes 1572868
  138.4 2.0 %copy-start.3 = (s32[10]{0:T(128)S(1)}, s32[10]{0:T(128)}, u32[]{:S(2)}) copy-start(s32[10]{0:T(128)} %pad_add_fusion.info_ref) | copy-start | bytes 124
  138.4 2.0 %copy-start.4 = (f32[4096]{0:T(1024)S(1)}, f32[4096]{0:T(1024)}, u32[]{:S(2)}) copy-start(f32[4096]{0:T(1024)} %param.6) | copy-start | bytes 49156
  144.2 10.6 %collective-permute-start.3 = (bf16[4,2,128,128]{3,2,1,0:T(8,128)(2,1)S(1)}, bf16[4,2,128,128]{3,2,1,0:T(8,128)(2,1)S(1)}, u32[]{:S(2)}, u32[]{:S(2)}) collective-permute-start(bf16[4,2,128,128]{3,2,1,0:T(8,128)(2,1)S(1)} %get-tuple-element.18.own0), channel_id=1, source_target_pairs={{0,64},{64,128},{128,192},{192,0},{1,65},{65,129},{129,193},{193,1... | collective-permute-start | bytes 786440 | tf_op jit(solution)/shard_map/ppermute | solution.py:34
  144.5 11.7 %collective-permute-start.5 = (bf16[4,2,128,128]{3,2,1,0:T(8,128)(2,1)S(1)}, bf16[4,2,128,128]{3,2,1,0:T(8,128)(2,1)S(1)}, u32[]{:S(2)}, u32[]{:S(2)}) collective-permute-start(bf16[4,2,128,128]{3,2,1,0:T(8,128)(2,1)S(1)} %get-tuple-element.19.own1), channel_id=1, source_target_pairs={{0,192},{64,0},{128,64},{192,128},{1,193},{65,1},{129,65},{193,129... | collective-permute-start | bytes 786440 | tf_op jit(solution)/shard_map/ppermute | solution.py:34
  146.8 10.8 %collective-permute-start.8 = (bf16[4,2,128,128]{3,2,1,0:T(8,128)(2,1)S(1)}, bf16[4,2,128,128]{3,2,1,0:T(8,128)(2,1)S(1)}, u32[]{:S(2)}, u32[]{:S(2)}) collective-permute-start(bf16[4,2,128,128]{3,2,1,0:T(8,128)(2,1)S(1)} %get-tuple-element.18.own0), channel_id=1, source_target_pairs={{0,192},{64,0},{128,64},{192,128},{1,193},{65,1},{129,65},{193,129... | collective-permute-start | bytes 786440 | tf_op jit(solution)/shard_map/ppermute | solution.py:34
  146.9 10.7 %collective-permute-start.7 = (bf16[4,2,128,128]{3,2,1,0:T(8,128)(2,1)S(1)}, bf16[4,2,128,128]{3,2,1,0:T(8,128)(2,1)S(1)}, u32[]{:S(2)}, u32[]{:S(2)}) collective-permute-start(bf16[4,2,128,128]{3,2,1,0:T(8,128)(2,1)S(1)} %get-tuple-element.19.own1), channel_id=1, source_target_pairs={{0,64},{64,128},{128,192},{192,0},{1,65},{65,129},{129,193},{193,1... | collective-permute-start | bytes 786440 | tf_op jit(solution)/shard_map/ppermute | solution.py:34
  149.0 18.6 %all-to-all-start.2 = ((f32[256,1,128]{2,1,0:T(1,128)}), f32[256,1,128]{2,1,0:T(1,128)S(1)}, u32[]{:S(2)}, u32[]{:S(2)}) async-start(f32[256,1,128]{2,1,0:T(1,128)} %broadcast_in_dim.28), calls=%async_computation.2 | async-start | bytes 262144 | tf_op jit(solution)/shard_map/all_to_all | solution.py:384
  154.8 13.7 %collective-permute-start.4 = (bf16[4,2,128,128]{3,2,1,0:T(8,128)(2,1)S(1)}, bf16[4,2,128,128]{3,2,1,0:T(8,128)(2,1)S(1)}, u32[]{:S(2)}, u32[]{:S(2)}) collective-permute-start(bf16[4,2,128,128]{3,2,1,0:T(8,128)(2,1)S(1)} %collective-permute-done.3.one0), channel_id=1, source_target_pairs={{0,64},{64,128},{128,192},{192,0},{1,65},{65,129},{129,193},{193,1... | collective-permute-start | bytes 786440 | tf_op jit(solution)/shard_map/ppermute | solution.py:34
  156.3 12.2 %collective-permute-start.6 = (bf16[4,2,128,128]{3,2,1,0:T(8,128)(2,1)S(1)}, bf16[4,2,128,128]{3,2,1,0:T(8,128)(2,1)S(1)}, u32[]{:S(2)}, u32[]{:S(2)}) collective-permute-start(bf16[4,2,128,128]{3,2,1,0:T(8,128)(2,1)S(1)} %collective-permute-done.5.three1), channel_id=1, source_target_pairs={{0,192},{64,0},{128,64},{192,128},{1,193},{65,1},{129,65},{193,129... | collective-permute-start | bytes 786440 | tf_op jit(solution)/shard_map/ppermute | solution.py:34
